TPU v7x, 128 devices: a whole 4x4x4 slice. The times are simulated.
128 devices in a mesh: gx: 32 (over z_lo, y, x), gy: 4 (over z_hi, core).
Axes of the slice: x: 4, y: 4, z: 4 (z_hi: 2, z_lo: 2; z = z_hi * 2 + z_lo), core: 2. Of those that a mesh axis runs over, the one named last changes fastest.
Arguments:
- tokens: bfloat16 [512, 256, 1024], P(('gx', 'gy')), may hold values from -128 to 128, as said below
- slot_params: bfloat16 [1024, 128], replicated, may hold values from -1 to 1, as said below
- expand_weight: bfloat16 [128, 1024, 2048], P(('gx', 'gy')), may hold values from -0.1875 to 0.1875
- shrink_weight: bfloat16 [128, 2048, 1024], P(('gx', 'gy')), may hold values from -0.125 to 0.125
- cotangent: bfloat16 [512, 256, 1024], P(('gx', 'gy')), may hold values from -6 to 6
Outputs:
- layer_out: bfloat16 [512, 256, 1024], P(('gx', 'gy'))
- grad_tokens: bfloat16 [512, 256, 1024], P(('gx', 'gy'))
- grad_phi: float32 [1024, 128], replicated
- grad_expand: bfloat16 [128, 1024, 2048], P(('gx', 'gy'))
- grad_shrink: bfloat16 [128, 2048, 1024], P(('gx', 'gy'))
Inputs may be any that keep to these rules, and one draw needn't show every extreme that they name: `tokens`: finite values. `slot_params`: finite values.
All inputs are finite; a program needn't handle non-finite values.
Results may differ from a plain program's by a relative error of at most 0.02.
Values may be sent and summed in bfloat16 or wider, within the bound.
No kernel may reach another device: no remote copies, remote signals or barrier semaphores. Data moves between devices by JAX's collectives and lax.ppermute only.
A program may use at most 128 MiB of HBM per device.

v0:
```python
import jax
import jax.numpy as jnp
from jax import lax
from jax.sharding import PartitionSpec as P


def gelu_value(values_in):
    return 0.5 * values_in * (1.0 + jax.scipy.special.erf(values_in * 0.7071067811865476))


def gelu_slope(values_in):
    cumulative = 0.5 * (1.0 + jax.scipy.special.erf(values_in * 0.7071067811865476))
    return cumulative + values_in * jnp.exp(-0.5 * values_in * values_in) * 0.3989422804014327


def direct_in(slot_rows):
    count, slot_count, model_width = slot_rows.shape
    moved = lax.all_to_all(
        slot_rows.reshape(count, slot_count, 1, model_width),
        ("gx", "gy"),
        split_axis=1,
        concat_axis=2,
        tiled=True,
    )
    return moved.reshape(-1, model_width)


def direct_out(expert_rows, count):
    model_width = expert_rows.shape[1]
    moved = lax.all_to_all(
        expert_rows.reshape(count, 1, -1, model_width),
        ("gx", "gy"),
        split_axis=2,
        concat_axis=1,
        tiled=True,
    )
    return moved.reshape(count, -1, model_width)


def body(tokens, slot_params, expand_weight, shrink_weight, cotangent):
    images = tokens.shape[0]
    logits = jnp.einsum("ipd,ds->ips", tokens, slot_params, preferred_element_type=jnp.float32)
    dispatch_prob = jax.nn.softmax(logits, axis=1)
    combine_prob = jax.nn.softmax(logits, axis=2)
    dispatch = dispatch_prob.astype(jnp.bfloat16)
    combine = combine_prob.astype(jnp.bfloat16)
    slot_in = jnp.einsum(
        "ips,ipd->isd", dispatch, tokens, preferred_element_type=jnp.float32
    ).astype(jnp.bfloat16)
    expert_rows = direct_in(slot_in)
    expand = expand_weight[0]
    shrink = shrink_weight[0]
    hidden = jnp.dot(expert_rows, expand, preferred_element_type=jnp.float32)
    activated = gelu_value(hidden).astype(jnp.bfloat16)
    result_rows = jnp.dot(activated, shrink, preferred_element_type=jnp.float32).astype(
        jnp.bfloat16
    )
    slot_out = direct_out(result_rows, images)
    layer_out = jnp.einsum(
        "ips,isd->ipd", combine, slot_out, preferred_element_type=jnp.float32
    ).astype(jnp.bfloat16)
    grad_combine = jnp.einsum(
        "ipd,isd->ips", cotangent, slot_out, preferred_element_type=jnp.float32
    )
    grad_slot_out = jnp.einsum(
        "ips,ipd->isd", combine, cotangent, preferred_element_type=jnp.float32
    ).astype(jnp.bfloat16)
    grad_rows = direct_in(grad_slot_out)
    grad_activated = jnp.dot(grad_rows, shrink.T, preferred_element_type=jnp.float32)
    grad_shrink = jnp.dot(activated.T, grad_rows, preferred_element_type=jnp.float32).astype(
        jnp.bfloat16
    )
    grad_hidden = (grad_activated * gelu_slope(hidden)).astype(jnp.bfloat16)
    grad_expand = jnp.dot(expert_rows.T, grad_hidden, preferred_element_type=jnp.float32).astype(
        jnp.bfloat16
    )
    grad_input_rows = jnp.dot(grad_hidden, expand.T, preferred_element_type=jnp.float32).astype(
        jnp.bfloat16
    )
    grad_slot_in = direct_out(grad_input_rows, images)
    grad_dispatch = jnp.einsum(
        "ipd,isd->ips", tokens, grad_slot_in, preferred_element_type=jnp.float32
    )
    part_dispatch = dispatch_prob * (
        grad_dispatch - jnp.sum(dispatch_prob * grad_dispatch, axis=1, keepdims=True)
    )
    part_combine = combine_prob * (
        grad_combine - jnp.sum(combine_prob * grad_combine, axis=2, keepdims=True)
    )
    grad_logits = (part_dispatch + part_combine).astype(jnp.bfloat16)
    grad_tokens = (
        jnp.einsum("ips,isd->ipd", dispatch, grad_slot_in, preferred_element_type=jnp.float32)
        + jnp.einsum("ips,ds->ipd", grad_logits, slot_params, preferred_element_type=jnp.float32)
    ).astype(jnp.bfloat16)
    phi_term = jnp.einsum("ipd,ips->ds", tokens, grad_logits, preferred_element_type=jnp.float32)
    grad_phi = lax.psum(phi_term, ("gx", "gy"))
    return (layer_out, grad_tokens, grad_phi, grad_expand[None], grad_shrink[None])


def solution(mesh):
    placed = (
        P(("gx", "gy"), None, None),
        P(),
        P(("gx", "gy"), None, None),
        P(("gx", "gy"), None, None),
        P(("gx", "gy"), None, None),
    )
    return jax.shard_map(
        body,
        mesh=mesh,
        in_specs=placed,
        out_specs=(
            P(("gx", "gy"), None, None),
            P(("gx", "gy"), None, None),
            P(),
            P(("gx", "gy"), None, None),
            P(("gx", "gy"), None, None),
        ),
        check_vma=False,
    )
```

profile of v0, /device:TPU:1, one launch (start us, length us, event | category | flops | bytes accessed | tf_op | source)
XLA Modules:
  0.0 279.0 jit_solution(7361044093879931239)
XLA Ops:
  7.2 0.0 copy-start
  7.2 1.6 copy-done
  8.8 1.6 fusion.53
  10.4 0.4 fusion.61
  10.8 1.5 fusion.26
  12.3 3.0 %copy.29 = bf16[4,128,1,1024]{3,0,2,1:T(4,128)(2,1)} copy(bf16[4,128,1,1024]{3,1,0,2:T(8,128)(2,1)} %fusion.26) | data formatting | bytes 2097152 | tf_op jit(solution)/shard_map/reshape | solution.py:19
  15.3 12.0 %all-to-all-start = ((bf16[4,128,1,1024]{3,0,2,1:T(4,128)(2,1)}), bf16[4,128,1,1024]{3,0,2,1:T(4,128)(2,1)}, u32[]{:S(2)}, u32[]{:S(2)}) async-start(bf16[4,128,1,1024]{3,0,2,1:T(4,128)(2,1)} %copy.29), calls=%async_computation | async-start | bytes 2097152 | tf_op jit(solution)/shard_map/all_to_all | solution.py:18
  27.3 1.0 fusion.62
  28.3 4.7 %fusion.27 = bf16[4,128,1,1024]{3,1,0,2:T(8,128)(2,1)} fusion(bf16[4,256,1024]{2,1,0:T(8,128)(2,1)} %param.9, f32[4,256]{1,0:T(4,128)S(1)} %get-tuple-element.24, f32[4,256,128]{2,1,0:T(8,128)S(1)} %fusion.53), kind=kOutput, calls=%fused_computation.30 | convolution fusion | flops 269354112 | bytes 3674112 | tf_op jit(solution)/shard_map/ips,ipd->isd/dot_general | solution.py:65
  33.0 3.0 %copy.34 = bf16[4,128,1,1024]{3,0,2,1:T(4,128)(2,1)} copy(bf16[4,128,1,1024]{3,1,0,2:T(8,128)(2,1)} %fusion.27) | data formatting | bytes 2097152 | tf_op jit(solution)/shard_map/reshape | solution.py:19
  36.0 9.7 %all-to-all-done = bf16[4,128,1,1024]{3,0,2,1:T(4,128)(2,1)} async-done(((bf16[4,128,1,1024]{3,0,2,1:T(4,128)(2,1)}), bf16[4,128,1,1024]{3,0,2,1:T(4,128)(2,1)}, u32[]{:S(2)}, u32[]{:S(2)}) %all-to-all-start) | async-done | bytes 1048608 | tf_op jit(solution)/shard_map/all_to_all | solution.py:18
  45.7 5.3 %all-to-all-start.2 = ((bf16[4,128,1,1024]{3,0,2,1:T(4,128)(2,1)}), bf16[4,128,1,1024]{3,0,2,1:T(4,128)(2,1)}, u32[]{:S(2)}, u32[]{:S(2)}) async-start(bf16[4,128,1,1024]{3,0,2,1:T(4,128)(2,1)} %copy.34), calls=%async_computation.2 | async-start | bytes 2097152 | tf_op jit(solution)/shard_map/all_to_all | solution.py:18
  51.1 1.5 copy.30
  52.6 0.0 copy-start.1
  52.6 0.0 copy-start.6
  52.6 6.8 %multiply_convert_fusion = (bf16[512,2048]{1,0:T(8,128)(2,1)S(1)}, f32[512,2048]{1,0:T(8,128)}) fusion(bf16[512,1024]{1,0:T(8,128)(2,1)S(1)} %bitcast.73, bf16[1,1024,2048]{2,1,0:T(8,128)(2,1)} %param.7), kind=kOutput, calls=%fused_computation.22 | convolution fusion | flops 2152726528 | bytes 11534336 | tf_op jit(solution)/shard_map/dot_general | solution.py:53
  59.4 0.0 copy-done.1
  59.4 0.0 copy-start.9
  59.4 0.0 copy-done.6
  59.4 2.3 fusion.23
  61.7 0.0 copy-done.9
  61.7 1.8 copy.31
  63.5 5.9 %all-to-all-done.2 = bf16[4,128,1,1024]{3,0,2,1:T(4,128)(2,1)} async-done(((bf16[4,128,1,1024]{3,0,2,1:T(4,128)(2,1)}), bf16[4,128,1,1024]{3,0,2,1:T(4,128)(2,1)}, u32[]{:S(2)}, u32[]{:S(2)}) %all-to-all-start.2) | async-done | bytes 1048608 | tf_op jit(solution)/shard_map/all_to_all | solution.py:18
  69.5 5.4 %all-to-all-start.1 = ((bf16[4,1,128,1024]{3,0,1,2:T(4,128)(2,1)}), bf16[4,1,128,1024]{3,0,1,2:T(4,128)(2,1)}, u32[]{:S(2)}, u32[]{:S(2)}) async-start(bf16[4,1,128,1024]{3,0,1,2:T(4,128)(2,1)} %copy.31), calls=%async_computation.1 | async-start | bytes 2097152 | tf_op jit(solution)/shard_map/all_to_all | solution.py:30
  74.8 1.5 copy.35
  76.4 0.0 copy-start.3
  76.4 1.0 copy-done.3
  77.4 0.0 copy-start.7
  77.4 6.4 %fusion.9 = bf16[512,2048]{1,0:T(8,128)(2,1)S(1)} fusion(f32[512,2048]{1,0:T(8,128)} %get-tuple-element.23, bf16[512,1024]{1,0:T(8,128)(2,1)S(1)} %bitcast.75, bf16[1,2048,1024]{2,1,0:T(8,128)(2,1)} %param.8), kind=kOutput, calls=%fused_computation.10 | convolution fusion | flops 2157969408 | bytes 11534336 | tf_op jit(solution)/shard_map/dot_general | solution.py:69
  83.8 0.0 copy-done.7
  83.8 0.0 copy-start.2
  83.8 2.4 fusion.20
  86.2 1.8 copy.36
  88.0 0.0 copy-done.2
  88.0 4.4 %convert_bitcast_fusion.1 = bf16[1,1024,2048]{2,1,0:T(8,128)(2,1)} fusion(bf16[512,1024]{1,0:T(8,128)(2,1)S(1)} %bitcast.74, bf16[512,2048]{1,0:T(8,128)(2,1)S(1)} %fusion.9), kind=kOutput, calls=%fused_computation.20 | convolution fusion | flops 2149580800 | bytes 7340032 | tf_op jit(solution)/shard_map/dot_general | solution.py:74
  92.4 0.8 all-to-all-done.1
  93.2 9.4 %all-to-all-start.3 = ((bf16[4,1,128,1024]{3,0,1,2:T(4,128)(2,1)}), bf16[4,1,128,1024]{3,0,1,2:T(4,128)(2,1)}, u32[]{:S(2)}, u32[]{:S(2)}) async-start(bf16[4,1,128,1024]{3,0,1,2:T(4,128)(2,1)} %copy.36), calls=%async_computation.3 | async-start | bytes 2097152 | tf_op jit(solution)/shard_map/all_to_all | solution.py:30
  102.7 0.3 all-reduce.2.cloned.1.call-start
  103.0 0.0 copy-start.8
  103.0 0.0 copy-start.5
  103.0 6.4 %convert_bitcast_fusion = bf16[1,2048,1024]{2,1,0:T(8,128)(2,1)} fusion(bf16[512,2048]{1,0:T(8,128)(2,1)} %copy-done.9, bf16[512,1024]{1,0:T(8,128)(2,1)} %bitcast.76), kind=kOutput, calls=%fused_computation.19 | convolution fusion | flops 2149580800 | bytes 7340032 | tf_op jit(solution)/shard_map/dot_general | solution.py:70
  109.4 0.0 copy-done.8
  109.4 2.0 convolution_bitcast_fusion.1
  111.3 0.0 copy-done.5
  111.4 6.3 %fusion.36 = f32[4,256,128]{2,1,0:T(8,128)} fusion(f32[4,256,128]{2,1,0:T(8,128)S(1)} %convolution_bitcast_fusion.1, f32[4,256,128]{2,1,0:T(8,128)S(1)} %copy-done.5, f32[4,256]{1,0:T(4,128)S(1)} %get-tuple-element.24), kind=kOutput, calls=%fused_computation.42 | output fusion | flops 656511 | bytes 1576960 | tf_op jit(solution)/shard_map/sub | solution.py:88
  117.7 3.4 %all-to-all-done.3 = bf16[4,1,128,1024]{3,0,1,2:T(4,128)(2,1)} async-done(((bf16[4,1,128,1024]{3,0,1,2:T(4,128)(2,1)}), bf16[4,1,128,1024]{3,0,1,2:T(4,128)(2,1)}, u32[]{:S(2)}, u32[]{:S(2)}) %all-to-all-start.3) | async-done | bytes 1048608 | tf_op jit(solution)/shard_map/all_to_all | solution.py:30
  121.1 2.8 convolution_bitcast_fusion.2
  123.8 0.0 copy-start.4
  123.9 2.8 convolution_bitcast_fusion
  126.6 0.0 all-reduce.2.cloned.1.call-update
  126.6 4.2 %fusion.39 = f32[4,256,1024]{2,1,0:T(8,128)} fusion(bf16[4,1,128,1024]{3,0,1,2:T(4,128)(2,1)} %all-to-all-done.3, f32[4,128]{1,0:T(4,128)S(1)} %get-tuple-element.20, f32[4,256,128]{2,1,0:T(8,128)S(1)} %fusion.53), kind=kOutput, calls=%fused_computation.45 | convolution fusion | flops 268829440 | bytes 5769216 | tf_op jit(solution)/shard_map/ips,isd->ipd/dot_general | solution.py:92
  130.8 0.0 copy-done.4
  130.8 4.8 %add_convert_fusion = bf16[4,256,1024]{2,1,0:T(8,128)(2,1)} fusion(f32[4,256,1024]{2,1,0:T(8,128)} %fusion.39, f32[4,256,128]{2,1,0:T(8,128)} %fusion.36, f32[4,256,128]{2,1,0:T(8,128)} %convolution_bitcast_fusion.2, bf16[1024,128]{1,0:T(8,128)(2,1)S(1)} %copy-done.4, f32[4,256,128]{2,1,0:T(8,128)S(1)} %get-tuple-element.21, f32[4,128]{1,0:T(4,128)S(1)} %get-tuple-element.20), kind=kOutput, calls=%fused_computation.21 | convolution fusion | flops 271450880 | bytes 8128512 | tf_op jit(solution)/shard_map/ips,ds->ipd/dot_general | solution.py:93
  135.6 4.6 %convolution_convert_fusion = bf16[4,256,1024]{2,1,0:T(8,128)(2,1)} fusion(bf16[4,1,128,1024]{3,0,1,2:T(4,128)(2,1)} %all-to-all-done.1, f32[4,256]{1,0:T(4,128)S(1)} %get-tuple-element.24, f32[4,256,128]{2,1,0:T(8,128)S(1)} %fusion.53), kind=kOutput, calls=%fused_computation.24 | convolution fusion | flops 269878400 | bytes 3674112 | tf_op jit(solution)/shard_map/ips,isd->ipd/dot_general | solution.py:59
  140.2 129.9 %all-reduce.2.cloned.1.call-done = f32[1024,128]{0,1:T(8,128)} async-done(((f32[1024,128]{0,1:T(8,128)}), f32[1024,128]{0,1:T(8,128)}) %all-reduce.2.cloned.1.call-update) | async-done | bytes 524304 | tf_op jit(solution)/shard_map/psum | solution.py:96
  270.1 2.0 copy.41
Async XLA Ops:
  7.2 1.6 copy-start
  15.3 30.4 %all-to-all-start = ((bf16[4,128,1,1024]{3,0,2,1:T(4,128)(2,1)}), bf16[4,128,1,1024]{3,0,2,1:T(4,128)(2,1)}, u32[]{:S(2)}, u32[]{:S(2)}) async-start(bf16[4,128,1,1024]{3,0,2,1:T(4,128)(2,1)} %copy.29), calls=%async_computation | async-start | bytes 2097152 | tf_op jit(solution)/shard_map/all_to_all | solution.py:18
  45.7 23.8 %all-to-all-start.2 = ((bf16[4,128,1,1024]{3,0,2,1:T(4,128)(2,1)}), bf16[4,128,1,1024]{3,0,2,1:T(4,128)(2,1)}, u32[]{:S(2)}, u32[]{:S(2)}) async-start(bf16[4,128,1,1024]{3,0,2,1:T(4,128)(2,1)} %copy.34), calls=%async_computation.2 | async-start | bytes 2097152 | tf_op jit(solution)/shard_map/all_to_all | solution.py:18
  52.6 6.8 %copy-start.1 = (bf16[4,128,1,1024]{3,1,0,2:T(8,128)(2,1)}, bf16[4,128,1,1024]{3,1,0,2:T(8,128)(2,1)S(1)}, u32[]{:S(2)}) copy-start(bf16[4,128,1,1024]{3,1,0,2:T(8,128)(2,1)S(1)} %copy.30) | copy-start | bytes 3145732
  52.6 6.8 %copy-start.6 = (bf16[1,2048,1024]{2,1,0:T(8,128)(2,1)S(1)}, bf16[1,2048,1024]{2,1,0:T(8,128)(2,1)}, u32[]{:S(2)}) copy-start(bf16[1,2048,1024]{2,1,0:T(8,128)(2,1)} %param.8) | copy-start | bytes 12582916
  59.4 2.4 copy-start.9
  69.5 23.8 %all-to-all-start.1 = ((bf16[4,1,128,1024]{3,0,1,2:T(4,128)(2,1)}), bf16[4,1,128,1024]{3,0,1,2:T(4,128)(2,1)}, u32[]{:S(2)}, u32[]{:S(2)}) async-start(bf16[4,1,128,1024]{3,0,1,2:T(4,128)(2,1)} %copy.31), calls=%async_computation.1 | async-start | bytes 2097152 | tf_op jit(solution)/shard_map/all_to_all | solution.py:30
  76.4 1.0 copy-start.3
  77.4 6.5 %copy-start.7 = (bf16[1,1024,2048]{2,1,0:T(8,128)(2,1)S(1)}, bf16[1,1024,2048]{2,1,0:T(8,128)(2,1)}, u32[]{:S(2)}) copy-start(bf16[1,1024,2048]{2,1,0:T(8,128)(2,1)} %param.7) | copy-start | bytes 12582916
  83.8 4.2 %copy-start.2 = (bf16[4,128,1,1024]{3,1,0,2:T(8,128)(2,1)S(1)}, bf16[4,128,1,1024]{3,1,0,2:T(8,128)(2,1)}, u32[]{:S(2)}) copy-start(bf16[4,128,1,1024]{3,1,0,2:T(8,128)(2,1)} %copy-done.1) | copy-start | bytes 3145732
  93.2 27.9 %all-to-all-start.3 = ((bf16[4,1,128,1024]{3,0,1,2:T(4,128)(2,1)}), bf16[4,1,128,1024]{3,0,1,2:T(4,128)(2,1)}, u32[]{:S(2)}, u32[]{:S(2)}) async-start(bf16[4,1,128,1024]{3,0,1,2:T(4,128)(2,1)} %copy.36), calls=%async_computation.3 | async-start | bytes 2097152 | tf_op jit(solution)/shard_map/all_to_all | solution.py:30
  102.7 167.4 %all-reduce.2.cloned.1.call-start = ((), (), s32[]{:S(2)}) async-start(), calls=%async_computation.4 | async-start | bytes 1048576 | tf_op jit(solution)/shard_map/psum | solution.py:96
  103.0 6.4 %copy-start.8 = (bf16[4,256,1024]{2,1,0:T(8,128)(2,1)S(1)}, bf16[4,256,1024]{2,1,0:T(8,128)(2,1)}, u32[]{:S(2)}) copy-start(bf16[4,256,1024]{2,1,0:T(8,128)(2,1)} %param.9) | copy-start | bytes 6291460
  103.0 8.4 %copy-start.5 = (f32[4,256,128]{2,1,0:T(8,128)S(1)}, f32[4,256,128]{2,1,0:T(8,128)}, u32[]{:S(2)}) copy-start(f32[4,256,128]{2,1,0:T(8,128)} %get-tuple-element.25) | copy-start | bytes 1572868
  123.8 7.0 %copy-start.4 = (bf16[1024,128]{1,0:T(8,128)(2,1)S(1)}, bf16[1024,128]{1,0:T(8,128)(2,1)}, u32[]{:S(2)}) copy-start(bf16[1024,128]{1,0:T(8,128)(2,1)} %param.6) | copy-start | bytes 786436
Sparse Core Ops, SparseCore 0:
  126.8 143.3 all-reduce.1
where the time goes:
time: 280 us; the launch traced here: 279 us
  waiting for transfers between devices  150 us (54%)
  matrix products  57.6 us (21%)
  starting transfers between devices  32.4 us (12%)
  local copies, waits for them, and re-layouts  17.3 us (6%)
  between operations  14.2 us (5%)
  other arithmetic  7.72 us (3%)
    psum x1, waiting for transfers between devices, body(): grad_phi = lax.psum(phi_term, ('gx', 'gy'))  130 us
    all_to_all x2, starting transfers between devices, direct_in(): lax.all_to_all(slot_rows.reshape(count, slot_count, 1, model_width), ('gx...  17.3 us
    all_to_all x2, waiting for transfers between devices, direct_in(): lax.all_to_all(slot_rows.reshape(count, slot_count, 1, model_width), ('gx...  15.6 us
    all_to_all x2, starting transfers between devices, direct_out(): lax.all_to_all(expert_rows.reshape(count, 1, -1, model_width), ('gx', 'gy...  14.8 us
    dot_general x1, matrix products, body(): hidden = jnp.dot(expert_rows, expand, preferred_element_type=jnp.float32)  6.75 us
    dot_general x1, matrix products, body(): jnp.dot(grad_rows, shrink.T, preferred_element_type=jnp.float32)  6.44 us
    dot_general x1, matrix products, body(): jnp.dot(activated.T, grad_rows, preferred_element_type=jnp.float32)  6.4 us
    sub x1, other arithmetic, body(): grad_combine - jnp.sum(combine_prob * grad_combine, axis=2, keepdims=True)  6.32 us
  transfers between devices with their start and end apart: 5, of which 5 were waited for; matrix products, arithmetic and copies ran while one was open for 24% of the time, Pallas kernels for 0%

commit v1 on v0

v1 whole, which is shorter than its diff:
```python
import jax
import jax.numpy as jnp
from jax import lax
from jax.sharding import PartitionSpec as P

AXES = ("gx", "gy")


def gelu_value(values_in):
    return 0.5 * values_in * (1.0 + jax.scipy.special.erf(values_in * 0.7071067811865476))


def gelu_slope(values_in):
    cumulative = 0.5 * (1.0 + jax.scipy.special.erf(values_in * 0.7071067811865476))
    return cumulative + values_in * jnp.exp(-0.5 * values_in * values_in) * 0.3989422804014327


def exchange(chunks):
    return lax.all_to_all(chunks, AXES, split_axis=0, concat_axis=0, tiled=True)


def sum_everywhere(partial):
    parts = lax.axis_size(AXES)
    rows, columns = partial.shape
    pieces = partial.astype(jnp.bfloat16).reshape(parts, rows // parts, columns)
    own = jnp.sum(exchange(pieces).astype(jnp.float32), axis=0).astype(jnp.bfloat16)
    copies = jnp.broadcast_to(own[None], (parts,) + own.shape)
    return exchange(copies).astype(jnp.float32).reshape(rows, columns)


def body(tokens, slot_params, expand_weight, shrink_weight, cotangent):
    images = tokens.shape[0]
    model_width = tokens.shape[2]
    logits = jnp.einsum("ipd,ds->ips", tokens, slot_params, preferred_element_type=jnp.float32)
    dispatch_prob = jax.nn.softmax(logits, axis=1)
    combine_prob = jax.nn.softmax(logits, axis=2)
    dispatch = dispatch_prob.astype(jnp.bfloat16)
    combine = combine_prob.astype(jnp.bfloat16)
    slot_in = jnp.einsum(
        "ips,ipd->sid", dispatch, tokens, preferred_element_type=jnp.float32
    ).astype(jnp.bfloat16)
    grad_slot_out = jnp.einsum(
        "ips,ipd->sid", combine, cotangent, preferred_element_type=jnp.float32
    ).astype(jnp.bfloat16)
    arrived = exchange(jnp.concatenate([slot_in, grad_slot_out], axis=1))
    expert_rows = arrived[:, :images].reshape(-1, model_width)
    grad_rows = arrived[:, images:].reshape(-1, model_width)
    expand = expand_weight[0]
    shrink = shrink_weight[0]
    hidden = jnp.dot(expert_rows, expand, preferred_element_type=jnp.float32)
    activated = gelu_value(hidden).astype(jnp.bfloat16)
    result_rows = jnp.dot(activated, shrink, preferred_element_type=jnp.float32).astype(
        jnp.bfloat16
    )
    grad_activated = jnp.dot(grad_rows, shrink.T, preferred_element_type=jnp.float32)
    grad_hidden = (grad_activated * gelu_slope(hidden)).astype(jnp.bfloat16)
    grad_input_rows = jnp.dot(grad_hidden, expand.T, preferred_element_type=jnp.float32).astype(
        jnp.bfloat16
    )
    returned = exchange(
        jnp.concatenate(
            [
                result_rows.reshape(-1, images, model_width),
                grad_input_rows.reshape(-1, images, model_width),
            ],
            axis=1,
        )
    )
    slot_out = returned[:, :images]
    grad_slot_in = returned[:, images:]
    grad_shrink = jnp.dot(activated.T, grad_rows, preferred_element_type=jnp.float32).astype(
        jnp.bfloat16
    )
    grad_expand = jnp.dot(expert_rows.T, grad_hidden, preferred_element_type=jnp.float32).astype(
        jnp.bfloat16
    )
    grad_combine = jnp.einsum(
        "ipd,sid->ips", cotangent, slot_out, preferred_element_type=jnp.float32
    )
    grad_dispatch = jnp.einsum(
        "ipd,sid->ips", tokens, grad_slot_in, preferred_element_type=jnp.float32
    )
    part_dispatch = dispatch_prob * (
        grad_dispatch - jnp.sum(dispatch_prob * grad_dispatch, axis=1, keepdims=True)
    )
    part_combine = combine_prob * (
        grad_combine - jnp.sum(combine_prob * grad_combine, axis=2, keepdims=True)
    )
    grad_logits = (part_dispatch + part_combine).astype(jnp.bfloat16)
    phi_term = jnp.einsum("ipd,ips->ds", tokens, grad_logits, preferred_element_type=jnp.float32)
    grad_phi = sum_everywhere(phi_term)
    layer_out = jnp.einsum(
        "ips,sid->ipd", combine, slot_out, preferred_element_type=jnp.float32
    ).astype(jnp.bfloat16)
    grad_tokens = (
        jnp.einsum("ips,sid->ipd", dispatch, grad_slot_in, preferred_element_type=jnp.float32)
        + jnp.einsum("ips,ds->ipd", grad_logits, slot_params, preferred_element_type=jnp.float32)
    ).astype(jnp.bfloat16)
    return (layer_out, grad_tokens, grad_phi, grad_expand[None], grad_shrink[None])


def solution(mesh):
    placed = (
        P(("gx", "gy"), None, None),
        P(),
        P(("gx", "gy"), None, None),
        P(("gx", "gy"), None, None),
        P(("gx", "gy"), None, None),
    )
    return jax.shard_map(
        body,
        mesh=mesh,
        in_specs=placed,
        out_specs=(
            P(("gx", "gy"), None, None),
            P(("gx", "gy"), None, None),
            P(),
            P(("gx", "gy"), None, None),
            P(("gx", "gy"), None, None),
        ),
        check_vma=False,
    )
```

time: 280 us -> 185 us (0.66)
  waiting for transfers between devices: 150 us -> 30.6 us
  blocking collectives: 0 us -> 41.4 us
  starting transfers between devices: 32.4 us -> 15 us
  between operations: 14.2 us -> 0.76 us
  other arithmetic: 7.72 us -> 16.1 us
  local copies, waits for them, and re-layouts: 17.3 us -> 21.6 us
    psum x1 -> x0, waiting for transfers between devices: 130 us -> none  [body(): grad_phi = lax.psum(phi_term, ('gx', 'gy'))]
    all_to_all x0 -> x1, blocking collectives: none -> 41.4 us  [exchange(): return lax.all_to_all(chunks, AXES, split_axis=0, concat_axis=0, tiled=True)]
    all_to_all x4 -> x3, starting transfers between devices: 32.1 us -> 15 us  [exchange(): return lax.all_to_all(chunks, AXES, split_axis=0, concat_axis=0, tiled=True)]
    all_to_all x4 -> x3, waiting for transfers between devices: 19.8 us -> 30.6 us  [exchange(): return lax.all_to_all(chunks, AXES, split_axis=0, concat_axis=0, tiled=True)]
    slice x0 -> x2, local copies, waits for them, and re-layouts: none -> 6.2 us  [the longest x1 4.18 us: body(): grad_slot_in = returned[:, images:]]
    concatenate x0 -> x2, other arithmetic: none -> 5.6 us  [the longest x1 3.88 us: body(): jnp.concatenate([result_rows.reshape(-1, images, model_width), grad_input...]
    dot_general x1, matrix products: 2.34 us -> 6.12 us  [body(): jnp.dot(activated, shrink, preferred_element_type=jnp.float32)]
    all_to_all x2 -> x0, local copies, waits for them, and re-layouts: 3.07 us -> none  [direct_in(): lax.all_to_all(slot_rows.reshape(count, slot_count, 1, model_width), ('gx...]
  transfers between devices with their start and end apart: 5 -> 3, of which waited for: 5 -> 3; matrix products, arithmetic and copies ran while one was open for 24% -> 11% of each run, Pallas kernels for 0% -> 0%
where the time goes in v1:
time: 185 us; the launch traced here: 184 us
  matrix products  58.7 us (32%)
  blocking collectives  41.4 us (22%)
  waiting for transfers between devices  30.6 us (17%)
  local copies, waits for them, and re-layouts  21.6 us (12%)
  other arithmetic  16.1 us (9%)
  starting transfers between devices  15 us (8%)
    all_to_all x1, blocking collectives, exchange(): return lax.all_to_all(chunks, AXES, split_axis=0, concat_axis=0, tiled=True)  41.4 us
    all_to_all x3, waiting for transfers between devices, exchange(): return lax.all_to_all(chunks, AXES, split_axis=0, concat_axis=0, tiled=True)  30.6 us
    all_to_all x3, starting transfers between devices, exchange(): return lax.all_to_all(chunks, AXES, split_axis=0, concat_axis=0, tiled=True)  15 us
    sub x1, other arithmetic, body(): grad_combine - jnp.sum(combine_prob * grad_combine, axis=2, keepdims=True)  7.57 us
    dot_general x1, matrix products, body(): hidden = jnp.dot(expert_rows, expand, preferred_element_type=jnp.float32)  6.58 us
    dot_general x1, matrix products, body(): jnp.dot(expert_rows.T, grad_hidden, preferred_element_type=jnp.float32)  6.46 us
    dot_general x1, matrix products, body(): jnp.dot(activated, shrink, preferred_element_type=jnp.float32)  6.12 us
    dot_general x1, matrix products, body(): jnp.einsum('ips,ds->ipd', grad_logits, slot_params, preferred_element_typ...  5.07 us
  transfers between devices with their start and end apart: 3, of which 3 were waited for; matrix products, arithmetic and copies ran while one was open for 11% of the time, Pallas kernels for 0%

profile of v1, /device:TPU:1, one launch (start us, length us, event | category | flops | bytes accessed | tf_op | source)
XLA Modules:
  0.0 184.2 jit_solution(5761489619498448314)
XLA Ops:
  0.6 0.0 copy-start
  0.6 1.6 copy-done
  2.2 1.6 fusion.51
  3.9 0.9 fusion.62
  4.8 1.0 fusion.61
  5.8 1.5 fusion.26
  7.3 4.7 %fusion.27 = bf16[128,4,1024]{2,0,1:T(8,128)(2,1)} fusion(bf16[4,256,1024]{2,1,0:T(8,128)(2,1)} %param.9, f32[4,256]{1,0:T(4,128)S(1)} %get-tuple-element.9, f32[4,256,128]{2,1,0:T(8,128)S(1)} %fusion.51), kind=kOutput, calls=%fused_computation.32 | convolution fusion | flops 269354112 | bytes 3674112 | tf_op jit(solution)/shard_map/ips,ipd->sid/dot_general | solution.py:42
  12.0 1.7 pad_maximum_fusion
  13.8 1.2 copy.29
  14.9 41.4 %all_to_all.20 = bf16[128,8,1024]{2,1,0:T(8,128)(2,1)S(1)} all-to-all(bf16[128,8,1024]{2,1,0:T(8,128)(2,1)S(1)} %copy.29), channel_id=1, replica_groups=mesh['gx'=32,'gy'=4] {'gx','gy'}, dimensions={0} | all-to-all | bytes 4194304 | tf_op jit(solution)/shard_map/all_to_all | solution.py:19
  56.3 2.0 %fusion.60 = (bf16[128,4,1024]{2,1,0:T(4,128)(2,1)}, bf16[128,4,1024]{2,1,0:T(4,128)(2,1)}) fusion(bf16[128,8,1024]{2,1,0:T(8,128)(2,1)S(1)} %all_to_all.20), kind=kLoop, calls=%fused_computation.71 | loop fusion | bytes 4194304 | tf_op jit(solution)/shard_map/slice | solution.py:47
  58.4 2.1 %reshape.38 = bf16[512,1024]{1,0:T(8,128)(2,1)} reshape(bf16[128,4,1024]{2,1,0:T(4,128)(2,1)} %get-tuple-element.8) | data formatting | bytes 2097152 | tf_op jit(solution)/shard_map/reshape | solution.py:46
  60.5 2.1 %reshape.40 = bf16[512,1024]{1,0:T(8,128)(2,1)} reshape(bf16[128,4,1024]{2,1,0:T(4,128)(2,1)} %get-tuple-element.7) | data formatting | bytes 2097152 | tf_op jit(solution)/shard_map/reshape | solution.py:47
  62.7 0.0 copy-start.2
  62.7 0.0 copy-start.6
  62.7 6.6 %multiply_convert_fusion = (bf16[512,2048]{1,0:T(8,128)(2,1)}, f32[512,2048]{1,0:T(8,128)S(1)}) fusion(bf16[512,1024]{1,0:T(8,128)(2,1)} %reshape.38, bf16[1,1024,2048]{2,1,0:T(8,128)(2,1)} %param.7), kind=kOutput, calls=%fused_computation.22 | convolution fusion | flops 2152726528 | bytes 11534336 | tf_op jit(solution)/shard_map/dot_general | solution.py:50
  69.2 0.0 copy-done.2
  69.2 0.0 copy-done.6
  69.2 0.0 copy-start.5
  69.2 3.5 %fusion.9 = bf16[512,2048]{1,0:T(8,128)(2,1)S(1)} fusion(f32[512,2048]{1,0:T(8,128)S(1)} %get-tuple-element.14, bf16[512,1024]{1,0:T(8,128)(2,1)S(1)} %copy-done.2, bf16[1,2048,1024]{2,1,0:T(8,128)(2,1)S(1)} %copy-done.6), kind=kOutput, calls=%fused_computation.10 | convolution fusion | flops 2157969408 | bytes 11534336 | tf_op jit(solution)/shard_map/dot_general | solution.py:55
  72.8 0.0 copy-start.8
  72.8 1.3 copy-done.8
  74.1 0.0 copy-done.5
  74.1 3.3 %fusion.20 = bf16[512,1024]{1,0:T(8,128)(2,1)} fusion(bf16[512,2048]{1,0:T(8,128)(2,1)S(1)} %fusion.9, bf16[1,1024,2048]{2,1,0:T(8,128)(2,1)S(1)} %copy-done.5), kind=kOutput, calls=%fused_computation.29 | convolution fusion | flops 2148007936 | bytes 7340032 | tf_op jit(solution)/shard_map/dot_general | solution.py:57
  77.5 2.2 %reshape.41 = bf16[128,4,1024]{2,1,0:T(4,128)(2,1)} reshape(bf16[512,1024]{1,0:T(8,128)(2,1)} %fusion.20) | data formatting | bytes 2097152 | tf_op jit(solution)/shard_map/reshape | solution.py:64
  79.7 6.1 %fusion.23 = bf16[512,1024]{1,0:T(8,128)(2,1)} fusion(bf16[512,2048]{1,0:T(8,128)(2,1)} %get-tuple-element.13, bf16[1,2048,1024]{2,1,0:T(8,128)(2,1)} %param.8), kind=kOutput, calls=%fused_computation.30 | convolution fusion | flops 2148007936 | bytes 7340032 | tf_op jit(solution)/shard_map/dot_general | solution.py:52
  85.8 2.3 %reshape.39 = bf16[128,4,1024]{2,1,0:T(4,128)(2,1)} reshape(bf16[512,1024]{1,0:T(8,128)(2,1)} %fusion.23) | data formatting | bytes 2097152 | tf_op jit(solution)/shard_map/reshape | solution.py:63
  88.1 3.9 %pad_maximum_fusion.1 = bf16[128,8,1024]{2,1,0:T(8,128)(2,1)} fusion(bf16[128,4,1024]{2,1,0:T(4,128)(2,1)} %reshape.41, bf16[128,4,1024]{2,1,0:T(4,128)(2,1)} %reshape.39), kind=kLoop, calls=%fused_computation.25 | loop fusion | flops 4194304 | bytes 4194304 | tf_op jit(solution)/shard_map/concatenate | solution.py:61
  92.0 5.4 %all-to-all-start.1 = ((bf16[128,8,1024]{2,1,0:T(8,128)(2,1)}), bf16[128,8,1024]{2,1,0:T(8,128)(2,1)}, u32[]{:S(2)}, u32[]{:S(2)}) async-start(bf16[128,8,1024]{2,1,0:T(8,128)(2,1)} %pad_maximum_fusion.1), calls=%async_computation.1 | async-start | bytes 4194304 | tf_op jit(solution)/shard_map/all_to_all | solution.py:19
  97.4 0.0 copy-start.3
  97.4 0.0 copy-start.7
  97.4 6.5 %convert_bitcast_fusion.1 = bf16[1,1024,2048]{2,1,0:T(8,128)(2,1)} fusion(bf16[512,1024]{1,0:T(8,128)(2,1)} %reshape.38, bf16[512,2048]{1,0:T(8,128)(2,1)} %copy-done.8), kind=kOutput, calls=%fused_computation.20 | convolution fusion | flops 2149580800 | bytes 7340032 | tf_op jit(solution)/shard_map/dot_general | solution.py:74
  103.8 0.0 copy-done.3
  103.9 0.0 copy-done.7
  103.9 4.4 %convert_bitcast_fusion = bf16[1,2048,1024]{2,1,0:T(8,128)(2,1)} fusion(bf16[512,2048]{1,0:T(8,128)(2,1)S(1)} %copy-done.7, bf16[512,1024]{1,0:T(8,128)(2,1)S(1)} %copy-done.3), kind=kOutput, calls=%fused_computation.19 | convolution fusion | flops 2149580800 | bytes 7340032 | tf_op jit(solution)/shard_map/dot_general | solution.py:71
  108.3 18.9 %all-to-all-done.1 = bf16[128,8,1024]{2,1,0:T(8,128)(2,1)} async-done(((bf16[128,8,1024]{2,1,0:T(8,128)(2,1)}), bf16[128,8,1024]{2,1,0:T(8,128)(2,1)}, u32[]{:S(2)}, u32[]{:S(2)}) %all-to-all-start.1) | async-done | bytes 2097184 | tf_op jit(solution)/shard_map/all_to_all | solution.py:19
  127.1 4.2 %fusion.59 = (bf16[128,4,1024]{2,1,0:T(4,128)(2,1)S(1)}, bf16[128,4,1024]{2,1,0:T(4,128)(2,1)}) fusion(bf16[128,8,1024]{2,1,0:T(8,128)(2,1)} %all-to-all-done.1), kind=kLoop, calls=%fused_computation.70 | loop fusion | bytes 4194304 | tf_op jit(solution)/shard_map/slice | solution.py:70
  131.3 0.0 copy-start.1
  131.3 1.0 copy-done.1
  132.3 1.6 convolution_bitcast_fusion.2
  133.8 4.2 %fusion.45 = f32[4,256,1024]{2,1,0:T(8,128)} fusion(bf16[128,4,1024]{2,1,0:T(4,128)(2,1)} %copy-done.1, f32[4,128]{1,0:T(4,128)S(1)} %get-tuple-element.11, f32[4,256,128]{2,1,0:T(8,128)S(1)} %fusion.51), kind=kOutput, calls=%fused_computation.52 | convolution fusion | flops 268829440 | bytes 5769216 | tf_op jit(solution)/shard_map/ips,sid->ipd/dot_general | solution.py:96
  138.0 2.6 %convolution_bitcast_fusion.1 = f32[4,256,128]{2,1,0:T(8,128)S(1)} fusion(bf16[4,256,1024]{2,1,0:T(8,128)(2,1)} %param.9, bf16[128,4,1024]{2,1,0:T(4,128)(2,1)} %get-tuple-element.6), kind=kOutput, calls=%fused_computation.38 | convolution fusion | flops 268435456 | bytes 3670016 | tf_op jit(solution)/shard_map/ipd,sid->ips/dot_general | solution.py:77
  140.7 0.0 copy-start.4
  140.7 7.6 %fusion.36 = f32[4,256,128]{2,1,0:T(8,128)} fusion(f32[4,256,128]{2,1,0:T(8,128)S(1)} %convolution_bitcast_fusion.1, f32[4,256,128]{2,1,0:T(8,128)} %get-tuple-element.10, f32[4,256]{1,0:T(4,128)S(1)} %get-tuple-element.9), kind=kOutput, calls=%fused_computation.44 | output fusion | flops 656511 | bytes 1576960 | tf_op jit(solution)/shard_map/sub | solution.py:87
  148.2 2.3 %fusion.39 = bf16[1024,128]{0,1:T(8,128)(2,1)S(1)} fusion(bf16[4,256,1024]{2,1,0:T(8,128)(2,1)S(1)} %copy-done, f32[4,256,128]{2,1,0:T(8,128)} %fusion.36, f32[4,256,128]{2,1,0:T(8,128)} %convolution_bitcast_fusion.2, f32[4,256,128]{2,1,0:T(8,128)} %get-tuple-element.12, f32[4,128]{1,0:T(4,128)S(1)} %get-tuple-element.11), kind=kOutput, calls=%fused_computation.47 | convolution fusion | flops 269484800 | bytes 3934208 | tf_op jit(solution)/shard_map/ipd,ips->ds/dot_general | solution.py:90
  150.5 0.8 copy.35
  151.4 4.9 %all-to-all-start.2 = ((bf16[128,8,128]{2,1,0:T(8,128)(2,1)}), bf16[128,8,128]{2,1,0:T(8,128)(2,1)S(1)}, u32[]{:S(2)}, u32[]{:S(2)}) async-start(bf16[128,8,128]{2,1,0:T(8,128)(2,1)} %bitcast.9), calls=%async_computation.2 | async-start | bytes 524288 | tf_op jit(solution)/shard_map/all_to_all | solution.py:19
  156.3 0.0 copy-done.4
  156.3 5.1 %add_convert_fusion = bf16[4,256,1024]{2,1,0:T(8,128)(2,1)} fusion(f32[4,256,1024]{2,1,0:T(8,128)} %fusion.45, f32[4,256,128]{2,1,0:T(8,128)} %fusion.36, f32[4,256,128]{2,1,0:T(8,128)} %convolution_bitcast_fusion.2, bf16[1024,128]{1,0:T(8,128)(2,1)S(1)} %copy-done.4, f32[4,256,128]{2,1,0:T(8,128)} %get-tuple-element.12, f32[4,128]{1,0:T(4,128)S(1)} %get-tuple-element.11), kind=kOutput, calls=%fused_computation.21 | convolution fusion | flops 271450880 | bytes 8128512 | tf_op jit(solution)/shard_map/ips,ds->ipd/dot_general | solution.py:97
  161.4 5.7 %all-to-all-done.2 = bf16[128,8,128]{2,1,0:T(8,128)(2,1)S(1)} async-done(((bf16[128,8,128]{2,1,0:T(8,128)(2,1)}), bf16[128,8,128]{2,1,0:T(8,128)(2,1)S(1)}, u32[]{:S(2)}, u32[]{:S(2)}) %all-to-all-start.2) | async-done | bytes 262176 | tf_op jit(solution)/shard_map/all_to_all | solution.py:19
  167.1 0.1 reduce_sum.52
  167.2 0.7 broadcast_in_dim.6
  167.9 4.6 %all-to-all-start.3 = ((bf16[128,8,128]{2,1,0:T(8,128)(2,1)}), bf16[128,8,128]{2,1,0:T(8,128)(2,1)S(1)}, u32[]{:S(2)}, u32[]{:S(2)}) async-start(bf16[128,8,128]{2,1,0:T(8,128)(2,1)} %broadcast_in_dim.6), calls=%async_computation.3 | async-start | bytes 524288 | tf_op jit(solution)/shard_map/all_to_all | solution.py:19
  172.6 4.6 %convolution_convert_fusion = bf16[4,256,1024]{2,1,0:T(8,128)(2,1)} fusion(bf16[128,4,1024]{2,1,0:T(4,128)(2,1)} %get-tuple-element.6, f32[4,256]{1,0:T(4,128)S(1)} %get-tuple-element.9, f32[4,256,128]{2,1,0:T(8,128)S(1)} %fusion.51), kind=kOutput, calls=%fused_computation.26 | convolution fusion | flops 269878400 | bytes 3674112 | tf_op jit(solution)/shard_map/ips,sid->ipd/dot_general | solution.py:92
  177.2 6.1 %all-to-all-done.3 = bf16[128,8,128]{2,1,0:T(8,128)(2,1)S(1)} async-done(((bf16[128,8,128]{2,1,0:T(8,128)(2,1)}), bf16[128,8,128]{2,1,0:T(8,128)(2,1)S(1)}, u32[]{:S(2)}, u32[]{:S(2)}) %all-to-all-start.3) | async-done | bytes 262176 | tf_op jit(solution)/shard_map/all_to_all | solution.py:19
  183.3 0.8 bitcast_convert_fusion
Async XLA Ops:
  0.6 1.6 copy-start
  62.7 6.6 %copy-start.2 = (bf16[512,1024]{1,0:T(8,128)(2,1)S(1)}, bf16[512,1024]{1,0:T(8,128)(2,1)}, u32[]{:S(2)}) copy-start(bf16[512,1024]{1,0:T(8,128)(2,1)} %reshape.40) | copy-start | bytes 3145732
  62.7 6.6 %copy-start.6 = (bf16[1,2048,1024]{2,1,0:T(8,128)(2,1)S(1)}, bf16[1,2048,1024]{2,1,0:T(8,128)(2,1)}, u32[]{:S(2)}) copy-start(bf16[1,2048,1024]{2,1,0:T(8,128)(2,1)} %param.8) | copy-start | bytes 12582916
  69.2 4.9 %copy-start.5 = (bf16[1,1024,2048]{2,1,0:T(8,128)(2,1)S(1)}, bf16[1,1024,2048]{2,1,0:T(8,128)(2,1)}, u32[]{:S(2)}) copy-start(bf16[1,1024,2048]{2,1,0:T(8,128)(2,1)} %param.7) | copy-start | bytes 12582916
  72.8 1.3 copy-start.8
  92.0 35.2 %all-to-all-start.1 = ((bf16[128,8,1024]{2,1,0:T(8,128)(2,1)}), bf16[128,8,1024]{2,1,0:T(8,128)(2,1)}, u32[]{:S(2)}, u32[]{:S(2)}) async-start(bf16[128,8,1024]{2,1,0:T(8,128)(2,1)} %pad_maximum_fusion.1), calls=%async_computation.1 | async-start | bytes 4194304 | tf_op jit(solution)/shard_map/all_to_all | solution.py:19
  97.4 6.5 %copy-start.3 = (bf16[512,1024]{1,0:T(8,128)(2,1)S(1)}, bf16[512,1024]{1,0:T(8,128)(2,1)}, u32[]{:S(2)}) copy-start(bf16[512,1024]{1,0:T(8,128)(2,1)} %reshape.40) | copy-start | bytes 3145732
  97.4 6.5 %copy-start.7 = (bf16[512,2048]{1,0:T(8,128)(2,1)S(1)}, bf16[512,2048]{1,0:T(8,128)(2,1)}, u32[]{:S(2)}) copy-start(bf16[512,2048]{1,0:T(8,128)(2,1)} %get-tuple-element.13) | copy-start | bytes 6291460
  131.3 1.0 copy-start.1
  140.7 15.7 %copy-start.4 = (bf16[1024,128]{1,0:T(8,128)(2,1)S(1)}, bf16[1024,128]{1,0:T(8,128)(2,1)}, u32[]{:S(2)}) copy-start(bf16[1024,128]{1,0:T(8,128)(2,1)} %param.6) | copy-start | bytes 786436
  151.4 15.7 %all-to-all-start.2 = ((bf16[128,8,128]{2,1,0:T(8,128)(2,1)}), bf16[128,8,128]{2,1,0:T(8,128)(2,1)S(1)}, u32[]{:S(2)}, u32[]{:S(2)}) async-start(bf16[128,8,128]{2,1,0:T(8,128)(2,1)} %bitcast.9), calls=%async_computation.2 | async-start | bytes 524288 | tf_op jit(solution)/shard_map/all_to_all | solution.py:19
  167.9 15.4 %all-to-all-start.3 = ((bf16[128,8,128]{2,1,0:T(8,128)(2,1)}), bf16[128,8,128]{2,1,0:T(8,128)(2,1)S(1)}, u32[]{:S(2)}, u32[]{:S(2)}) async-start(bf16[128,8,128]{2,1,0:T(8,128)(2,1)} %broadcast_in_dim.6), calls=%async_computation.3 | async-start | bytes 524288 | tf_op jit(solution)/shard_map/all_to_all | solution.py:19

commit v2 on v1

v2 whole, which is shorter than its diff:
```python
import jax
import jax.numpy as jnp
from jax import lax
from jax.experimental import pallas as pl
from jax.experimental.pallas import tpu as pltpu
from jax.sharding import PartitionSpec as P

AXES = ("gx", "gy")
BF16 = jnp.bfloat16
F32 = jnp.float32
TILE = 256
NN = (((1,), (0,)), ((), ()))
NT = (((1,), (1,)), ((), ()))


def mul(left, right, how=NN):
    return lax.dot_general(left, right, how, preferred_element_type=F32)


def exchange(chunks):
    return lax.all_to_all(chunks, AXES, split_axis=0, concat_axis=0, tiled=True)


def one_hot_rows(kinds, grouped_to_mixed):
    span = TILE // kinds
    row = lax.broadcasted_iota(jnp.int32, (TILE, TILE), 0)
    column = lax.broadcasted_iota(jnp.int32, (TILE, TILE), 1)
    if grouped_to_mixed:
        source = (row % kinds) * span + row // kinds
    else:
        source = (row % span) * kinds + row // span
    return jnp.where(column == source, 1.0, 0.0).astype(BF16)


def pre_kernel(tokens_ref, cotangent_ref, params_ref, send_ref, dispatch_ref, combine_ref, rows_ref):
    step = pl.program_id(0)
    images = rows_ref.shape[0] // 2

    @pl.when(step < images)
    def _():
        one_image = tokens_ref[0]
        logits = mul(one_image, params_ref[...])
        down = jnp.exp(logits - jnp.max(logits, axis=0, keepdims=True))
        down = down / jnp.sum(down, axis=0, keepdims=True)
        across = jnp.exp(logits - jnp.max(logits, axis=1, keepdims=True))
        across = across / jnp.sum(across, axis=1, keepdims=True)
        dispatch_ref[0] = down
        combine_ref[0] = across
        rows_ref[step] = mul(down.T.astype(BF16), one_image).astype(BF16)
        rows_ref[images + step] = mul(across.T.astype(BF16), cotangent_ref[0]).astype(BF16)

    @pl.when(step >= images)
    def _():
        kinds = 2 * images
        span = TILE // kinds
        block = step - images
        grouped = rows_ref[:, pl.ds(block * span, span), :].reshape(TILE, rows_ref.shape[2])
        send_ref[...] = mul(one_hot_rows(kinds, True), grouped).astype(BF16)


def pre(tokens, cotangent, params):
    images, patches, width = tokens.shape
    slots = params.shape[1]
    kinds = 2 * images
    blocks = slots * kinds // TILE

    def image_map(step):
        return (jnp.minimum(step, images - 1), 0, 0)

    return pl.pallas_call(
        pre_kernel,
        grid=(images + blocks,),
        in_specs=[
            pl.BlockSpec((1, patches, width), image_map),
            pl.BlockSpec((1, patches, width), image_map),
            pl.BlockSpec((width, slots), lambda step: (0, 0)),
        ],
        out_specs=[
            pl.BlockSpec((TILE, width), lambda step: (jnp.maximum(step - images, 0), 0)),
            pl.BlockSpec((1, patches, slots), image_map),
            pl.BlockSpec((1, patches, slots), image_map),
        ],
        out_shape=[
            jax.ShapeDtypeStruct((slots * kinds, width), BF16),
            jax.ShapeDtypeStruct((images, patches, slots), F32),
            jax.ShapeDtypeStruct((images, patches, slots), F32),
        ],
        scratch_shapes=[pltpu.VMEM((kinds, slots, width), BF16)],
        compiler_params=pltpu.CompilerParams(vmem_limit_bytes=24 << 20),
        name="pre",
    )(tokens, cotangent, params)


def expert_kernel(
    kinds,
    arrived_ref,
    expand_ref,
    shrink_ref,
    send_ref,
    rows_ref,
    grads_ref,
    activated_ref,
    hidden_grad_ref,
    result_ref,
    input_grad_ref,
):
    step = pl.program_id(0)
    last = pl.num_programs(0) - 1
    half = TILE // 2
    blocks = arrived_ref.shape[0] // TILE

    @pl.when(step == 0)
    def _():
        order = one_hot_rows(kinds, False)
        for block in range(blocks):
            grouped = mul(order, arrived_ref[block * TILE : (block + 1) * TILE]).astype(BF16)
            rows_ref[block * half : (block + 1) * half] = grouped[:half]
            grads_ref[block * half : (block + 1) * half] = grouped[half:]

    expand = expand_ref[...]
    shrink = shrink_ref[...]
    hidden = mul(rows_ref[...], expand)
    grad_activated = mul(grads_ref[...], shrink, NT)
    cumulative = 0.5 * (1.0 + lax.erf(hidden * 0.7071067811865476))
    bell = jnp.exp(-0.5 * hidden * hidden) * 0.3989422804014327
    activated = (hidden * cumulative).astype(BF16)
    hidden_grad = (grad_activated * (cumulative + hidden * bell)).astype(BF16)
    activated_ref[...] = activated
    hidden_grad_ref[...] = hidden_grad
    result = mul(activated, shrink)
    input_grad = mul(hidden_grad, expand, NT)

    @pl.when(step == 0)
    def _():
        result_ref[...] = result
        input_grad_ref[...] = input_grad

    @pl.when(step > 0)
    def _():
        result_ref[...] += result
        input_grad_ref[...] += input_grad

    @pl.when(step == last)
    def _():
        order = one_hot_rows(kinds, True)
        for block in range(blocks):
            span = slice(block * half, (block + 1) * half)
            grouped = jnp.concatenate(
                [result_ref[span].astype(BF16), input_grad_ref[span].astype(BF16)], axis=0
            )
            send_ref[block * TILE : (block + 1) * TILE] = mul(order, grouped).astype(BF16)


def expert(arrived, expand, shrink, kinds):
    total, width = arrived.shape
    hidden_width = expand.shape[1]
    rows = total // 2
    chunk = 512
    whole = lambda step: (0, 0)
    return pl.pallas_call(
        lambda *refs: expert_kernel(kinds, *refs),
        grid=(hidden_width // chunk,),
        in_specs=[
            pl.BlockSpec((total, width), whole),
            pl.BlockSpec((width, chunk), lambda step: (0, step)),
            pl.BlockSpec((chunk, width), lambda step: (step, 0)),
        ],
        out_specs=[
            pl.BlockSpec((total, width), whole),
            pl.BlockSpec((rows, width), whole),
            pl.BlockSpec((rows, width), whole),
            pl.BlockSpec((rows, chunk), lambda step: (0, step)),
            pl.BlockSpec((rows, chunk), lambda step: (0, step)),
        ],
        out_shape=[
            jax.ShapeDtypeStruct((total, width), BF16),
            jax.ShapeDtypeStruct((rows, width), BF16),
            jax.ShapeDtypeStruct((rows, width), BF16),
            jax.ShapeDtypeStruct((rows, hidden_width), BF16),
            jax.ShapeDtypeStruct((rows, hidden_width), BF16),
        ],
        scratch_shapes=[pltpu.VMEM((rows, width), F32), pltpu.VMEM((rows, width), F32)],
        compiler_params=pltpu.CompilerParams(vmem_limit_bytes=48 << 20),
        name="expert",
    )(arrived, expand, shrink)


def post_kernel(
    arrived_ref,
    tokens_ref,
    cotangent_ref,
    dispatch_ref,
    combine_ref,
    rows_ref,
    grad_logits_ref,
    phi_ref,
    total_ref,
):
    step = pl.program_id(0)
    kinds, slots, width = rows_ref.shape
    images = kinds // 2

    @pl.when(step == 0)
    def _():
        order = one_hot_rows(kinds, False)
        span = TILE // kinds
        for block in range(slots // span):
            grouped = mul(order, arrived_ref[block * TILE : (block + 1) * TILE]).astype(BF16)
            rows_ref[:, block * span : (block + 1) * span, :] = grouped.reshape(kinds, span, width)

    one_image = tokens_ref[0]
    down = dispatch_ref[0]
    across = combine_ref[0]
    grad_combine = mul(cotangent_ref[0], rows_ref[step], NT)
    grad_dispatch = mul(one_image, rows_ref[images + step], NT)
    part_dispatch = down * (grad_dispatch - jnp.sum(down * grad_dispatch, axis=0, keepdims=True))
    part_combine = across * (grad_combine - jnp.sum(across * grad_combine, axis=1, keepdims=True))
    grad_logits = part_dispatch + part_combine
    grad_logits_ref[0] = grad_logits.astype(BF16)
    term = mul(grad_logits.T.astype(BF16), one_image)

    @pl.when(step == 0)
    def _():
        total_ref[...] = term

    @pl.when(step > 0)
    def _():
        total_ref[...] += term

    @pl.when(step == images - 1)
    def _():
        phi_ref[...] = total_ref[...].T.astype(BF16)


def post(arrived, tokens, cotangent, dispatch, combine):
    images, patches, width = tokens.shape
    slots = dispatch.shape[2]
    kinds = 2 * images
    image_map = lambda step: (step, 0, 0)
    return pl.pallas_call(
        post_kernel,
        grid=(images,),
        in_specs=[
            pl.BlockSpec((slots * kinds, width), lambda step: (0, 0)),
            pl.BlockSpec((1, patches, width), image_map),
            pl.BlockSpec((1, patches, width), image_map),
            pl.BlockSpec((1, patches, slots), image_map),
            pl.BlockSpec((1, patches, slots), image_map),
        ],
        out_specs=[
            pl.BlockSpec((kinds, slots, width), lambda step: (0, 0, 0)),
            pl.BlockSpec((1, patches, slots), image_map),
            pl.BlockSpec((width, slots), lambda step: (0, 0)),
        ],
        out_shape=[
            jax.ShapeDtypeStruct((kinds, slots, width), BF16),
            jax.ShapeDtypeStruct((images, patches, slots), BF16),
            jax.ShapeDtypeStruct((width, slots), BF16),
        ],
        scratch_shapes=[pltpu.VMEM((slots, width), F32)],
        compiler_params=pltpu.CompilerParams(vmem_limit_bytes=24 << 20),
        name="post",
    )(arrived, tokens, cotangent, dispatch, combine)


def tail_kernel(
    out_rows_ref, in_rows_ref, dispatch_ref, combine_ref, grad_logits_ref, params_ref, layer_ref, grad_ref
):
    layer_ref[0] = mul(combine_ref[0].astype(BF16), out_rows_ref[0]).astype(BF16)
    grad_ref[0] = (
        mul(dispatch_ref[0].astype(BF16), in_rows_ref[0])
        + mul(grad_logits_ref[0], params_ref[...], NT)
    ).astype(BF16)


def tail(rows, dispatch, combine, grad_logits, params):
    images, patches, slots = dispatch.shape
    width = rows.shape[2]
    image_map = lambda step: (step, 0, 0)
    out = jax.ShapeDtypeStruct((images, patches, width), BF16)
    return pl.pallas_call(
        tail_kernel,
        grid=(images,),
        in_specs=[
            pl.BlockSpec((1, slots, width), image_map),
            pl.BlockSpec((1, slots, width), lambda step: (images + step, 0, 0)),
            pl.BlockSpec((1, patches, slots), image_map),
            pl.BlockSpec((1, patches, slots), image_map),
            pl.BlockSpec((1, patches, slots), image_map),
            pl.BlockSpec((width, slots), lambda step: (0, 0)),
        ],
        out_specs=[
            pl.BlockSpec((1, patches, width), image_map),
            pl.BlockSpec((1, patches, width), image_map),
        ],
        out_shape=[out, out],
        compiler_params=pltpu.CompilerParams(vmem_limit_bytes=24 << 20),
        cost_estimate=pl.CostEstimate(
            flops=6 * images * patches * slots * width, bytes_accessed=8 << 20, transcendentals=0
        ),
        name="tail",
    )(rows, rows, dispatch, combine, grad_logits, params)


def sum_everywhere(partial):
    parts = lax.axis_size(AXES)
    rows, columns = partial.shape
    pieces = partial.reshape(parts, rows // parts, columns)
    own = jnp.sum(exchange(pieces).astype(F32), axis=0).astype(BF16)
    copies = jnp.broadcast_to(own[None], (parts,) + own.shape)
    return exchange(copies).astype(F32).reshape(rows, columns)


def body(tokens, slot_params, expand_weight, shrink_weight, cotangent):
    images, _, width = tokens.shape
    slots = slot_params.shape[1]
    kinds = 2 * images
    send, dispatch, combine = pre(tokens, cotangent, slot_params)
    arrived = exchange(send.reshape(slots, kinds, width)).reshape(slots * kinds, width)
    send_back, expert_rows, grad_rows, activated, grad_hidden = expert(
        arrived, expand_weight[0], shrink_weight[0], kinds
    )
    returned = exchange(send_back.reshape(slots, kinds, width)).reshape(slots * kinds, width)
    grad_shrink = jnp.dot(activated.T, grad_rows, preferred_element_type=F32).astype(BF16)
    grad_expand = jnp.dot(expert_rows.T, grad_hidden, preferred_element_type=F32).astype(BF16)
    rows, grad_logits, phi_term = post(returned, tokens, cotangent, dispatch, combine)
    grad_phi = sum_everywhere(phi_term)
    layer_out, grad_tokens = tail(rows, dispatch, combine, grad_logits, slot_params)
    return (layer_out, grad_tokens, grad_phi, grad_expand[None], grad_shrink[None])


def solution(mesh):
    placed = (
        P(("gx", "gy"), None, None),
        P(),
        P(("gx", "gy"), None, None),
        P(("gx", "gy"), None, None),
        P(("gx", "gy"), None, None),
    )
    return jax.shard_map(
        body,
        mesh=mesh,
        in_specs=placed,
        out_specs=(
            P(("gx", "gy"), None, None),
            P(("gx", "gy"), None, None),
            P(),
            P(("gx", "gy"), None, None),
            P(("gx", "gy"), None, None),
        ),
        check_vma=False,
    )
```

time: 185 us -> 143 us (0.77)
  matrix products: 58.7 us -> 12.6 us
  blocking collectives: 41.4 us -> 76.4 us
  Pallas kernels: 0 us -> 27.5 us
  waiting for transfers between devices: 30.6 us -> 5.1 us
  local copies, waits for them, and re-layouts: 21.6 us -> 5.59 us
  other arithmetic: 16.1 us -> 2.87 us
  starting transfers between devices: 15 us -> 11.4 us
    dot_general x15 -> x2, matrix products: 58.7 us -> 12.6 us  [the longest x1 6.32 us: body(): jnp.dot(expert_rows.T, grad_hidden, preferred_element_type=F32).astype(BF16)]
    all_to_all x1 -> x2, blocking collectives: 41.4 us -> 76.4 us  [exchange(): return lax.all_to_all(chunks, AXES, split_axis=0, concat_axis=0, tiled=True)]
    pallas_call x0 -> x4, Pallas kernels: none -> 27.5 us  [the longest x1 15.7 us: expert(): pl.pallas_call(lambda *refs: expert_kernel(kinds, *refs), grid=(hidden_wi...]
    all_to_all x3 -> x2, waiting for transfers between devices: 30.6 us -> 5.1 us  [exchange(): return lax.all_to_all(chunks, AXES, split_axis=0, concat_axis=0, tiled=True)]
    sub x3 -> x0, other arithmetic: 9.51 us -> none  [the longest x1 7.57 us: body(): grad_combine - jnp.sum(combine_prob * grad_combine, axis=2, keepdims=True)]
    reshape x4 -> x0, local copies, waits for them, and re-layouts: 8.79 us -> none  [the longest x1 2.26 us: body(): result_rows.reshape(-1, images, model_width)]
    slice x2 -> x0, local copies, waits for them, and re-layouts: 6.2 us -> none  [the longest x1 4.18 us: body(): grad_slot_in = returned[:, images:]]
    concatenate x2 -> x0, other arithmetic: 5.6 us -> none  [the longest x1 3.88 us: body(): jnp.concatenate([result_rows.reshape(-1, images, model_width), grad_input...]
  transfers between devices with their start and end apart: 3 -> 2, of which waited for: 3 -> 2; matrix products, arithmetic and copies ran while one was open for 11% -> 9% of each run, Pallas kernels for 0% -> 2%
where the time goes in v2:
time: 143 us; the launch traced here: 142 us
  blocking collectives  76.4 us (53%)
  Pallas kernels  27.5 us (19%)
  matrix products  12.6 us (9%)
  starting transfers between devices  11.4 us (8%)
  local copies, waits for them, and re-layouts  5.59 us (4%)
  waiting for transfers between devices  5.1 us (4%)
  other arithmetic  2.87 us (2%)
    all_to_all x2, blocking collectives, exchange(): return lax.all_to_all(chunks, AXES, split_axis=0, concat_axis=0, tiled=True)  76.4 us
    pallas_call x1, Pallas kernels, expert(): pl.pallas_call(lambda *refs: expert_kernel(kinds, *refs), grid=(hidden_wi...  15.7 us
    all_to_all x2, starting transfers between devices, exchange(): return lax.all_to_all(chunks, AXES, split_axis=0, concat_axis=0, tiled=True)  11.4 us
    dot_general x1, matrix products, body(): jnp.dot(expert_rows.T, grad_hidden, preferred_element_type=F32).astype(BF16)  6.32 us
    dot_general x1, matrix products, body(): jnp.dot(activated.T, grad_rows, preferred_element_type=F32).astype(BF16)  6.29 us
    all_to_all x2, waiting for transfers between devices, exchange(): return lax.all_to_all(chunks, AXES, split_axis=0, concat_axis=0, tiled=True)  5.1 us
    unnamed x18, local copies, waits for them, and re-layouts  4.85 us
    pallas_call x1, Pallas kernels, pre(): pl.pallas_call(pre_kernel, grid=(images + blocks,), in_specs=[pl.BlockSpe...  4.4 us
  transfers between devices with their start and end apart: 2, of which 2 were waited for; matrix products, arithmetic and copies ran while one was open for 9% of the time, Pallas kernels for 2%

profile of v2, /device:TPU:1, one launch (start us, length us, event | category | flops | bytes accessed | tf_op | source)
XLA Modules:
  0.0 142.2 jit_solution(14486599118117409459)
XLA Ops:
  0.6 0.0 copy-start
  0.6 1.6 %copy-done = bf16[4,256,1024]{2,1,0:T(8,128)(2,1)S(1)} copy-done((bf16[4,256,1024]{2,1,0:T(8,128)(2,1)S(1)}, bf16[4,256,1024]{2,1,0:T(8,128)(2,1)}, u32[]{:S(2)}) %copy-start) | copy-done | bytes 2097176
  2.2 0.0 copy-start.2
  2.2 1.6 %copy-done.2 = bf16[4,256,1024]{2,1,0:T(8,128)(2,1)S(1)} copy-done((bf16[4,256,1024]{2,1,0:T(8,128)(2,1)S(1)}, bf16[4,256,1024]{2,1,0:T(8,128)(2,1)}, u32[]{:S(2)}) %copy-start.2) | copy-done | bytes 2097176
  3.8 0.0 copy-start.4
  3.8 0.9 copy-done.4
  4.8 4.4 %pre.1 = (bf16[1024,1024]{1,0:T(8,128)(2,1)S(1)}, f32[4,256,128]{2,1,0:T(8,128)S(1)}, f32[4,256,128]{2,1,0:T(8,128)S(1)}) custom-call(bf16[4,256,1024]{2,1,0:T(8,128)(2,1)S(1)} %copy-done, bf16[4,256,1024]{2,1,0:T(8,128)(2,1)S(1)} %copy-done.2, bf16[1024,128]{1,0:T(8,128)(2,1)S(1)} %copy-done.4), custom_call_target="tpu_custom_call" | custom-call | tf_op jit(solution)/shard_map/pre/pallas_call | solution.py:70
  9.2 41.5 %all_to_all.20 = bf16[128,8,1024]{2,1,0:T(8,128)(2,1)} all-to-all(bf16[128,8,1024]{2,1,0:T(8,128)(2,1)S(1)} %bitcast.20), channel_id=1, replica_groups=mesh['gx'=32,'gy'=4] {'gx','gy'}, dimensions={0} | all-to-all | bytes 4194304 | tf_op jit(solution)/shard_map/all_to_all | solution.py:21
  50.7 15.7 %expert.1 = (bf16[1024,1024]{1,0:T(8,128)(2,1)S(1)}, bf16[512,1024]{1,0:T(8,128)(2,1)S(1)}, bf16[512,1024]{1,0:T(8,128)(2,1)S(1)}, bf16[512,2048]{1,0:T(8,128)(2,1)}, bf16[512,2048]{1,0:T(8,128)(2,1)}) custom-call(bf16[1024,1024]{1,0:T(8,128)(2,1)} %bitcast.22, bf16[1024,2048]{1,0:T(8,128)(2,1)} %bitcast.23, bf16[2048,1024]{1,0:T(8,128)(2,1)} %bitcast.24), custom_call_target="tpu_custom_call" | custom-call | tf_op jit(solution)/shard_map/expert/pallas_call | solution.py:160
  66.4 0.0 copy-start.7
  66.4 0.0 copy-start.8
  66.4 0.0 copy-start.1
  66.4 0.0 copy-start.3
  66.4 34.9 %all_to_all.21 = bf16[128,8,1024]{2,1,0:T(8,128)(2,1)S(1)} all-to-all(bf16[128,8,1024]{2,1,0:T(8,128)(2,1)S(1)} %bitcast.19), channel_id=1, replica_groups=mesh['gx'=32,'gy'=4] {'gx','gy'}, dimensions={0} | all-to-all | bytes 4194304 | tf_op jit(solution)/shard_map/all_to_all | solution.py:21
  101.3 0.0 copy-done.7
  101.3 0.0 copy-done.8
  101.3 0.0 copy-done.1
  101.3 0.0 copy-done.3
  101.3 4.1 %post.1 = (bf16[8,128,1024]{2,1,0:T(8,128)(2,1)S(1)}, bf16[4,256,128]{2,1,0:T(8,128)(2,1)S(1)}, bf16[1024,128]{1,0:T(8,128)(2,1)S(1)}) custom-call(bf16[1024,1024]{1,0:T(8,128)(2,1)S(1)} %bitcast.18, bf16[4,256,1024]{2,1,0:T(8,128)(2,1)S(1)} %copy-done.1, bf16[4,256,1024]{2,1,0:T(8,128)(2,1)S(1)} %copy-done.3, ...), custom_call_target="tpu_custom_call" | custom-call | tf_op jit(solution)/shard_map/post/pallas_call | solution.py:240
  105.4 0.0 copy-start.6
  105.4 0.7 copy-done.6
  106.1 5.4 %all-to-all-start.2 = ((bf16[128,8,128]{2,1,0:T(8,128)(2,1)}), bf16[128,8,128]{2,1,0:T(8,128)(2,1)}, u32[]{:S(2)}, u32[]{:S(2)}) async-start(bf16[128,8,128]{2,1,0:T(8,128)(2,1)} %bitcast.21), calls=%async_computation.2 | async-start | bytes 524288 | tf_op jit(solution)/shard_map/all_to_all | solution.py:21
  111.5 6.3 %convert_bitcast_fusion.1 = bf16[1,1024,2048]{2,1,0:T(8,128)(2,1)} fusion(bf16[512,1024]{1,0:T(8,128)(2,1)} %copy-done.8, bf16[512,2048]{1,0:T(8,128)(2,1)} %get-tuple-element.28), kind=kOutput, calls=%fused_computation.1 | convolution fusion | flops 2149580800 | bytes 7340032 | tf_op jit(solution)/shard_map/dot_general | solution.py:325
  117.8 4.2 %all-to-all-done.2 = bf16[128,8,128]{2,1,0:T(8,128)(2,1)} async-done(((bf16[128,8,128]{2,1,0:T(8,128)(2,1)}), bf16[128,8,128]{2,1,0:T(8,128)(2,1)}, u32[]{:S(2)}, u32[]{:S(2)}) %all-to-all-start.2) | async-done | bytes 262176 | tf_op jit(solution)/shard_map/all_to_all | solution.py:21
  122.0 1.1 reduce_sum.12
  123.1 0.7 broadcast_in_dim.12
  123.8 6.1 %all-to-all-start.3 = ((bf16[128,8,128]{2,1,0:T(8,128)(2,1)}), bf16[128,8,128]{2,1,0:T(8,128)(2,1)}, u32[]{:S(2)}, u32[]{:S(2)}) async-start(bf16[128,8,128]{2,1,0:T(8,128)(2,1)} %broadcast_in_dim.12), calls=%async_computation.3 | async-start | bytes 524288 | tf_op jit(solution)/shard_map/all_to_all | solution.py:21
  129.9 0.0 copy-start.5
  129.9 6.3 %convert_bitcast_fusion = bf16[1,2048,1024]{2,1,0:T(8,128)(2,1)} fusion(bf16[512,2048]{1,0:T(8,128)(2,1)} %get-tuple-element.29, bf16[512,1024]{1,0:T(8,128)(2,1)} %copy-done.7), kind=kOutput, calls=%fused_computation | convolution fusion | flops 2149580800 | bytes 7340032 | tf_op jit(solution)/shard_map/dot_general | solution.py:324
  136.2 0.0 copy-done.5
  136.2 3.3 %tail.1 = (bf16[4,256,1024]{2,1,0:T(8,128)(2,1)}, bf16[4,256,1024]{2,1,0:T(8,128)(2,1)}) custom-call(bf16[8,128,1024]{2,1,0:T(8,128)(2,1)S(1)} %get-tuple-element.22.out_rows_ref.in_rows_ref, bf16[8,128,1024]{2,1,0:T(8,128)(2,1)S(1)} %get-tuple-element.22.out_rows_ref.in_rows_ref, f32[4,256,128]{2,1,0:T(8,128)S(1)} %get-tuple-element.20.dispatch_ref, ...), custom_call_target="tpu_custom_call" | custom-call | flops 805306368 | bytes 8388608 | tf_op jit(solution)/shard_map/tail/pallas_call | solution.py:281
  139.5 0.9 all-to-all-done.3
  140.4 1.8 %bitcast_convert_fusion = f32[1024,128]{1,0:T(8,128)} fusion(bf16[128,8,128]{2,1,0:T(8,128)(2,1)} %all-to-all-done.3), kind=kLoop, calls=%fused_computation.2 | loop fusion | flops 131072 | bytes 786432 | tf_op jit(solution)/shard_map/reshape | solution.py:311
Async XLA Ops:
  0.6 1.6 %copy-start = (bf16[4,256,1024]{2,1,0:T(8,128)(2,1)S(1)}, bf16[4,256,1024]{2,1,0:T(8,128)(2,1)}, u32[]{:S(2)}) copy-start(bf16[4,256,1024]{2,1,0:T(8,128)(2,1)} %tokens_ref.3) | copy-start | bytes 6291460
  2.2 1.6 %copy-start.2 = (bf16[4,256,1024]{2,1,0:T(8,128)(2,1)S(1)}, bf16[4,256,1024]{2,1,0:T(8,128)(2,1)}, u32[]{:S(2)}) copy-start(bf16[4,256,1024]{2,1,0:T(8,128)(2,1)} %cotangent_ref.3) | copy-start | bytes 6291460
  3.8 0.9 copy-start.4
  66.4 34.9 %copy-start.7 = (bf16[512,1024]{1,0:T(8,128)(2,1)}, bf16[512,1024]{1,0:T(8,128)(2,1)S(1)}, u32[]{:S(2)}) copy-start(bf16[512,1024]{1,0:T(8,128)(2,1)S(1)} %get-tuple-element.30) | copy-start | bytes 3145732
  66.4 34.9 %copy-start.8 = (bf16[512,1024]{1,0:T(8,128)(2,1)}, bf16[512,1024]{1,0:T(8,128)(2,1)S(1)}, u32[]{:S(2)}) copy-start(bf16[512,1024]{1,0:T(8,128)(2,1)S(1)} %get-tuple-element.27) | copy-start | bytes 3145732
  66.4 34.9 %copy-start.1 = (bf16[4,256,1024]{2,1,0:T(8,128)(2,1)S(1)}, bf16[4,256,1024]{2,1,0:T(8,128)(2,1)}, u32[]{:S(2)}) copy-start(bf16[4,256,1024]{2,1,0:T(8,128)(2,1)} %tokens_ref.3) | copy-start | bytes 6291460
  66.4 34.9 %copy-start.3 = (bf16[4,256,1024]{2,1,0:T(8,128)(2,1)S(1)}, bf16[4,256,1024]{2,1,0:T(8,128)(2,1)}, u32[]{:S(2)}) copy-start(bf16[4,256,1024]{2,1,0:T(8,128)(2,1)} %cotangent_ref.3) | copy-start | bytes 6291460
  105.4 0.7 copy-start.6
  106.1 15.9 %all-to-all-start.2 = ((bf16[128,8,128]{2,1,0:T(8,128)(2,1)}), bf16[128,8,128]{2,1,0:T(8,128)(2,1)}, u32[]{:S(2)}, u32[]{:S(2)}) async-start(bf16[128,8,128]{2,1,0:T(8,128)(2,1)} %bitcast.21), calls=%async_computation.2 | async-start | bytes 524288 | tf_op jit(solution)/shard_map/all_to_all | solution.py:21
  123.8 16.6 %all-to-all-start.3 = ((bf16[128,8,128]{2,1,0:T(8,128)(2,1)}), bf16[128,8,128]{2,1,0:T(8,128)(2,1)}, u32[]{:S(2)}, u32[]{:S(2)}) async-start(bf16[128,8,128]{2,1,0:T(8,128)(2,1)} %broadcast_in_dim.12), calls=%async_computation.3 | async-start | bytes 524288 | tf_op jit(solution)/shard_map/all_to_all | solution.py:21
  129.9 6.3 %copy-start.5 = (bf16[1024,128]{1,0:T(8,128)(2,1)S(1)}, bf16[1024,128]{1,0:T(8,128)(2,1)}, u32[]{:S(2)}) copy-start(bf16[1024,128]{1,0:T(8,128)(2,1)} %params_ref.3) | copy-start | bytes 786436

commit v3 on v2

v3 whole, which is shorter than its diff:
```python
import jax
import jax.numpy as jnp
from jax import lax
from jax.experimental import pallas as pl
from jax.experimental.pallas import tpu as pltpu
from jax.sharding import PartitionSpec as P

AXES = ("gx", "gy")
BF16 = jnp.bfloat16
F32 = jnp.float32
TILE = 256
NN = (((1,), (0,)), ((), ()))
NT = (((1,), (1,)), ((), ()))
TN = (((0,), (0,)), ((), ()))


def mul(left, right, how=NN):
    return lax.dot_general(left, right, how, preferred_element_type=F32)


def in_space(array, space):
    return pltpu.with_memory_space_constraint(array, space)


def exchange(chunks):
    return lax.all_to_all(chunks, AXES, split_axis=0, concat_axis=0, tiled=True)


def one_hot_rows(kinds, grouped_to_mixed):
    span = TILE // kinds
    row = lax.broadcasted_iota(jnp.int32, (TILE, TILE), 0)
    column = lax.broadcasted_iota(jnp.int32, (TILE, TILE), 1)
    if grouped_to_mixed:
        source = (row % kinds) * span + row // kinds
    else:
        source = (row % span) * kinds + row // span
    return jnp.where(column == source, 1.0, 0.0).astype(BF16)


def pre_kernel(tokens_ref, cotangent_ref, params_ref, send_ref, dispatch_ref, combine_ref, rows_ref):
    step = pl.program_id(0)
    images = rows_ref.shape[0] // 2

    @pl.when(step < images)
    def _():
        one_image = tokens_ref[0]
        logits = mul(one_image, params_ref[...])
        down = jnp.exp(logits - jnp.max(logits, axis=0, keepdims=True))
        down = down / jnp.sum(down, axis=0, keepdims=True)
        across = jnp.exp(logits - jnp.max(logits, axis=1, keepdims=True))
        across = across / jnp.sum(across, axis=1, keepdims=True)
        dispatch_ref[0] = down
        combine_ref[0] = across
        rows_ref[step] = mul(down.T.astype(BF16), one_image).astype(BF16)
        rows_ref[images + step] = mul(across.T.astype(BF16), cotangent_ref[0]).astype(BF16)

    @pl.when(step >= images)
    def _():
        kinds = 2 * images
        span = TILE // kinds
        block = step - images
        grouped = rows_ref[:, pl.ds(block * span, span), :].reshape(TILE, rows_ref.shape[2])
        send_ref[...] = mul(one_hot_rows(kinds, True), grouped).astype(BF16)


def pre(tokens, cotangent, params):
    images, patches, width = tokens.shape
    slots = params.shape[1]
    kinds = 2 * images
    blocks = slots * kinds // TILE

    def image_map(step):
        return (jnp.minimum(step, images - 1), 0, 0)

    return pl.pallas_call(
        pre_kernel,
        grid=(images + blocks,),
        in_specs=[
            pl.BlockSpec((1, patches, width), image_map),
            pl.BlockSpec((1, patches, width), image_map),
            pl.BlockSpec((width, slots), lambda step: (0, 0)),
        ],
        out_specs=[
            pl.BlockSpec((TILE, width), lambda step: (jnp.maximum(step - images, 0), 0)),
            pl.BlockSpec((1, patches, slots), image_map),
            pl.BlockSpec((1, patches, slots), image_map),
        ],
        out_shape=[
            jax.ShapeDtypeStruct((slots * kinds, width), BF16),
            jax.ShapeDtypeStruct((images, patches, slots), F32),
            jax.ShapeDtypeStruct((images, patches, slots), F32),
        ],
        scratch_shapes=[pltpu.VMEM((kinds, slots, width), BF16)],
        compiler_params=pltpu.CompilerParams(vmem_limit_bytes=36 << 20),
        name="pre",
    )(*(in_space(array, pltpu.HBM) for array in (tokens, cotangent, params)))


def whole(*shapes):
    return [pl.BlockSpec(memory_space=pltpu.VMEM) for _ in shapes]


def expert_kernel(
    kinds,
    arrived_ref,
    expand_ref,
    shrink_ref,
    send_ref,
    kept_rows_ref,
    kept_grads_ref,
    activated_ref,
    hidden_grad_ref,
    rows_ref,
    grads_ref,
    rows_sem,
    grads_sem,
):
    half = TILE // 2
    blocks = arrived_ref.shape[0] // TILE
    width, hidden_width = expand_ref.shape
    step = 512

    order = one_hot_rows(kinds, False)
    for block in range(blocks):
        grouped = mul(order, arrived_ref[block * TILE : (block + 1) * TILE]).astype(BF16)
        rows_ref[block * half : (block + 1) * half] = grouped[:half]
        grads_ref[block * half : (block + 1) * half] = grouped[half:]
    keep_rows = pltpu.make_async_copy(rows_ref, kept_rows_ref, rows_sem)
    keep_grads = pltpu.make_async_copy(grads_ref, kept_grads_ref, grads_sem)
    keep_rows.start()
    keep_grads.start()

    def inner(index, carry):
        span = pl.ds(pl.multiple_of(index * step, step), step)
        hidden = mul(rows_ref[...], expand_ref[:, span])
        grad_activated = mul(grads_ref[...], shrink_ref[span, :], NT)
        cumulative = 0.5 * (1.0 + lax.erf(hidden * 0.7071067811865476))
        bell = jnp.exp(-0.5 * hidden * hidden) * 0.3989422804014327
        activated_ref[:, span] = (hidden * cumulative).astype(BF16)
        hidden_grad_ref[:, span] = (grad_activated * (cumulative + hidden * bell)).astype(BF16)
        return carry

    lax.fori_loop(0, hidden_width // step, inner, 0)
    back = one_hot_rows(kinds, True)

    def outer(index, carry):
        span = pl.ds(pl.multiple_of(index * step, step), step)
        result = mul(activated_ref[...], shrink_ref[:, span]).astype(BF16)
        input_grad = mul(hidden_grad_ref[...], expand_ref[span, :], NT).astype(BF16)
        for block in range(blocks):
            part = slice(block * half, (block + 1) * half)
            grouped = jnp.concatenate([result[part], input_grad[part]], axis=0)
            send_ref[block * TILE : (block + 1) * TILE, span] = mul(back, grouped).astype(BF16)
        return carry

    lax.fori_loop(0, width // step, outer, 0)
    keep_rows.wait()
    keep_grads.wait()


def expert(arrived, expand, shrink, kinds):
    total, width = arrived.shape
    hidden_width = expand.shape[1]
    rows = total // 2
    out_shape = [
        jax.ShapeDtypeStruct((total, width), BF16),
        pltpu.HBM((rows, width), BF16),
        pltpu.HBM((rows, width), BF16),
        jax.ShapeDtypeStruct((rows, hidden_width), BF16),
        jax.ShapeDtypeStruct((rows, hidden_width), BF16),
    ]
    vmem = pl.BlockSpec(memory_space=pltpu.VMEM)
    hbm = pl.BlockSpec(memory_space=pltpu.HBM)
    return pl.pallas_call(
        lambda *refs: expert_kernel(kinds, *refs),
        in_specs=whole(arrived, expand, shrink),
        out_specs=[vmem, hbm, hbm, vmem, vmem],
        out_shape=out_shape,
        scratch_shapes=[
            pltpu.VMEM((rows, width), BF16),
            pltpu.VMEM((rows, width), BF16),
            pltpu.SemaphoreType.DMA(()),
            pltpu.SemaphoreType.DMA(()),
        ],
        compiler_params=pltpu.CompilerParams(vmem_limit_bytes=32 << 20),
        name="expert",
    )(arrived, in_space(expand, pltpu.VMEM), in_space(shrink, pltpu.VMEM))


def weights_kernel(rows_ref, grads_ref, activated_ref, hidden_grad_ref, expand_ref, shrink_ref):
    expand_ref[...] = mul(rows_ref[...], hidden_grad_ref[...], TN).astype(BF16)
    shrink_ref[...] = mul(activated_ref[...], grads_ref[...], TN).astype(BF16)


def weights(rows, grads, activated, hidden_grad):
    count, width = rows.shape
    hidden_width = activated.shape[1]
    step = 512
    return pl.pallas_call(
        weights_kernel,
        grid=(hidden_width // step,),
        in_specs=[
            pl.BlockSpec((count, width), lambda index: (0, 0)),
            pl.BlockSpec((count, width), lambda index: (0, 0)),
            pl.BlockSpec((count, step), lambda index: (0, index)),
            pl.BlockSpec((count, step), lambda index: (0, index)),
        ],
        out_specs=[
            pl.BlockSpec((width, step), lambda index: (0, index)),
            pl.BlockSpec((step, width), lambda index: (index, 0)),
        ],
        out_shape=[
            jax.ShapeDtypeStruct((width, hidden_width), BF16),
            jax.ShapeDtypeStruct((hidden_width, width), BF16),
        ],
        compiler_params=pltpu.CompilerParams(vmem_limit_bytes=24 << 20),
        cost_estimate=pl.CostEstimate(
            flops=4 * count * width * hidden_width, bytes_accessed=14 << 20, transcendentals=0
        ),
        name="weights",
    )(*(in_space(array, pltpu.HBM) for array in (rows, grads, activated, hidden_grad)))


def post_kernel(
    images,
    arrived_ref,
    tokens_ref,
    cotangent_ref,
    dispatch_ref,
    combine_ref,
    kept_ref,
    grad_logits_ref,
    phi_ref,
    rows_ref,
    kept_sem,
):
    kinds, slots, width = rows_ref.shape
    span = TILE // kinds
    order = one_hot_rows(kinds, False)
    for block in range(slots // span):
        grouped = mul(order, arrived_ref[block * TILE : (block + 1) * TILE]).astype(BF16)
        rows_ref[:, block * span : (block + 1) * span, :] = grouped.reshape(kinds, span, width)
    keep = pltpu.make_async_copy(rows_ref, kept_ref, kept_sem)
    keep.start()
    total = jnp.zeros((slots, width), F32)
    for image in range(images):
        one_image = tokens_ref[image]
        down = dispatch_ref[image]
        across = combine_ref[image]
        grad_combine = mul(cotangent_ref[image], rows_ref[image], NT)
        grad_dispatch = mul(one_image, rows_ref[images + image], NT)
        grad_logits = down * (
            grad_dispatch - jnp.sum(down * grad_dispatch, axis=0, keepdims=True)
        ) + across * (grad_combine - jnp.sum(across * grad_combine, axis=1, keepdims=True))
        grad_logits_ref[image] = grad_logits.astype(BF16)
        total += mul(grad_logits.T.astype(BF16), one_image)
    phi_ref[...] = total.T.astype(BF16)
    keep.wait()


def post(arrived, tokens, cotangent, dispatch, combine):
    images, patches, width = tokens.shape
    slots = dispatch.shape[2]
    out_shape = [
        pltpu.HBM((2 * images, slots, width), BF16),
        jax.ShapeDtypeStruct((images, patches, slots), BF16),
        jax.ShapeDtypeStruct((width, slots), BF16),
    ]
    return pl.pallas_call(
        lambda *refs: post_kernel(images, *refs),
        in_specs=whole(arrived, tokens, cotangent, dispatch, combine),
        out_specs=[pl.BlockSpec(memory_space=pltpu.HBM)] + whole(*out_shape[1:]),
        out_shape=out_shape,
        scratch_shapes=[pltpu.VMEM(out_shape[0].shape, BF16), pltpu.SemaphoreType.DMA(())],
        compiler_params=pltpu.CompilerParams(vmem_limit_bytes=20 << 20),
        name="post",
    )(arrived, tokens, cotangent, dispatch, combine)


def tail_kernel(rows_ref, dispatch_ref, combine_ref, grad_logits_ref, params_ref, layer_ref, grad_ref):
    step = pl.program_id(0)
    images = pl.num_programs(0)
    layer_ref[0] = mul(combine_ref[step].astype(BF16), rows_ref[step]).astype(BF16)
    grad_ref[0] = (
        mul(dispatch_ref[step].astype(BF16), rows_ref[images + step])
        + mul(grad_logits_ref[step], params_ref[...], NT)
    ).astype(BF16)


def tail(rows, dispatch, combine, grad_logits, params):
    images, patches, slots = dispatch.shape
    width = rows.shape[2]
    image_map = lambda step: (step, 0, 0)
    out = jax.ShapeDtypeStruct((images, patches, width), BF16)
    return pl.pallas_call(
        tail_kernel,
        grid=(images,),
        in_specs=whole(rows, dispatch, combine, grad_logits, params),
        out_specs=[
            pl.BlockSpec((1, patches, width), image_map),
            pl.BlockSpec((1, patches, width), image_map),
        ],
        out_shape=[out, out],
        compiler_params=pltpu.CompilerParams(vmem_limit_bytes=16 << 20),
        cost_estimate=pl.CostEstimate(
            flops=6 * images * patches * slots * width, bytes_accessed=8 << 20, transcendentals=0
        ),
        name="tail",
    )(rows, dispatch, combine, grad_logits, params)


def sum_kernel(pieces_ref, copies_ref):
    own = jnp.sum(pieces_ref[...].astype(F32), axis=0, keepdims=True).astype(BF16)
    copies_ref[...] = jnp.broadcast_to(own, copies_ref.shape)


def widen_kernel(narrow_ref, wide_ref):
    wide_ref[...] = narrow_ref[...].astype(F32)


def sum_everywhere(partial):
    parts = lax.axis_size(AXES)
    rows, columns = partial.shape
    pieces = partial.reshape(parts, rows // parts, columns)
    copies = pl.pallas_call(
        sum_kernel,
        in_specs=whole(pieces),
        out_specs=whole(pieces)[0],
        out_shape=jax.ShapeDtypeStruct(pieces.shape, BF16),
        compiler_params=pltpu.CompilerParams(vmem_limit_bytes=4 << 20),
        name="sum",
    )(exchange(pieces))
    return pl.pallas_call(
        widen_kernel,
        in_specs=whole(partial),
        out_specs=whole(partial)[0],
        out_shape=jax.ShapeDtypeStruct(partial.shape, F32),
        compiler_params=pltpu.CompilerParams(vmem_limit_bytes=4 << 20),
        name="widen",
    )(exchange(copies).reshape(rows, columns))


def body(tokens, slot_params, expand_weight, shrink_weight, cotangent):
    images, _, width = tokens.shape
    slots = slot_params.shape[1]
    kinds = 2 * images
    send, dispatch, combine = pre(tokens, cotangent, slot_params)
    arrived = exchange(send.reshape(slots, kinds, width)).reshape(slots * kinds, width)
    send_back, expert_rows, grad_rows, activated, grad_hidden = expert(
        arrived, expand_weight[0], shrink_weight[0], kinds
    )
    returned = exchange(send_back.reshape(slots, kinds, width)).reshape(slots * kinds, width)
    grad_expand, grad_shrink = weights(expert_rows, grad_rows, activated, grad_hidden)
    rows, grad_logits, phi_term = post(returned, tokens, cotangent, dispatch, combine)
    grad_phi = sum_everywhere(phi_term)
    layer_out, grad_tokens = tail(rows, dispatch, combine, grad_logits, slot_params)
    return (layer_out, grad_tokens, grad_phi, grad_expand[None], grad_shrink[None])


def solution(mesh):
    placed = (
        P(("gx", "gy"), None, None),
        P(),
        P(("gx", "gy"), None, None),
        P(("gx", "gy"), None, None),
        P(("gx", "gy"), None, None),
    )
    return jax.shard_map(
        body,
        mesh=mesh,
        in_specs=placed,
        out_specs=(
            P(("gx", "gy"), None, None),
            P(("gx", "gy"), None, None),
            P(),
            P(("gx", "gy"), None, None),
            P(("gx", "gy"), None, None),
        ),
        check_vma=False,
    )
```

time: 143 us -> 133 us (0.930)
  blocking collectives: 76.4 us -> 91.8 us
  matrix products: 12.6 us -> 0 us
  Pallas kernels: 27.5 us -> 35.3 us
  starting transfers between devices: 11.4 us -> 4.56 us
  local copies, waits for them, and re-layouts: 5.59 us -> 0.05 us
  waiting for transfers between devices: 5.1 us -> 0.01 us
  other arithmetic: 2.87 us -> 0 us
    all_to_all x2 -> x3, blocking collectives: 76.4 us -> 91.8 us  [exchange(): return lax.all_to_all(chunks, AXES, split_axis=0, concat_axis=0, tiled=True)]
    dot_general x2 -> x0, matrix products: 12.6 us -> none  [the longest x1 6.32 us: body(): jnp.dot(expert_rows.T, grad_hidden, preferred_element_type=F32).astype(BF16)]
    all_to_all x2 -> x1, starting transfers between devices: 11.4 us -> 4.56 us  [exchange(): return lax.all_to_all(chunks, AXES, split_axis=0, concat_axis=0, tiled=True)]
    pallas_call x3 -> x6, Pallas kernels: 23.1 us -> 28.9 us  [the longest x1 11.3 us: expert(): pl.pallas_call(lambda *refs: expert_kernel(kinds, *refs), in_specs=whole(...]
    all_to_all x2 -> x1, waiting for transfers between devices: 5.1 us -> 0.01 us  [exchange(): return lax.all_to_all(chunks, AXES, split_axis=0, concat_axis=0, tiled=True)]
    unnamed x18 -> x16, local copies, waits for them, and re-layouts: 4.85 us -> 0.05 us
    pallas_call x1, Pallas kernels: 4.4 us -> 6.41 us  [pre(): pl.pallas_call(pre_kernel, grid=(images + blocks,), in_specs=[pl.BlockSpe...]
    reshape x1 -> x0, other arithmetic: 1.78 us -> none  [sum_everywhere(): return exchange(copies).astype(F32).reshape(rows, columns)]
  transfers between devices with their start and end apart: 2 -> 1, of which waited for: 2 -> 0; matrix products, arithmetic and copies ran while one was open for 9% -> 0% of each run, Pallas kernels for 2% -> 9%
where the time goes in v3:
time: 133 us; the launch traced here: 132 us
  blocking collectives  91.8 us (69%)
  Pallas kernels  35.3 us (27%)
  starting transfers between devices  4.56 us (3%)
    all_to_all x3, blocking collectives, exchange(): return lax.all_to_all(chunks, AXES, split_axis=0, concat_axis=0, tiled=True)  91.8 us
    pallas_call x1, Pallas kernels, expert(): pl.pallas_call(lambda *refs: expert_kernel(kinds, *refs), in_specs=whole(...  11.3 us
    pallas_call x1, Pallas kernels, weights(): pl.pallas_call(weights_kernel, grid=(hidden_width // step,), in_specs=[pl...  8.58 us
    pallas_call x1, Pallas kernels, pre(): pl.pallas_call(pre_kernel, grid=(images + blocks,), in_specs=[pl.BlockSpe...  6.41 us
    all_to_all x1, starting transfers between devices, exchange(): return lax.all_to_all(chunks, AXES, split_axis=0, concat_axis=0, tiled=True)  4.56 us
    pallas_call x1, Pallas kernels, post(): pl.pallas_call(lambda *refs: post_kernel(images, *refs), in_specs=whole(a...  4.02 us
    pallas_call x1, Pallas kernels, tail(): pl.pallas_call(tail_kernel, grid=(images,), in_specs=whole(rows, dispatch...  3.29 us
  transfers between devices with their start and end apart: 1, of which 0 were waited for; matrix products, arithmetic and copies ran while one was open for 0% of the time, Pallas kernels for 9%

profile of v3, /device:TPU:1, one launch (start us, length us, event | category | flops | bytes accessed | tf_op | source)
XLA Modules:
  0.0 132.4 jit_solution(2687608178660600817)
XLA Ops:
  0.6 0.0 copy-start.3
  0.6 6.4 %pre.1 = (bf16[1024,1024]{1,0:T(8,128)(2,1)S(1)}, f32[4,256,128]{2,1,0:T(8,128)S(1)}, f32[4,256,128]{2,1,0:T(8,128)S(1)}) custom-call(bf16[4,256,1024]{2,1,0:T(8,128)(2,1)} %refs_1_.1, bf16[4,256,1024]{2,1,0:T(8,128)(2,1)} %refs_2_.1, bf16[1024,128]{1,0:T(8,128)(2,1)} %params_ref.3), custom_call_target="tpu_custom_call" | custom-call | tf_op jit(solution)/shard_map/pre/pallas_call | solution.py:75
  7.1 0.0 copy-start.2
  7.1 41.4 %all_to_all.20 = bf16[128,8,1024]{2,1,0:T(8,128)(2,1)S(1)} all-to-all(bf16[128,8,1024]{2,1,0:T(8,128)(2,1)S(1)} %bitcast.15), channel_id=1, replica_groups=mesh['gx'=32,'gy'=4] {'gx','gy'}, dimensions={0} | all-to-all | bytes 4194304 | tf_op jit(solution)/shard_map/all_to_all | solution.py:26
  48.5 0.0 copy-done.3
  48.5 0.0 copy-done.2
  48.5 11.3 %expert.1 = (bf16[1024,1024]{1,0:T(8,128)(2,1)S(1)}, bf16[512,1024]{1,0:T(8,128)(2,1)}, bf16[512,1024]{1,0:T(8,128)(2,1)}, bf16[512,2048]{1,0:T(8,128)(2,1)S(1)}, bf16[512,2048]{1,0:T(8,128)(2,1)S(1)}) custom-call(bf16[1024,1024]{1,0:T(8,128)(2,1)S(1)} %bitcast.10, bf16[1024,2048]{1,0:T(8,128)(2,1)S(1)} %bitcast.12, bf16[2048,1024]{1,0:T(8,128)(2,1)S(1)} %bitcast.13), custom_call_target="tpu_custom_call" | custom-call | tf_op jit(solution)/shard_map/expert/pallas_call | solution.py:174
  59.8 0.0 copy-start.6
  59.8 0.0 copy-start.7
  59.8 0.0 copy-start
  59.8 0.0 copy-start.1
  59.8 34.9 %all_to_all.21 = bf16[128,8,1024]{2,1,0:T(8,128)(2,1)S(1)} all-to-all(bf16[128,8,1024]{2,1,0:T(8,128)(2,1)S(1)} %bitcast.14), channel_id=1, replica_groups=mesh['gx'=32,'gy'=4] {'gx','gy'}, dimensions={0} | all-to-all | bytes 4194304 | tf_op jit(solution)/shard_map/all_to_all | solution.py:26
  94.7 0.0 copy-done.6
  94.7 0.0 copy-done.7
  94.7 0.0 copy-done
  94.7 0.0 copy-done.1
  94.7 4.0 %post.1 = (bf16[8,128,1024]{2,1,0:T(8,128)(2,1)}, bf16[4,256,128]{2,1,0:T(8,128)(2,1)S(1)}, bf16[1024,128]{1,0:T(8,128)(2,1)S(1)}) custom-call(bf16[1024,1024]{1,0:T(8,128)(2,1)S(1)} %bitcast.11, bf16[4,256,1024]{2,1,0:T(8,128)(2,1)S(1)} %copy-done, bf16[4,256,1024]{2,1,0:T(8,128)(2,1)S(1)} %copy-done.1, ...), custom_call_target="tpu_custom_call" | custom-call | tf_op jit(solution)/shard_map/post/pallas_call | solution.py:269
  98.7 15.6 %all_to_all.22.pieces_ref = bf16[128,8,128]{2,1,0:T(8,128)(2,1)S(1)} all-to-all(bf16[128,8,128]{2,1,0:T(8,128)(2,1)S(1)} %bitcast.17), channel_id=1, replica_groups=mesh['gx'=32,'gy'=4] {'gx','gy'}, dimensions={0} | all-to-all | bytes 524288 | tf_op jit(solution)/shard_map/all_to_all | solution.py:26
  114.3 0.9 sum.1
  115.1 4.6 %all-to-all-start.3 = ((bf16[128,8,128]{2,1,0:T(8,128)(2,1)}), bf16[128,8,128]{2,1,0:T(8,128)(2,1)S(1)}, u32[]{:S(2)}, u32[]{:S(2)}) async-start(bf16[128,8,128]{2,1,0:T(8,128)(2,1)} %sum.1), calls=%async_computation.3 | async-start | bytes 524288 | tf_op jit(solution)/shard_map/all_to_all | solution.py:26
  119.7 0.0 copy-start.4
  119.7 0.0 copy-start.5
  119.7 8.6 %weights.1 = (bf16[1024,2048]{1,0:T(8,128)(2,1)}, bf16[2048,1024]{1,0:T(8,128)(2,1)}) custom-call(bf16[512,1024]{1,0:T(8,128)(2,1)} %get-tuple-element.29.rows_ref, bf16[512,1024]{1,0:T(8,128)(2,1)} %get-tuple-element.30.grads_ref, bf16[512,2048]{1,0:T(8,128)(2,1)} %copy-done.6, bf16[512,2048]{1,0:T(8,128)(2,1)} %copy-done.7), custom_call_target="tpu_custom_call" | custom-call | flops 4294967296 | bytes 14680064 | tf_op jit(solution)/shard_map/weights/pallas_call | solution.py:199
  128.3 0.0 copy-done.4
  128.3 0.0 copy-done.5
  128.3 3.3 %tail.1 = (bf16[4,256,1024]{2,1,0:T(8,128)(2,1)}, bf16[4,256,1024]{2,1,0:T(8,128)(2,1)}) custom-call(bf16[8,128,1024]{2,1,0:T(8,128)(2,1)S(1)} %copy-done.4, f32[4,256,128]{2,1,0:T(8,128)S(1)} %get-tuple-element.22.refs_3_.dispatch_ref, f32[4,256,128]{2,1,0:T(8,128)S(1)} %get-tuple-element.23.refs_4_.combine_ref, ...), custom_call_target="tpu_custom_call" | custom-call | flops 805306368 | bytes 8388608 | tf_op jit(solution)/shard_map/tail/pallas_call | solution.py:295
  131.6 0.0 all-to-all-done.3
  131.6 0.8 widen.1
Async XLA Ops:
  0.6 47.8 %copy-start.3 = (bf16[1,2048,1024]{2,1,0:T(8,128)(2,1)S(1)}, bf16[1,2048,1024]{2,1,0:T(8,128)(2,1)}, u32[]{:S(2)}) copy-start(bf16[1,2048,1024]{2,1,0:T(8,128)(2,1)} %param.8) | copy-start | bytes 12582916
  7.1 41.4 %copy-start.2 = (bf16[1,1024,2048]{2,1,0:T(8,128)(2,1)S(1)}, bf16[1,1024,2048]{2,1,0:T(8,128)(2,1)}, u32[]{:S(2)}) copy-start(bf16[1,1024,2048]{2,1,0:T(8,128)(2,1)} %param.7) | copy-start | bytes 12582916
  59.8 34.9 %copy-start.6 = (bf16[512,2048]{1,0:T(8,128)(2,1)}, bf16[512,2048]{1,0:T(8,128)(2,1)S(1)}, u32[]{:S(2)}) copy-start(bf16[512,2048]{1,0:T(8,128)(2,1)S(1)} %get-tuple-element.31.activated_ref) | copy-start | bytes 6291460
  59.8 34.9 %copy-start.7 = (bf16[512,2048]{1,0:T(8,128)(2,1)}, bf16[512,2048]{1,0:T(8,128)(2,1)S(1)}, u32[]{:S(2)}) copy-start(bf16[512,2048]{1,0:T(8,128)(2,1)S(1)} %get-tuple-element.32.hidden_grad_ref) | copy-start | bytes 6291460
  59.8 34.9 %copy-start = (bf16[4,256,1024]{2,1,0:T(8,128)(2,1)S(1)}, bf16[4,256,1024]{2,1,0:T(8,128)(2,1)}, u32[]{:S(2)}) copy-start(bf16[4,256,1024]{2,1,0:T(8,128)(2,1)} %refs_1_.1) | copy-start | bytes 6291460
  59.8 34.9 %copy-start.1 = (bf16[4,256,1024]{2,1,0:T(8,128)(2,1)S(1)}, bf16[4,256,1024]{2,1,0:T(8,128)(2,1)}, u32[]{:S(2)}) copy-start(bf16[4,256,1024]{2,1,0:T(8,128)(2,1)} %refs_2_.1) | copy-start | bytes 6291460
  115.1 16.5 %all-to-all-start.3 = ((bf16[128,8,128]{2,1,0:T(8,128)(2,1)}), bf16[128,8,128]{2,1,0:T(8,128)(2,1)S(1)}, u32[]{:S(2)}, u32[]{:S(2)}) async-start(bf16[128,8,128]{2,1,0:T(8,128)(2,1)} %sum.1), calls=%async_computation.3 | async-start | bytes 524288 | tf_op jit(solution)/shard_map/all_to_all | solution.py:26
  119.7 8.6 %copy-start.4 = (bf16[8,128,1024]{2,1,0:T(8,128)(2,1)S(1)}, bf16[8,128,1024]{2,1,0:T(8,128)(2,1)}, u32[]{:S(2)}) copy-start(bf16[8,128,1024]{2,1,0:T(8,128)(2,1)} %get-tuple-element.24.rows_ref) | copy-start | bytes 6291460
  119.7 8.6 %copy-start.5 = (bf16[1024,128]{1,0:T(8,128)(2,1)S(1)}, bf16[1024,128]{1,0:T(8,128)(2,1)}, u32[]{:S(2)}) copy-start(bf16[1024,128]{1,0:T(8,128)(2,1)} %params_ref.3) | copy-start | bytes 786436

commit v4 on v3

v4 whole, which is shorter than its diff:
```python
import jax
import jax.numpy as jnp
from jax import lax
from jax.experimental import pallas as pl
from jax.experimental.pallas import tpu as pltpu
from jax.sharding import PartitionSpec as P

AXES = ("gx", "gy")
BF16 = jnp.bfloat16
F32 = jnp.float32
TILE = 256
NN = (((1,), (0,)), ((), ()))
NT = (((1,), (1,)), ((), ()))


def mul(left, right, how=NN):
    return lax.dot_general(left, right, how, preferred_element_type=F32)


def in_space(array, space):
    return pltpu.with_memory_space_constraint(array, space)


def exchange(chunks):
    return lax.all_to_all(chunks, AXES, split_axis=0, concat_axis=0, tiled=True)


def one_hot_rows(kinds, grouped_to_mixed):
    span = TILE // kinds
    row = lax.broadcasted_iota(jnp.int32, (TILE, TILE), 0)
    column = lax.broadcasted_iota(jnp.int32, (TILE, TILE), 1)
    if grouped_to_mixed:
        source = (row % kinds) * span + row // kinds
    else:
        source = (row % span) * kinds + row // span
    return jnp.where(column == source, 1.0, 0.0).astype(BF16)


def whole(*shapes):
    return [pl.BlockSpec(memory_space=pltpu.VMEM) for _ in shapes]


def pre_kernel(
    tokens_hbm,
    cotangent_hbm,
    params_hbm,
    send_ref,
    dispatch_ref,
    combine_ref,
    tokens_ref,
    cotangent_ref,
    params_ref,
    rows_ref,
    token_sems,
    cotangent_sems,
    params_sem,
):
    images, _, width = tokens_ref.shape
    slots = params_ref.shape[1]
    kinds = 2 * images
    get_params = pltpu.make_async_copy(params_hbm, params_ref, params_sem)
    get_tokens = [
        pltpu.make_async_copy(tokens_hbm.at[n], tokens_ref.at[n], token_sems.at[n])
        for n in range(images)
    ]
    get_cotangent = [
        pltpu.make_async_copy(cotangent_hbm.at[n], cotangent_ref.at[n], cotangent_sems.at[n])
        for n in range(images)
    ]
    get_params.start()
    for copy in get_tokens:
        copy.start()
    get_params.wait()
    for copy in get_tokens:
        copy.wait()
    for copy in get_cotangent:
        copy.start()
    patches = tokens_ref.shape[1]
    all_logits = mul(tokens_ref[...].reshape(images * patches, width), params_ref[...])
    for image in range(images):
        one_image = tokens_ref[image]
        logits = all_logits[image * patches : (image + 1) * patches]
        down = jnp.exp(logits - jnp.max(logits, axis=0, keepdims=True))
        down = down / jnp.sum(down, axis=0, keepdims=True)
        across = jnp.exp(logits - jnp.max(logits, axis=1, keepdims=True))
        across = across / jnp.sum(across, axis=1, keepdims=True)
        dispatch_ref[image] = down
        combine_ref[image] = across
        rows_ref[image] = mul(down.T.astype(BF16), one_image).astype(BF16)
    for copy in get_cotangent:
        copy.wait()
    for image in range(images):
        rows_ref[images + image] = mul(
            combine_ref[image].T.astype(BF16), cotangent_ref[image]
        ).astype(BF16)
    order = one_hot_rows(kinds, True)
    span = TILE // kinds
    for block in range(slots // span):
        grouped = rows_ref[:, block * span : (block + 1) * span, :].reshape(TILE, width)
        send_ref[block * TILE : (block + 1) * TILE] = mul(order, grouped).astype(BF16)


def pre(tokens, cotangent, params):
    images, patches, width = tokens.shape
    slots = params.shape[1]
    kinds = 2 * images
    out_shape = [
        jax.ShapeDtypeStruct((slots * kinds, width), BF16),
        jax.ShapeDtypeStruct((images, patches, slots), F32),
        jax.ShapeDtypeStruct((images, patches, slots), F32),
    ]
    arguments = (tokens, cotangent, params)
    return pl.pallas_call(
        pre_kernel,
        in_specs=[pl.BlockSpec(memory_space=pltpu.HBM) for _ in arguments],
        out_specs=whole(*out_shape),
        out_shape=out_shape,
        scratch_shapes=[
            pltpu.VMEM(tokens.shape, BF16),
            pltpu.VMEM(cotangent.shape, BF16),
            pltpu.VMEM(params.shape, BF16),
            pltpu.VMEM((kinds, slots, width), BF16),
            pltpu.SemaphoreType.DMA((images,)),
            pltpu.SemaphoreType.DMA((images,)),
            pltpu.SemaphoreType.DMA(()),
        ],
        compiler_params=pltpu.CompilerParams(vmem_limit_bytes=36 << 20),
        name="pre",
    )(*(in_space(array, pltpu.HBM) for array in arguments))


def expert_kernel(
    kinds,
    arrived_ref,
    expand_ref,
    shrink_ref,
    send_ref,
    kept_rows_ref,
    kept_grads_ref,
    activated_ref,
    hidden_grad_ref,
    rows_ref,
    grads_ref,
    rows_sem,
    grads_sem,
):
    half = TILE // 2
    blocks = arrived_ref.shape[0] // TILE
    width, hidden_width = expand_ref.shape
    step = 1024

    order = one_hot_rows(kinds, False)
    for block in range(blocks):
        grouped = mul(order, arrived_ref[block * TILE : (block + 1) * TILE]).astype(BF16)
        rows_ref[block * half : (block + 1) * half] = grouped[:half]
        grads_ref[block * half : (block + 1) * half] = grouped[half:]
    keep_rows = pltpu.make_async_copy(rows_ref, kept_rows_ref, rows_sem)
    keep_grads = pltpu.make_async_copy(grads_ref, kept_grads_ref, grads_sem)
    keep_rows.start()
    keep_grads.start()

    def inner(index, carry):
        span = pl.ds(pl.multiple_of(index * step, step), step)
        hidden = mul(rows_ref[...], expand_ref[:, span])
        grad_activated = mul(grads_ref[...], shrink_ref[span, :], NT)
        cumulative = 0.5 * (1.0 + lax.erf(hidden * 0.7071067811865476))
        bell = jnp.exp(-0.5 * hidden * hidden) * 0.3989422804014327
        activated_ref[:, span] = (hidden * cumulative).astype(BF16)
        hidden_grad_ref[:, span] = (grad_activated * (cumulative + hidden * bell)).astype(BF16)
        return carry

    lax.fori_loop(0, hidden_width // step, inner, 0, unroll=True)
    back = one_hot_rows(kinds, True)

    def outer(index, carry):
        span = pl.ds(pl.multiple_of(index * step, step), step)
        result = mul(activated_ref[...], shrink_ref[:, span]).astype(BF16)
        input_grad = mul(hidden_grad_ref[...], expand_ref[span, :], NT).astype(BF16)
        for block in range(blocks):
            part = slice(block * half, (block + 1) * half)
            grouped = jnp.concatenate([result[part], input_grad[part]], axis=0)
            send_ref[block * TILE : (block + 1) * TILE, span] = mul(back, grouped).astype(BF16)
        return carry

    lax.fori_loop(0, width // step, outer, 0, unroll=True)
    keep_rows.wait()
    keep_grads.wait()


def expert(arrived, expand, shrink, kinds):
    total, width = arrived.shape
    hidden_width = expand.shape[1]
    rows = total // 2
    out_shape = [
        jax.ShapeDtypeStruct((total, width), BF16),
        pltpu.HBM((rows, width), BF16),
        pltpu.HBM((rows, width), BF16),
        jax.ShapeDtypeStruct((rows, hidden_width), BF16),
        jax.ShapeDtypeStruct((rows, hidden_width), BF16),
    ]
    vmem = pl.BlockSpec(memory_space=pltpu.VMEM)
    hbm = pl.BlockSpec(memory_space=pltpu.HBM)
    return pl.pallas_call(
        lambda *refs: expert_kernel(kinds, *refs),
        in_specs=whole(arrived, expand, shrink),
        out_specs=[vmem, hbm, hbm, vmem, vmem],
        out_shape=out_shape,
        scratch_shapes=[
            pltpu.VMEM((rows, width), BF16),
            pltpu.VMEM((rows, width), BF16),
            pltpu.SemaphoreType.DMA(()),
            pltpu.SemaphoreType.DMA(()),
        ],
        compiler_params=pltpu.CompilerParams(vmem_limit_bytes=32 << 20),
        name="expert",
    )(arrived, in_space(expand, pltpu.VMEM), in_space(shrink, pltpu.VMEM))


def post_kernel(
    images,
    arrived_ref,
    tokens_ref,
    cotangent_ref,
    dispatch_ref,
    combine_ref,
    kept_ref,
    grad_logits_ref,
    phi_ref,
    rows_ref,
    kept_sem,
):
    kinds, slots, width = rows_ref.shape
    span = TILE // kinds
    order = one_hot_rows(kinds, False)
    for block in range(slots // span):
        grouped = mul(order, arrived_ref[block * TILE : (block + 1) * TILE]).astype(BF16)
        rows_ref[:, block * span : (block + 1) * span, :] = grouped.reshape(kinds, span, width)
    keep = pltpu.make_async_copy(rows_ref, kept_ref, kept_sem)
    keep.start()
    patches = tokens_ref.shape[1]
    parts = []
    for image in range(images):
        down = dispatch_ref[image]
        across = combine_ref[image]
        grad_combine = mul(cotangent_ref[image], rows_ref[image], NT)
        grad_dispatch = mul(tokens_ref[image], rows_ref[images + image], NT)
        grad_logits = down * (
            grad_dispatch - jnp.sum(down * grad_dispatch, axis=0, keepdims=True)
        ) + across * (grad_combine - jnp.sum(across * grad_combine, axis=1, keepdims=True))
        grad_logits_ref[image] = grad_logits.astype(BF16)
        parts.append(grad_logits.T.astype(BF16))
    all_tokens = tokens_ref[...].reshape(images * patches, width)
    total = mul(jnp.concatenate(parts, axis=1), all_tokens)
    phi_ref[...] = total.astype(BF16).T
    keep.wait()


def post(arrived, tokens, cotangent, dispatch, combine):
    images, patches, width = tokens.shape
    slots = dispatch.shape[2]
    out_shape = [
        pltpu.HBM((2 * images, slots, width), BF16),
        jax.ShapeDtypeStruct((images, patches, slots), BF16),
        jax.ShapeDtypeStruct((width, slots), BF16),
    ]
    return pl.pallas_call(
        lambda *refs: post_kernel(images, *refs),
        in_specs=whole(arrived, tokens, cotangent, dispatch, combine),
        out_specs=[pl.BlockSpec(memory_space=pltpu.HBM)] + whole(*out_shape[1:]),
        out_shape=out_shape,
        scratch_shapes=[pltpu.VMEM(out_shape[0].shape, BF16), pltpu.SemaphoreType.DMA(())],
        compiler_params=pltpu.CompilerParams(vmem_limit_bytes=20 << 20),
        name="post",
    )(arrived, tokens, cotangent, dispatch, combine)


CUT = 512


def flow(hbm_ref, vmem_ref, sems, pieces):
    return [
        (
            pltpu.make_async_copy(hbm_ref.at[piece], vmem_ref.at[piece], sems.at[index]),
            pltpu.make_async_copy(vmem_ref.at[piece], hbm_ref.at[piece], sems.at[index]),
        )
        for index, piece in enumerate(pieces)
    ]


def column_cuts(ref):
    return [(slice(None), pl.ds(start, CUT)) for start in range(0, ref.shape[1], CUT)]


def row_cuts(ref):
    return [(pl.ds(start, CUT), slice(None)) for start in range(0, ref.shape[0], CUT)]


def forward_finish_kernel(
    inputs_hbm,
    hidden_grad_hbm,
    slots_hbm,
    combine_ref,
    layer_hbm,
    expand_hbm,
    inputs_ref,
    hidden_grad_ref,
    slots_ref,
    layer_ref,
    expand_ref,
    inputs_sem,
    slots_sem,
    hidden_sems,
    expand_sems,
    layer_sems,
):
    images = combine_ref.shape[0]
    get_slots = pltpu.make_async_copy(slots_hbm.at[pl.ds(0, images)], slots_ref, slots_sem)
    get_inputs = pltpu.make_async_copy(inputs_hbm, inputs_ref, inputs_sem)
    hidden = flow(hidden_grad_hbm, hidden_grad_ref, hidden_sems, column_cuts(hidden_grad_ref))
    put_expand = flow(expand_hbm, expand_ref, expand_sems, column_cuts(expand_ref))
    put_layer = flow(layer_hbm, layer_ref, layer_sems, range(images))
    get_inputs.start()
    for get, _ in hidden:
        get.start()
    get_slots.start()
    get_inputs.wait()
    turned = inputs_ref[...].T
    for (get, _), (_, put), piece in zip(hidden, put_expand, column_cuts(expand_ref)):
        get.wait()
        expand_ref[piece] = mul(turned, hidden_grad_ref[piece]).astype(BF16)
        put.start()
    get_slots.wait()
    for image in range(images):
        layer_ref[image] = mul(combine_ref[image].astype(BF16), slots_ref[image]).astype(BF16)
        put_layer[image][1].start()
    for _, put in put_expand + put_layer:
        put.wait()


def backward_finish_kernel(
    grads_hbm,
    activated_hbm,
    slots_hbm,
    dispatch_ref,
    grad_logits_ref,
    params_ref,
    tokens_hbm,
    shrink_hbm,
    grads_ref,
    activated_ref,
    slots_ref,
    tokens_ref,
    shrink_ref,
    grads_sem,
    slots_sem,
    activated_sems,
    shrink_sems,
    tokens_sems,
):
    images = dispatch_ref.shape[0]
    get_slots = pltpu.make_async_copy(slots_hbm.at[pl.ds(images, images)], slots_ref, slots_sem)
    get_grads = pltpu.make_async_copy(grads_hbm, grads_ref, grads_sem)
    activated = flow(activated_hbm, activated_ref, activated_sems, column_cuts(activated_ref))
    put_shrink = flow(shrink_hbm, shrink_ref, shrink_sems, row_cuts(shrink_ref))
    put_tokens = flow(tokens_hbm, tokens_ref, tokens_sems, range(images))
    get_grads.start()
    for get, _ in activated:
        get.start()
    get_slots.start()
    back = params_ref[...].T
    get_grads.wait()
    pieces = zip(column_cuts(activated_ref), row_cuts(shrink_ref))
    for (get, _), (_, put), (source, target) in zip(activated, put_shrink, pieces):
        get.wait()
        shrink_ref[target] = mul(activated_ref[source].T, grads_ref[...]).astype(BF16)
        put.start()
    get_slots.wait()
    for image in range(images):
        factors = jnp.concatenate([dispatch_ref[image].astype(BF16), grad_logits_ref[image]], axis=1)
        sources = jnp.concatenate([slots_ref[image], back], axis=0)
        tokens_ref[image] = mul(factors, sources).astype(BF16)
        put_tokens[image][1].start()
    for _, put in put_shrink + put_tokens:
        put.wait()


def finish(kernel, name, held, near, outputs):
    images = near[0].shape[0]
    slots_shape = (images,) + held[2].shape[1:]
    return pl.pallas_call(
        kernel,
        in_specs=[pl.BlockSpec(memory_space=pltpu.HBM)] * len(held) + whole(*near),
        out_specs=[pl.BlockSpec(memory_space=pltpu.HBM)] * len(outputs),
        out_shape=[jax.ShapeDtypeStruct(shape, BF16) for shape in outputs],
        scratch_shapes=[
            pltpu.VMEM(held[0].shape, BF16),
            pltpu.VMEM(held[1].shape, BF16),
            pltpu.VMEM(slots_shape, BF16),
            *(pltpu.VMEM(shape, BF16) for shape in outputs),
            pltpu.SemaphoreType.DMA(()),
            pltpu.SemaphoreType.DMA(()),
            pltpu.SemaphoreType.DMA((held[1].shape[1] // CUT,)),
            pltpu.SemaphoreType.DMA((held[1].shape[1] // CUT,)),
            pltpu.SemaphoreType.DMA((images,)),
        ],
        compiler_params=pltpu.CompilerParams(vmem_limit_bytes=24 << 20),
        cost_estimate=pl.CostEstimate(flops=6 << 30, bytes_accessed=10 << 20, transcendentals=0),
        name=name,
    )(*(in_space(array, pltpu.HBM) for array in held), *near)


def sum_kernel(pieces_ref, copies_ref):
    own = jnp.sum(pieces_ref[...].astype(F32), axis=0, keepdims=True).astype(BF16)
    copies_ref[...] = jnp.broadcast_to(own, copies_ref.shape)


def widen_kernel(narrow_ref, wide_ref):
    wide_ref[...] = narrow_ref[...].astype(F32)


def add_pieces(pieces):
    return pl.pallas_call(
        sum_kernel,
        in_specs=whole(pieces),
        out_specs=whole(pieces)[0],
        out_shape=jax.ShapeDtypeStruct(pieces.shape, BF16),
        compiler_params=pltpu.CompilerParams(vmem_limit_bytes=4 << 20),
        name="sum",
    )(pieces)


def widen(narrow):
    return pl.pallas_call(
        widen_kernel,
        in_specs=whole(narrow),
        out_specs=whole(narrow)[0],
        out_shape=jax.ShapeDtypeStruct(narrow.shape, F32),
        compiler_params=pltpu.CompilerParams(vmem_limit_bytes=4 << 20),
        name="widen",
    )(narrow)


def body(tokens, slot_params, expand_weight, shrink_weight, cotangent):
    images, _, width = tokens.shape
    slots = slot_params.shape[1]
    kinds = 2 * images
    send, dispatch, combine = pre(tokens, cotangent, slot_params)
    arrived = exchange(send.reshape(slots, kinds, width)).reshape(slots * kinds, width)
    send_back, expert_rows, grad_rows, activated, grad_hidden = expert(
        arrived, expand_weight[0], shrink_weight[0], kinds
    )
    returned = exchange(send_back.reshape(slots, kinds, width)).reshape(slots * kinds, width)
    rows, grad_logits, phi_term = post(returned, tokens, cotangent, dispatch, combine)
    parts = lax.axis_size(AXES)
    pieces = exchange(phi_term.reshape(parts, width // parts, slots))
    layer_out, grad_expand = finish(
        forward_finish_kernel,
        "forward_finish",
        (expert_rows, grad_hidden, rows),
        (combine,),
        (tokens.shape, expand_weight.shape[1:]),
    )
    pieces, layer_out, grad_expand = lax.optimization_barrier((pieces, layer_out, grad_expand))
    copies = add_pieces(pieces)
    copies, activated = lax.optimization_barrier((copies, activated))
    grad_phi = widen(exchange(copies).reshape(width, slots))
    grad_tokens, grad_shrink = finish(
        backward_finish_kernel,
        "backward_finish",
        (grad_rows, activated, rows),
        (dispatch, grad_logits, slot_params),
        (tokens.shape, shrink_weight.shape[1:]),
    )
    return (layer_out, grad_tokens, grad_phi, grad_expand[None], grad_shrink[None])


def solution(mesh):
    placed = (
        P(("gx", "gy"), None, None),
        P(),
        P(("gx", "gy"), None, None),
        P(("gx", "gy"), None, None),
        P(("gx", "gy"), None, None),
    )
    return jax.shard_map(
        body,
        mesh=mesh,
        in_specs=placed,
        out_specs=(
            P(("gx", "gy"), None, None),
            P(("gx", "gy"), None, None),
            P(),
            P(("gx", "gy"), None, None),
            P(("gx", "gy"), None, None),
        ),
        check_vma=False,
    )
```

time: 133 us -> 131 us (0.985)
  blocking collectives: 91.8 us -> 76.3 us
  waiting for transfers between devices: 0.01 us -> 8.38 us
  starting transfers between devices: 4.56 us -> 10.6 us
    all_to_all x3 -> x2, blocking collectives: 91.8 us -> 76.3 us  [exchange(): return lax.all_to_all(chunks, AXES, split_axis=0, concat_axis=0, tiled=True)]
    all_to_all x1 -> x2, waiting for transfers between devices: 0.01 us -> 8.38 us  [exchange(): return lax.all_to_all(chunks, AXES, split_axis=0, concat_axis=0, tiled=True)]
    all_to_all x1 -> x2, starting transfers between devices: 4.56 us -> 10.6 us  [exchange(): return lax.all_to_all(chunks, AXES, split_axis=0, concat_axis=0, tiled=True)]
  transfers between devices with their start and end apart: 1 -> 2, of which waited for: 0 -> 2; matrix products, arithmetic and copies ran while one was open for 0% -> 0% of each run, Pallas kernels for 9% -> 10%
where the time goes in v4:
time: 131 us
  blocking collectives  76.3 us (58%)
  Pallas kernels  34.6 us (26%)
  starting transfers between devices  10.6 us (8%)
  waiting for transfers between devices  8.38 us (6%)
    all_to_all x2, blocking collectives, exchange(): return lax.all_to_all(chunks, AXES, split_axis=0, concat_axis=0, tiled=True)  76.3 us
    pallas_call x2, Pallas kernels, finish(): pl.pallas_call(kernel, in_specs=[pl.BlockSpec(memory_space=pltpu.HBM)] *...  13.1 us
    all_to_all x2, starting transfers between devices, exchange(): return lax.all_to_all(chunks, AXES, split_axis=0, concat_axis=0, tiled=True)  10.6 us
    pallas_call x1, Pallas kernels, expert(): pl.pallas_call(lambda *refs: expert_kernel(kinds, *refs), in_specs=whole(...  10.5 us
    all_to_all x2, waiting for transfers between devices, exchange(): return lax.all_to_all(chunks, AXES, split_axis=0, concat_axis=0, tiled=True)  8.38 us
    pallas_call x1, Pallas kernels, pre(): pl.pallas_call(pre_kernel, in_specs=[pl.BlockSpec(memory_space=pltpu.HBM)...  5.09 us
    pallas_call x1, Pallas kernels, post(): pl.pallas_call(lambda *refs: post_kernel(images, *refs), in_specs=whole(a...  4.2 us
  transfers between devices with their start and end apart: 2, of which 2 were waited for; matrix products, arithmetic and copies ran while one was open for 0% of the time, Pallas kernels for 10%

profile of v4, /device:TPU:1, one launch (start us, length us, event | category | flops | bytes accessed | tf_op | source)
XLA Modules:
  0.0 130.7 jit_solution(3489410149597078661)
XLA Ops:
  0.6 0.0 copy-start.3
  0.6 5.1 %pre.1 = (bf16[1024,1024]{1,0:T(8,128)(2,1)S(1)}, f32[4,256,128]{2,1,0:T(8,128)S(1)}, f32[4,256,128]{2,1,0:T(8,128)S(1)}) custom-call(bf16[4,256,1024]{2,1,0:T(8,128)(2,1)} %refs_1_.1, bf16[4,256,1024]{2,1,0:T(8,128)(2,1)} %refs_2_.1, bf16[1024,128]{1,0:T(8,128)(2,1)} %params_ref.1), custom_call_target="tpu_custom_call" | custom-call | tf_op jit(solution)/shard_map/pre/pallas_call | solution.py:113
  5.7 0.0 copy-start.2
  5.7 41.4 %all_to_all.20 = bf16[128,8,1024]{2,1,0:T(8,128)(2,1)S(1)} all-to-all(bf16[128,8,1024]{2,1,0:T(8,128)(2,1)S(1)} %bitcast.15), channel_id=1, replica_groups=mesh['gx'=32,'gy'=4] {'gx','gy'}, dimensions={0} | all-to-all | bytes 4194304 | tf_op jit(solution)/shard_map/all_to_all | solution.py:25
  47.2 0.0 copy-done.3
  47.2 0.0 copy-done.2
  47.2 10.5 %expert.1 = (bf16[1024,1024]{1,0:T(8,128)(2,1)S(1)}, bf16[512,1024]{1,0:T(8,128)(2,1)}, bf16[512,1024]{1,0:T(8,128)(2,1)}, bf16[512,2048]{1,0:T(8,128)(2,1)S(1)}, bf16[512,2048]{1,0:T(8,128)(2,1)S(1)}) custom-call(bf16[1024,1024]{1,0:T(8,128)(2,1)S(1)} %bitcast.10, bf16[1024,2048]{1,0:T(8,128)(2,1)S(1)} %bitcast.12, bf16[2048,1024]{1,0:T(8,128)(2,1)S(1)} %bitcast.13), custom_call_target="tpu_custom_call" | custom-call | tf_op jit(solution)/shard_map/expert/pallas_call | solution.py:203
  57.7 0.0 copy-start.5
  57.7 0.0 copy-start.6
  57.7 0.0 copy-start
  57.7 0.0 copy-start.1
  57.8 34.8 %all_to_all.21 = bf16[128,8,1024]{2,1,0:T(8,128)(2,1)S(1)} all-to-all(bf16[128,8,1024]{2,1,0:T(8,128)(2,1)S(1)} %bitcast.14), channel_id=1, replica_groups=mesh['gx'=32,'gy'=4] {'gx','gy'}, dimensions={0} | all-to-all | bytes 4194304 | tf_op jit(solution)/shard_map/all_to_all | solution.py:25
  92.6 0.0 copy-done.5
  92.6 0.0 copy-done.6
  92.6 0.0 copy-done
  92.6 0.0 copy-done.1
  92.6 4.2 %post.1 = (bf16[8,128,1024]{2,1,0:T(8,128)(2,1)}, bf16[4,256,128]{2,1,0:T(8,128)(2,1)S(1)}, bf16[1024,128]{1,0:T(8,128)(2,1)}) custom-call(bf16[1024,1024]{1,0:T(8,128)(2,1)S(1)} %bitcast.11, bf16[4,256,1024]{2,1,0:T(8,128)(2,1)S(1)} %copy-done, bf16[4,256,1024]{2,1,0:T(8,128)(2,1)S(1)} %copy-done.1, ...), custom_call_target="tpu_custom_call" | custom-call | tf_op jit(solution)/shard_map/post/pallas_call | solution.py:266
  96.8 4.9 %all-to-all-start.2 = ((bf16[128,8,128]{2,1,0:T(8,128)(2,1)}), bf16[128,8,128]{2,1,0:T(8,128)(2,1)S(1)}, u32[]{:S(2)}, u32[]{:S(2)}) async-start(bf16[128,8,128]{2,1,0:T(8,128)(2,1)} %bitcast.6), calls=%async_computation.2 | async-start | bytes 524288 | tf_op jit(solution)/shard_map/all_to_all | solution.py:25
  101.8 0.0 copy-start.4
  101.8 6.7 %forward_finish.1 = (bf16[4,256,1024]{2,1,0:T(8,128)(2,1)}, bf16[1024,2048]{1,0:T(8,128)(2,1)}) custom-call(bf16[512,1024]{1,0:T(8,128)(2,1)} %get-tuple-element.30.inputs_hbm, bf16[512,2048]{1,0:T(8,128)(2,1)} %copy-done.6, bf16[8,128,1024]{2,1,0:T(8,128)(2,1)} %get-tuple-element.32.slots_hbm, f32[4,256,128]{2,1,0:T(8,128)S(1)} %get-tuple-element.28.refs_4_.combine_ref), custom_call_target="tpu_custom_call" | custom-call | flops 6442450944 | bytes 10485760 | tf_op jit(solution)/shard_map/forward_finish/pallas_call | solution.py:390
  108.5 4.1 %all-to-all-done.2.pieces_ref = bf16[128,8,128]{2,1,0:T(8,128)(2,1)S(1)} async-done(((bf16[128,8,128]{2,1,0:T(8,128)(2,1)}), bf16[128,8,128]{2,1,0:T(8,128)(2,1)S(1)}, u32[]{:S(2)}, u32[]{:S(2)}) %all-to-all-start.2) | async-done | bytes 262176 | tf_op jit(solution)/shard_map/all_to_all | solution.py:25
  112.5 0.9 sum.1
  113.4 5.7 %all-to-all-start.3 = ((bf16[128,8,128]{2,1,0:T(8,128)(2,1)}), bf16[128,8,128]{2,1,0:T(8,128)(2,1)S(1)}, u32[]{:S(2)}, u32[]{:S(2)}) async-start(bf16[128,8,128]{2,1,0:T(8,128)(2,1)} %sum.1), calls=%async_computation.3 | async-start | bytes 524288 | tf_op jit(solution)/shard_map/all_to_all | solution.py:25
  119.1 0.0 copy-done.4
  119.1 6.4 %backward_finish.1 = (bf16[4,256,1024]{2,1,0:T(8,128)(2,1)}, bf16[2048,1024]{1,0:T(8,128)(2,1)}) custom-call(bf16[512,1024]{1,0:T(8,128)(2,1)} %get-tuple-element.36.grads_hbm, bf16[512,2048]{1,0:T(8,128)(2,1)} %copy-done.5, bf16[8,128,1024]{2,1,0:T(8,128)(2,1)} %get-tuple-element.32.slots_hbm, f32[4,256,128]{2,1,0:T(8,128)S(1)} %get-tuple-element.27.refs_3_.dispatch_ref, ...), custom_call_target="tpu_custom_call" | custom-call | flops 6442450944 | bytes 10485760 | tf_op jit(solution)/shard_map/backward_finish/pallas_call | solution.py:390
  125.5 4.3 %all-to-all-done.3 = bf16[128,8,128]{2,1,0:T(8,128)(2,1)S(1)} async-done(((bf16[128,8,128]{2,1,0:T(8,128)(2,1)}), bf16[128,8,128]{2,1,0:T(8,128)(2,1)S(1)}, u32[]{:S(2)}, u32[]{:S(2)}) %all-to-all-start.3) | async-done | bytes 262176 | tf_op jit(solution)/shard_map/all_to_all | solution.py:25
  129.8 0.8 widen.1
Async XLA Ops:
  0.6 46.5 %copy-start.3 = (bf16[1,2048,1024]{2,1,0:T(8,128)(2,1)S(1)}, bf16[1,2048,1024]{2,1,0:T(8,128)(2,1)}, u32[]{:S(2)}) copy-start(bf16[1,2048,1024]{2,1,0:T(8,128)(2,1)} %param.8) | copy-start | bytes 12582916
  5.7 41.4 %copy-start.2 = (bf16[1,1024,2048]{2,1,0:T(8,128)(2,1)S(1)}, bf16[1,1024,2048]{2,1,0:T(8,128)(2,1)}, u32[]{:S(2)}) copy-start(bf16[1,1024,2048]{2,1,0:T(8,128)(2,1)} %param.7) | copy-start | bytes 12582916
  57.7 34.9 %copy-start.5 = (bf16[512,2048]{1,0:T(8,128)(2,1)}, bf16[512,2048]{1,0:T(8,128)(2,1)S(1)}, u32[]{:S(2)}) copy-start(bf16[512,2048]{1,0:T(8,128)(2,1)S(1)} %get-tuple-element.39.activated_hbm) | copy-start | bytes 6291460
  57.7 34.9 %copy-start.6 = (bf16[512,2048]{1,0:T(8,128)(2,1)}, bf16[512,2048]{1,0:T(8,128)(2,1)S(1)}, u32[]{:S(2)}) copy-start(bf16[512,2048]{1,0:T(8,128)(2,1)S(1)} %get-tuple-element.31.hidden_grad_hbm) | copy-start | bytes 6291460
  57.7 34.9 %copy-start = (bf16[4,256,1024]{2,1,0:T(8,128)(2,1)S(1)}, bf16[4,256,1024]{2,1,0:T(8,128)(2,1)}, u32[]{:S(2)}) copy-start(bf16[4,256,1024]{2,1,0:T(8,128)(2,1)} %refs_1_.1) | copy-start | bytes 6291460
  57.7 34.9 %copy-start.1 = (bf16[4,256,1024]{2,1,0:T(8,128)(2,1)S(1)}, bf16[4,256,1024]{2,1,0:T(8,128)(2,1)}, u32[]{:S(2)}) copy-start(bf16[4,256,1024]{2,1,0:T(8,128)(2,1)} %refs_2_.1) | copy-start | bytes 6291460
  96.8 15.7 %all-to-all-start.2 = ((bf16[128,8,128]{2,1,0:T(8,128)(2,1)}), bf16[128,8,128]{2,1,0:T(8,128)(2,1)S(1)}, u32[]{:S(2)}, u32[]{:S(2)}) async-start(bf16[128,8,128]{2,1,0:T(8,128)(2,1)} %bitcast.6), calls=%async_computation.2 | async-start | bytes 524288 | tf_op jit(solution)/shard_map/all_to_all | solution.py:25
  101.8 17.3 %copy-start.4 = (bf16[1024,128]{1,0:T(8,128)(2,1)S(1)}, bf16[1024,128]{1,0:T(8,128)(2,1)}, u32[]{:S(2)}) copy-start(bf16[1024,128]{1,0:T(8,128)(2,1)} %params_ref.1) | copy-start | bytes 786436
  113.4 16.4 %all-to-all-start.3 = ((bf16[128,8,128]{2,1,0:T(8,128)(2,1)}), bf16[128,8,128]{2,1,0:T(8,128)(2,1)S(1)}, u32[]{:S(2)}, u32[]{:S(2)}) async-start(bf16[128,8,128]{2,1,0:T(8,128)(2,1)} %sum.1), calls=%async_computation.3 | async-start | bytes 524288 | tf_op jit(solution)/shard_map/all_to_all | solution.py:25

commit v5 on v4

--- a/solution.py
+++ b/solution.py
@@ -78,21 +78,19 @@
     patches = tokens_ref.shape[1]
     all_logits = mul(tokens_ref[...].reshape(images * patches, width), params_ref[...])
     for image in range(images):
-        one_image = tokens_ref[image]
         logits = all_logits[image * patches : (image + 1) * patches]
         down = jnp.exp(logits - jnp.max(logits, axis=0, keepdims=True))
-        down = down / jnp.sum(down, axis=0, keepdims=True)
-        across = jnp.exp(logits - jnp.max(logits, axis=1, keepdims=True))
-        across = across / jnp.sum(across, axis=1, keepdims=True)
+        down = down * (1.0 / jnp.sum(down, axis=0, keepdims=True))
         dispatch_ref[image] = down
-        combine_ref[image] = across
-        rows_ref[image] = mul(down.T.astype(BF16), one_image).astype(BF16)
+        rows_ref[image] = mul(down.astype(BF16).T, tokens_ref[image]).astype(BF16)
+    all_across = jnp.exp(all_logits - jnp.max(all_logits, axis=1, keepdims=True))
+    all_across = all_across * (1.0 / jnp.sum(all_across, axis=1, keepdims=True))
+    for image in range(images):
+        combine_ref[image] = all_across[image * patches : (image + 1) * patches]
     for copy in get_cotangent:
         copy.wait()
     for image in range(images):
-        rows_ref[images + image] = mul(
-            combine_ref[image].T.astype(BF16), cotangent_ref[image]
-        ).astype(BF16)
+        rows_ref[images + image] = mul(combine_ref[image].astype(BF16).T, cotangent_ref[image]).astype(BF16)
     order = one_hot_rows(kinds, True)
     span = TILE // kinds
     for block in range(slots // span):
@@ -149,11 +147,17 @@
     width, hidden_width = expand_ref.shape
     step = 1024
 
-    order = one_hot_rows(kinds, False)
+    group = kinds // 2
+    low = lax.broadcasted_iota(jnp.int32, (1, kinds, 1), 1) < group
     for block in range(blocks):
-        grouped = mul(order, arrived_ref[block * TILE : (block + 1) * TILE]).astype(BF16)
-        rows_ref[block * half : (block + 1) * half] = grouped[:half]
-        grads_ref[block * half : (block + 1) * half] = grouped[half:]
+        mixed = arrived_ref[block * TILE : (block + 1) * TILE].astype(F32)
+        pairs = mixed.reshape(TILE // (2 * kinds), 2, kinds, width)
+        left, right = pairs[:, 0], pairs[:, 1]
+        part = slice(block * half, (block + 1) * half)
+        first = jnp.where(low, left, pltpu.roll(right, group, 1))
+        second = jnp.where(low, pltpu.roll(left, group, 1), right)
+        rows_ref[part] = first.reshape(half, width).astype(BF16)
+        grads_ref[part] = second.reshape(half, width).astype(BF16)
     keep_rows = pltpu.make_async_copy(rows_ref, kept_rows_ref, rows_sem)
     keep_grads = pltpu.make_async_copy(grads_ref, kept_grads_ref, grads_sem)
     keep_rows.start()
@@ -170,16 +174,16 @@
         return carry
 
     lax.fori_loop(0, hidden_width // step, inner, 0, unroll=True)
-    back = one_hot_rows(kinds, True)
-
     def outer(index, carry):
         span = pl.ds(pl.multiple_of(index * step, step), step)
-        result = mul(activated_ref[...], shrink_ref[:, span]).astype(BF16)
-        input_grad = mul(hidden_grad_ref[...], expand_ref[span, :], NT).astype(BF16)
-        for block in range(blocks):
-            part = slice(block * half, (block + 1) * half)
-            grouped = jnp.concatenate([result[part], input_grad[part]], axis=0)
-            send_ref[block * TILE : (block + 1) * TILE, span] = mul(back, grouped).astype(BF16)
+        result = mul(activated_ref[...], shrink_ref[:, span])
+        input_grad = mul(hidden_grad_ref[...], expand_ref[span, :], NT)
+        first = result.reshape(-1, kinds, step)
+        second = input_grad.reshape(-1, kinds, step)
+        left = jnp.where(low, first, pltpu.roll(second, group, 1))
+        right = jnp.where(low, pltpu.roll(first, group, 1), second)
+        mixed = jnp.stack([left, right], axis=1)
+        send_ref[:, span] = mixed.reshape(-1, step).astype(BF16)
         return carry
 
     lax.fori_loop(0, width // step, outer, 0, unroll=True)
@@ -248,7 +252,7 @@
             grad_dispatch - jnp.sum(down * grad_dispatch, axis=0, keepdims=True)
         ) + across * (grad_combine - jnp.sum(across * grad_combine, axis=1, keepdims=True))
         grad_logits_ref[image] = grad_logits.astype(BF16)
-        parts.append(grad_logits.T.astype(BF16))
+        parts.append(grad_logits.astype(BF16).T)
     all_tokens = tokens_ref[...].reshape(images * patches, width)
     total = mul(jnp.concatenate(parts, axis=1), all_tokens)
     phi_ref[...] = total.astype(BF16).T

time: 131 us -> 130 us (level)
  no operation moved by 1% of the time
where the time goes in v5:
time: 130 us; the launch traced here: 129 us
  blocking collectives  76.3 us (59%)
  Pallas kernels  33.3 us (26%)
  starting transfers between devices  10.6 us (8%)
  waiting for transfers between devices  8.38 us (6%)
    all_to_all x2, blocking collectives, exchange(): return lax.all_to_all(chunks, AXES, split_axis=0, concat_axis=0, tiled=True)  76.3 us
    pallas_call x2, Pallas kernels, finish(): pl.pallas_call(kernel, in_specs=[pl.BlockSpec(memory_space=pltpu.HBM)] *...  13.1 us
    all_to_all x2, starting transfers between devices, exchange(): return lax.all_to_all(chunks, AXES, split_axis=0, concat_axis=0, tiled=True)  10.6 us
    pallas_call x1, Pallas kernels, expert(): pl.pallas_call(lambda *refs: expert_kernel(kinds, *refs), in_specs=whole(...  9.46 us
    all_to_all x2, waiting for transfers between devices, exchange(): return lax.all_to_all(chunks, AXES, split_axis=0, concat_axis=0, tiled=True)  8.38 us
    pallas_call x1, Pallas kernels, pre(): pl.pallas_call(pre_kernel, in_specs=[pl.BlockSpec(memory_space=pltpu.HBM)...  4.93 us
    pallas_call x1, Pallas kernels, post(): pl.pallas_call(lambda *refs: post_kernel(images, *refs), in_specs=whole(a...  4.16 us
  transfers between devices with their start and end apart: 2, of which 2 were waited for; matrix products, arithmetic and copies ran while one was open for 0% of the time, Pallas kernels for 10%

profile of v5, /device:TPU:1, one launch (start us, length us, event | category | flops | bytes accessed | tf_op | source)
XLA Modules:
  0.0 129.4 jit_solution(4758494192099201683)
XLA Ops:
  0.6 0.0 copy-start.3
  0.6 4.9 %pre.1 = (bf16[1024,1024]{1,0:T(8,128)(2,1)S(1)}, f32[4,256,128]{2,1,0:T(8,128)S(1)}, f32[4,256,128]{2,1,0:T(8,128)S(1)}) custom-call(bf16[4,256,1024]{2,1,0:T(8,128)(2,1)} %refs_1_.1, bf16[4,256,1024]{2,1,0:T(8,128)(2,1)} %refs_2_.1, bf16[1024,128]{1,0:T(8,128)(2,1)} %params_ref.1), custom_call_target="tpu_custom_call" | custom-call | tf_op jit(solution)/shard_map/pre/pallas_call | solution.py:111
  5.6 0.0 copy-start.2
  5.6 41.4 %all_to_all.20 = bf16[128,8,1024]{2,1,0:T(8,128)(2,1)S(1)} all-to-all(bf16[128,8,1024]{2,1,0:T(8,128)(2,1)S(1)} %bitcast.15), channel_id=1, replica_groups=mesh['gx'=32,'gy'=4] {'gx','gy'}, dimensions={0} | all-to-all | bytes 4194304 | tf_op jit(solution)/shard_map/all_to_all | solution.py:25
  47.0 0.0 copy-done.3
  47.0 0.0 copy-done.2
  47.0 9.5 %expert.1 = (bf16[1024,1024]{1,0:T(8,128)(2,1)S(1)}, bf16[512,1024]{1,0:T(8,128)(2,1)}, bf16[512,1024]{1,0:T(8,128)(2,1)}, bf16[512,2048]{1,0:T(8,128)(2,1)S(1)}, bf16[512,2048]{1,0:T(8,128)(2,1)S(1)}) custom-call(bf16[1024,1024]{1,0:T(8,128)(2,1)S(1)} %bitcast.10, bf16[1024,2048]{1,0:T(8,128)(2,1)S(1)} %bitcast.12, bf16[2048,1024]{1,0:T(8,128)(2,1)S(1)} %bitcast.13), custom_call_target="tpu_custom_call" | custom-call | tf_op jit(solution)/shard_map/expert/pallas_call | solution.py:207
  56.5 0.0 copy-start.5
  56.5 0.0 copy-start.6
  56.5 0.0 copy-start
  56.5 0.0 copy-start.1
  56.5 34.9 %all_to_all.21 = bf16[128,8,1024]{2,1,0:T(8,128)(2,1)S(1)} all-to-all(bf16[128,8,1024]{2,1,0:T(8,128)(2,1)S(1)} %bitcast.14), channel_id=1, replica_groups=mesh['gx'=32,'gy'=4] {'gx','gy'}, dimensions={0} | all-to-all | bytes 4194304 | tf_op jit(solution)/shard_map/all_to_all | solution.py:25
  91.4 0.0 copy-done.5
  91.4 0.0 copy-done.6
  91.4 0.0 copy-done
  91.4 0.0 copy-done.1
  91.4 4.2 %post.1 = (bf16[8,128,1024]{2,1,0:T(8,128)(2,1)}, bf16[4,256,128]{2,1,0:T(8,128)(2,1)S(1)}, bf16[1024,128]{1,0:T(8,128)(2,1)}) custom-call(bf16[1024,1024]{1,0:T(8,128)(2,1)S(1)} %bitcast.11, bf16[4,256,1024]{2,1,0:T(8,128)(2,1)S(1)} %copy-done, bf16[4,256,1024]{2,1,0:T(8,128)(2,1)S(1)} %copy-done.1, ...), custom_call_target="tpu_custom_call" | custom-call | tf_op jit(solution)/shard_map/post/pallas_call | solution.py:270
  95.6 4.9 %all-to-all-start.2 = ((bf16[128,8,128]{2,1,0:T(8,128)(2,1)}), bf16[128,8,128]{2,1,0:T(8,128)(2,1)S(1)}, u32[]{:S(2)}, u32[]{:S(2)}) async-start(bf16[128,8,128]{2,1,0:T(8,128)(2,1)} %bitcast.6), calls=%async_computation.2 | async-start | bytes 524288 | tf_op jit(solution)/shard_map/all_to_all | solution.py:25
  100.5 0.0 copy-start.4
  100.5 6.7 %forward_finish.1 = (bf16[4,256,1024]{2,1,0:T(8,128)(2,1)}, bf16[1024,2048]{1,0:T(8,128)(2,1)}) custom-call(bf16[512,1024]{1,0:T(8,128)(2,1)} %get-tuple-element.30.inputs_hbm, bf16[512,2048]{1,0:T(8,128)(2,1)} %copy-done.6, bf16[8,128,1024]{2,1,0:T(8,128)(2,1)} %get-tuple-element.32.slots_hbm, f32[4,256,128]{2,1,0:T(8,128)S(1)} %get-tuple-element.28.refs_4_.combine_ref), custom_call_target="tpu_custom_call" | custom-call | flops 6442450944 | bytes 10485760 | tf_op jit(solution)/shard_map/forward_finish/pallas_call | solution.py:394
  107.2 4.1 %all-to-all-done.2.pieces_ref = bf16[128,8,128]{2,1,0:T(8,128)(2,1)S(1)} async-done(((bf16[128,8,128]{2,1,0:T(8,128)(2,1)}), bf16[128,8,128]{2,1,0:T(8,128)(2,1)S(1)}, u32[]{:S(2)}, u32[]{:S(2)}) %all-to-all-start.2) | async-done | bytes 262176 | tf_op jit(solution)/shard_map/all_to_all | solution.py:25
  111.3 0.9 sum.1
  112.1 5.7 %all-to-all-start.3 = ((bf16[128,8,128]{2,1,0:T(8,128)(2,1)}), bf16[128,8,128]{2,1,0:T(8,128)(2,1)S(1)}, u32[]{:S(2)}, u32[]{:S(2)}) async-start(bf16[128,8,128]{2,1,0:T(8,128)(2,1)} %sum.1), calls=%async_computation.3 | async-start | bytes 524288 | tf_op jit(solution)/shard_map/all_to_all | solution.py:25
  117.8 0.0 copy-done.4
  117.8 6.4 %backward_finish.1 = (bf16[4,256,1024]{2,1,0:T(8,128)(2,1)}, bf16[2048,1024]{1,0:T(8,128)(2,1)}) custom-call(bf16[512,1024]{1,0:T(8,128)(2,1)} %get-tuple-element.36.grads_hbm, bf16[512,2048]{1,0:T(8,128)(2,1)} %copy-done.5, bf16[8,128,1024]{2,1,0:T(8,128)(2,1)} %get-tuple-element.32.slots_hbm, f32[4,256,128]{2,1,0:T(8,128)S(1)} %get-tuple-element.27.refs_3_.dispatch_ref, ...), custom_call_target="tpu_custom_call" | custom-call | flops 6442450944 | bytes 10485760 | tf_op jit(solution)/shard_map/backward_finish/pallas_call | solution.py:394
  124.3 4.3 %all-to-all-done.3 = bf16[128,8,128]{2,1,0:T(8,128)(2,1)S(1)} async-done(((bf16[128,8,128]{2,1,0:T(8,128)(2,1)}), bf16[128,8,128]{2,1,0:T(8,128)(2,1)S(1)}, u32[]{:S(2)}, u32[]{:S(2)}) %all-to-all-start.3) | async-done | bytes 262176 | tf_op jit(solution)/shard_map/all_to_all | solution.py:25
  128.6 0.8 widen.1
Async XLA Ops:
  0.6 46.4 %copy-start.3 = (bf16[1,2048,1024]{2,1,0:T(8,128)(2,1)S(1)}, bf16[1,2048,1024]{2,1,0:T(8,128)(2,1)}, u32[]{:S(2)}) copy-start(bf16[1,2048,1024]{2,1,0:T(8,128)(2,1)} %param.8) | copy-start | bytes 12582916
  5.6 41.4 %copy-start.2 = (bf16[1,1024,2048]{2,1,0:T(8,128)(2,1)S(1)}, bf16[1,1024,2048]{2,1,0:T(8,128)(2,1)}, u32[]{:S(2)}) copy-start(bf16[1,1024,2048]{2,1,0:T(8,128)(2,1)} %param.7) | copy-start | bytes 12582916
  56.5 34.9 %copy-start.5 = (bf16[512,2048]{1,0:T(8,128)(2,1)}, bf16[512,2048]{1,0:T(8,128)(2,1)S(1)}, u32[]{:S(2)}) copy-start(bf16[512,2048]{1,0:T(8,128)(2,1)S(1)} %get-tuple-element.39.activated_hbm) | copy-start | bytes 6291460
  56.5 34.9 %copy-start.6 = (bf16[512,2048]{1,0:T(8,128)(2,1)}, bf16[512,2048]{1,0:T(8,128)(2,1)S(1)}, u32[]{:S(2)}) copy-start(bf16[512,2048]{1,0:T(8,128)(2,1)S(1)} %get-tuple-element.31.hidden_grad_hbm) | copy-start | bytes 6291460
  56.5 34.9 %copy-start = (bf16[4,256,1024]{2,1,0:T(8,128)(2,1)S(1)}, bf16[4,256,1024]{2,1,0:T(8,128)(2,1)}, u32[]{:S(2)}) copy-start(bf16[4,256,1024]{2,1,0:T(8,128)(2,1)} %refs_1_.1) | copy-start | bytes 6291460
  56.5 34.9 %copy-start.1 = (bf16[4,256,1024]{2,1,0:T(8,128)(2,1)S(1)}, bf16[4,256,1024]{2,1,0:T(8,128)(2,1)}, u32[]{:S(2)}) copy-start(bf16[4,256,1024]{2,1,0:T(8,128)(2,1)} %refs_2_.1) | copy-start | bytes 6291460
  95.6 15.7 %all-to-all-start.2 = ((bf16[128,8,128]{2,1,0:T(8,128)(2,1)}), bf16[128,8,128]{2,1,0:T(8,128)(2,1)S(1)}, u32[]{:S(2)}, u32[]{:S(2)}) async-start(bf16[128,8,128]{2,1,0:T(8,128)(2,1)} %bitcast.6), calls=%async_computation.2 | async-start | bytes 524288 | tf_op jit(solution)/shard_map/all_to_all | solution.py:25
  100.5 17.3 %copy-start.4 = (bf16[1024,128]{1,0:T(8,128)(2,1)S(1)}, bf16[1024,128]{1,0:T(8,128)(2,1)}, u32[]{:S(2)}) copy-start(bf16[1024,128]{1,0:T(8,128)(2,1)} %params_ref.1) | copy-start | bytes 786436
  112.1 16.5 %all-to-all-start.3 = ((bf16[128,8,128]{2,1,0:T(8,128)(2,1)}), bf16[128,8,128]{2,1,0:T(8,128)(2,1)S(1)}, u32[]{:S(2)}, u32[]{:S(2)}) async-start(bf16[128,8,128]{2,1,0:T(8,128)(2,1)} %sum.1), calls=%async_computation.3 | async-start | bytes 524288 | tf_op jit(solution)/shard_map/all_to_all | solution.py:25

commit v6 on v5

--- a/solution.py
+++ b/solution.py
@@ -3,9 +3,11 @@
 from jax import lax
 from jax.experimental import pallas as pl
 from jax.experimental.pallas import tpu as pltpu
-from jax.sharding import PartitionSpec as P
-
-AXES = ("gx", "gy")
+from jax.sharding import Mesh, PartitionSpec as P
+
+HELD = ("gx", "zh", "core")
+AXES = ("core", "gx", "zh")
+CORES = 2
 BF16 = jnp.bfloat16
 F32 = jnp.float32
 TILE = 256
@@ -38,6 +40,13 @@
 
 def whole(*shapes):
     return [pl.BlockSpec(memory_space=pltpu.VMEM) for _ in shapes]
+
+
+def place_order(slots):
+    slot = lax.broadcasted_iota(jnp.int32, (slots, slots), 0)
+    place = lax.broadcasted_iota(jnp.int32, (slots, slots), 1)
+    per_core = slots // CORES
+    return jnp.where(slot == (place % per_core) * CORES + place // per_core, 1.0, 0.0).astype(BF16)
 
 
 def pre_kernel(
@@ -71,12 +80,13 @@
     for copy in get_tokens:
         copy.start()
     get_params.wait()
+    params = mul(params_ref[...], place_order(slots)).astype(BF16)
     for copy in get_tokens:
         copy.wait()
     for copy in get_cotangent:
         copy.start()
     patches = tokens_ref.shape[1]
-    all_logits = mul(tokens_ref[...].reshape(images * patches, width), params_ref[...])
+    all_logits = mul(tokens_ref[...].reshape(images * patches, width), params)
     for image in range(images):
         logits = all_logits[image * patches : (image + 1) * patches]
         down = jnp.exp(logits - jnp.max(logits, axis=0, keepdims=True))
@@ -229,9 +239,11 @@
     combine_ref,
     kept_ref,
     grad_logits_ref,
+    phi_hbm,
+    rows_ref,
     phi_ref,
-    rows_ref,
     kept_sem,
+    phi_sems,
 ):
     kinds, slots, width = rows_ref.shape
     span = TILE // kinds
@@ -254,8 +266,17 @@
         grad_logits_ref[image] = grad_logits.astype(BF16)
         parts.append(grad_logits.astype(BF16).T)
     all_tokens = tokens_ref[...].reshape(images * patches, width)
-    total = mul(jnp.concatenate(parts, axis=1), all_tokens)
-    phi_ref[...] = total.astype(BF16).T
+    turned = mul(place_order(slots), jnp.concatenate(parts, axis=1)).astype(BF16)
+    cut = width // 2
+    puts = []
+    for index in range(2):
+        span = slice(index * cut, (index + 1) * cut)
+        phi_ref[span] = mul(turned, all_tokens[:, span]).astype(BF16).T
+        put = pltpu.make_async_copy(phi_ref.at[pl.ds(index * cut, cut)], phi_hbm.at[pl.ds(index * cut, cut)], phi_sems.at[index])
+        put.start()
+        puts.append(put)
+    for put in puts:
+        put.wait()
     keep.wait()
 
 
@@ -265,14 +286,23 @@
     out_shape = [
         pltpu.HBM((2 * images, slots, width), BF16),
         jax.ShapeDtypeStruct((images, patches, slots), BF16),
-        jax.ShapeDtypeStruct((width, slots), BF16),
+        pltpu.HBM((width, slots), BF16),
     ]
     return pl.pallas_call(
         lambda *refs: post_kernel(images, *refs),
         in_specs=whole(arrived, tokens, cotangent, dispatch, combine),
-        out_specs=[pl.BlockSpec(memory_space=pltpu.HBM)] + whole(*out_shape[1:]),
+        out_specs=[
+            pl.BlockSpec(memory_space=pltpu.HBM),
+            pl.BlockSpec(memory_space=pltpu.VMEM),
+            pl.BlockSpec(memory_space=pltpu.HBM),
+        ],
         out_shape=out_shape,
-        scratch_shapes=[pltpu.VMEM(out_shape[0].shape, BF16), pltpu.SemaphoreType.DMA(())],
+        scratch_shapes=[
+            pltpu.VMEM(out_shape[0].shape, BF16),
+            pltpu.VMEM((width, slots), BF16),
+            pltpu.SemaphoreType.DMA(()),
+            pltpu.SemaphoreType.DMA((2,)),
+        ],
         compiler_params=pltpu.CompilerParams(vmem_limit_bytes=20 << 20),
         name="post",
     )(arrived, tokens, cotangent, dispatch, combine)
@@ -371,7 +401,7 @@
     for get, _ in activated:
         get.start()
     get_slots.start()
-    back = params_ref[...].T
+    back = mul(params_ref[...], place_order(params_ref.shape[1])).astype(BF16).T
     get_grads.wait()
     pieces = zip(column_cuts(activated_ref), row_cuts(shrink_ref))
     for (get, _), (_, put), (source, target) in zip(activated, put_shrink, pieces):
@@ -479,23 +509,12 @@
 
 
 def solution(mesh):
-    placed = (
-        P(("gx", "gy"), None, None),
-        P(),
-        P(("gx", "gy"), None, None),
-        P(("gx", "gy"), None, None),
-        P(("gx", "gy"), None, None),
-    )
+    split = Mesh(mesh.devices.reshape(mesh.shape["gx"], -1, CORES), HELD)
+    shared = P(HELD, None, None)
     return jax.shard_map(
         body,
-        mesh=mesh,
-        in_specs=placed,
-        out_specs=(
-            P(("gx", "gy"), None, None),
-            P(("gx", "gy"), None, None),
-            P(),
-            P(("gx", "gy"), None, None),
-            P(("gx", "gy"), None, None),
-        ),
+        mesh=split,
+        in_specs=(shared, P(), shared, shared, shared),
+        out_specs=(shared, shared, P(), shared, shared),
         check_vma=False,
     )

time: 130 us -> 128 us (0.985)
  no operation moved by 1% of the time
where the time goes in v6:
time: 128 us
  blocking collectives  75.7 us (59%)
  Pallas kernels  32.2 us (25%)
  starting transfers between devices  10.3 us (8%)
  waiting for transfers between devices  9.23 us (7%)
    all_to_all x2, blocking collectives, exchange(): return lax.all_to_all(chunks, AXES, split_axis=0, concat_axis=0, tiled=True)  75.7 us
    pallas_call x2, Pallas kernels, finish(): pl.pallas_call(kernel, in_specs=[pl.BlockSpec(memory_space=pltpu.HBM)] *...  12.8 us
    all_to_all x2, starting transfers between devices, exchange(): return lax.all_to_all(chunks, AXES, split_axis=0, concat_axis=0, tiled=True)  10.3 us
    pallas_call x1, Pallas kernels, expert(): pl.pallas_call(lambda *refs: expert_kernel(kinds, *refs), in_specs=whole(...  9.47 us
    all_to_all x2, waiting for transfers between devices, exchange(): return lax.all_to_all(chunks, AXES, split_axis=0, concat_axis=0, tiled=True)  9.23 us
    pallas_call x1, Pallas kernels, pre(): pl.pallas_call(pre_kernel, in_specs=[pl.BlockSpec(memory_space=pltpu.HBM)...  5.02 us
    pallas_call x1, Pallas kernels, post(): pl.pallas_call(lambda *refs: post_kernel(images, *refs), in_specs=whole(a...  3.26 us
  transfers between devices with their start and end apart: 2, of which 2 were waited for; matrix products, arithmetic and copies ran while one was open for 0% of the time, Pallas kernels for 10%

profile of v6, /device:TPU:1, one launch (start us, length us, event | category | flops | bytes accessed | tf_op | source)
XLA Modules:
  0.0 128.3 jit_solution(5058333668096115841)
XLA Ops:
  0.6 0.0 copy-start.3
  0.6 5.0 %pre.1 = (bf16[1024,1024]{1,0:T(8,128)(2,1)S(1)}, f32[4,256,128]{2,1,0:T(8,128)S(1)}, f32[4,256,128]{2,1,0:T(8,128)S(1)}) custom-call(bf16[4,256,1024]{2,1,0:T(8,128)(2,1)} %refs_1_.1, bf16[4,256,1024]{2,1,0:T(8,128)(2,1)} %refs_2_.1, bf16[1024,128]{1,0:T(8,128)(2,1)} %params_ref.1), custom_call_target="tpu_custom_call" | custom-call | tf_op jit(solution)/shard_map/pre/pallas_call | solution.py:121
  5.7 0.0 copy-start.2
  5.7 41.2 %all_to_all.20 = bf16[128,8,1024]{2,1,0:T(8,128)(2,1)S(1)} all-to-all(bf16[128,8,1024]{2,1,0:T(8,128)(2,1)S(1)} %bitcast.15), channel_id=1, replica_groups=mesh['gx'=32,'zh'=2,'core'=2] {'core','gx','zh'}, dimensions={0} | all-to-all | bytes 4194304 | tf_op jit(solution)/shard_map/all_to_all | solution.py:27
  46.9 0.0 copy-done.3
  46.9 0.0 copy-done.2
  46.9 9.5 %expert.1 = (bf16[1024,1024]{1,0:T(8,128)(2,1)S(1)}, bf16[512,1024]{1,0:T(8,128)(2,1)}, bf16[512,1024]{1,0:T(8,128)(2,1)}, bf16[512,2048]{1,0:T(8,128)(2,1)S(1)}, bf16[512,2048]{1,0:T(8,128)(2,1)S(1)}) custom-call(bf16[1024,1024]{1,0:T(8,128)(2,1)S(1)} %bitcast.10, bf16[1024,2048]{1,0:T(8,128)(2,1)S(1)} %bitcast.12, bf16[2048,1024]{1,0:T(8,128)(2,1)S(1)} %bitcast.13), custom_call_target="tpu_custom_call" | custom-call | tf_op jit(solution)/shard_map/expert/pallas_call | solution.py:217
  56.3 0.0 copy-start.5
  56.4 0.0 copy-start.6
  56.4 0.0 copy-start
  56.4 0.0 copy-start.1
  56.4 34.6 %all_to_all.21 = bf16[128,8,1024]{2,1,0:T(8,128)(2,1)S(1)} all-to-all(bf16[128,8,1024]{2,1,0:T(8,128)(2,1)S(1)} %bitcast.14), channel_id=1, replica_groups=mesh['gx'=32,'zh'=2,'core'=2] {'core','gx','zh'}, dimensions={0} | all-to-all | bytes 4194304 | tf_op jit(solution)/shard_map/all_to_all | solution.py:27
  91.0 0.0 copy-done.5
  91.0 0.0 copy-done.6
  91.0 0.0 copy-done
  91.0 0.0 copy-done.1
  91.0 3.3 %post.1 = (bf16[8,128,1024]{2,1,0:T(8,128)(2,1)}, bf16[4,256,128]{2,1,0:T(8,128)(2,1)S(1)}, bf16[1024,128]{1,0:T(8,128)(2,1)}) custom-call(bf16[1024,1024]{1,0:T(8,128)(2,1)S(1)} %bitcast.11, bf16[4,256,1024]{2,1,0:T(8,128)(2,1)S(1)} %copy-done, bf16[4,256,1024]{2,1,0:T(8,128)(2,1)S(1)} %copy-done.1, ...), custom_call_target="tpu_custom_call" | custom-call | tf_op jit(solution)/shard_map/post/pallas_call | solution.py:291
  94.2 4.9 %all-to-all-start.2 = ((bf16[128,8,128]{2,1,0:T(8,128)(2,1)}), bf16[128,8,128]{2,1,0:T(8,128)(2,1)S(1)}, u32[]{:S(2)}, u32[]{:S(2)}) async-start(bf16[128,8,128]{2,1,0:T(8,128)(2,1)} %bitcast.17), calls=%async_computation.2 | async-start | bytes 524288 | tf_op jit(solution)/shard_map/all_to_all | solution.py:27
  99.1 0.0 copy-start.4
  99.2 6.6 %forward_finish.1 = (bf16[4,256,1024]{2,1,0:T(8,128)(2,1)}, bf16[1024,2048]{1,0:T(8,128)(2,1)}) custom-call(bf16[512,1024]{1,0:T(8,128)(2,1)} %get-tuple-element.30.inputs_hbm, bf16[512,2048]{1,0:T(8,128)(2,1)} %copy-done.6, bf16[8,128,1024]{2,1,0:T(8,128)(2,1)} %get-tuple-element.32.slots_hbm, f32[4,256,128]{2,1,0:T(8,128)S(1)} %get-tuple-element.28.refs_4_.combine_ref), custom_call_target="tpu_custom_call" | custom-call | flops 6442450944 | bytes 10485760 | tf_op jit(solution)/shard_map/forward_finish/pallas_call | solution.py:424
  105.8 4.4 %all-to-all-done.2.pieces_ref = bf16[128,8,128]{2,1,0:T(8,128)(2,1)S(1)} async-done(((bf16[128,8,128]{2,1,0:T(8,128)(2,1)}), bf16[128,8,128]{2,1,0:T(8,128)(2,1)S(1)}, u32[]{:S(2)}, u32[]{:S(2)}) %all-to-all-start.2) | async-done | bytes 262176 | tf_op jit(solution)/shard_map/all_to_all | solution.py:27
  110.2 0.9 sum.1
  111.0 5.4 %all-to-all-start.3 = ((bf16[128,8,128]{2,1,0:T(8,128)(2,1)}), bf16[128,8,128]{2,1,0:T(8,128)(2,1)S(1)}, u32[]{:S(2)}, u32[]{:S(2)}) async-start(bf16[128,8,128]{2,1,0:T(8,128)(2,1)} %sum.1), calls=%async_computation.3 | async-start | bytes 524288 | tf_op jit(solution)/shard_map/all_to_all | solution.py:27
  116.4 0.0 copy-done.4
  116.5 6.1 %backward_finish.1 = (bf16[4,256,1024]{2,1,0:T(8,128)(2,1)}, bf16[2048,1024]{1,0:T(8,128)(2,1)}) custom-call(bf16[512,1024]{1,0:T(8,128)(2,1)} %get-tuple-element.36.grads_hbm, bf16[512,2048]{1,0:T(8,128)(2,1)} %copy-done.5, bf16[8,128,1024]{2,1,0:T(8,128)(2,1)} %get-tuple-element.32.slots_hbm, f32[4,256,128]{2,1,0:T(8,128)S(1)} %get-tuple-element.27.refs_3_.dispatch_ref, ...), custom_call_target="tpu_custom_call" | custom-call | flops 6442450944 | bytes 10485760 | tf_op jit(solution)/shard_map/backward_finish/pallas_call | solution.py:424
  122.6 4.9 %all-to-all-done.3 = bf16[128,8,128]{2,1,0:T(8,128)(2,1)S(1)} async-done(((bf16[128,8,128]{2,1,0:T(8,128)(2,1)}), bf16[128,8,128]{2,1,0:T(8,128)(2,1)S(1)}, u32[]{:S(2)}, u32[]{:S(2)}) %all-to-all-start.3) | async-done | bytes 262176 | tf_op jit(solution)/shard_map/all_to_all | solution.py:27
  127.5 0.8 widen.1
Async XLA Ops:
  0.6 46.2 %copy-start.3 = (bf16[1,2048,1024]{2,1,0:T(8,128)(2,1)S(1)}, bf16[1,2048,1024]{2,1,0:T(8,128)(2,1)}, u32[]{:S(2)}) copy-start(bf16[1,2048,1024]{2,1,0:T(8,128)(2,1)} %param.8) | copy-start | bytes 12582916
  5.7 41.2 %copy-start.2 = (bf16[1,1024,2048]{2,1,0:T(8,128)(2,1)S(1)}, bf16[1,1024,2048]{2,1,0:T(8,128)(2,1)}, u32[]{:S(2)}) copy-start(bf16[1,1024,2048]{2,1,0:T(8,128)(2,1)} %param.7) | copy-start | bytes 12582916
  56.3 34.6 %copy-start.5 = (bf16[512,2048]{1,0:T(8,128)(2,1)}, bf16[512,2048]{1,0:T(8,128)(2,1)S(1)}, u32[]{:S(2)}) copy-start(bf16[512,2048]{1,0:T(8,128)(2,1)S(1)} %get-tuple-element.39.activated_hbm) | copy-start | bytes 6291460
  56.4 34.6 %copy-start.6 = (bf16[512,2048]{1,0:T(8,128)(2,1)}, bf16[512,2048]{1,0:T(8,128)(2,1)S(1)}, u32[]{:S(2)}) copy-start(bf16[512,2048]{1,0:T(8,128)(2,1)S(1)} %get-tuple-element.31.hidden_grad_hbm) | copy-start | bytes 6291460
  56.4 34.6 %copy-start = (bf16[4,256,1024]{2,1,0:T(8,128)(2,1)S(1)}, bf16[4,256,1024]{2,1,0:T(8,128)(2,1)}, u32[]{:S(2)}) copy-start(bf16[4,256,1024]{2,1,0:T(8,128)(2,1)} %refs_1_.1) | copy-start | bytes 6291460
  56.4 34.6 %copy-start.1 = (bf16[4,256,1024]{2,1,0:T(8,128)(2,1)S(1)}, bf16[4,256,1024]{2,1,0:T(8,128)(2,1)}, u32[]{:S(2)}) copy-start(bf16[4,256,1024]{2,1,0:T(8,128)(2,1)} %refs_2_.1) | copy-start | bytes 6291460
  94.2 15.9 %all-to-all-start.2 = ((bf16[128,8,128]{2,1,0:T(8,128)(2,1)}), bf16[128,8,128]{2,1,0:T(8,128)(2,1)S(1)}, u32[]{:S(2)}, u32[]{:S(2)}) async-start(bf16[128,8,128]{2,1,0:T(8,128)(2,1)} %bitcast.17), calls=%async_computation.2 | async-start | bytes 524288 | tf_op jit(solution)/shard_map/all_to_all | solution.py:27
  99.1 17.3 %copy-start.4 = (bf16[1024,128]{1,0:T(8,128)(2,1)S(1)}, bf16[1024,128]{1,0:T(8,128)(2,1)}, u32[]{:S(2)}) copy-start(bf16[1024,128]{1,0:T(8,128)(2,1)} %params_ref.1) | copy-start | bytes 786436
  111.0 16.4 %all-to-all-start.3 = ((bf16[128,8,128]{2,1,0:T(8,128)(2,1)}), bf16[128,8,128]{2,1,0:T(8,128)(2,1)S(1)}, u32[]{:S(2)}, u32[]{:S(2)}) async-start(bf16[128,8,128]{2,1,0:T(8,128)(2,1)} %sum.1), calls=%async_computation.3 | async-start | bytes 524288 | tf_op jit(solution)/shard_map/all_to_all | solution.py:27

commit v7 on v6

--- a/solution.py
+++ b/solution.py
@@ -311,12 +311,9 @@
 CUT = 512
 
 
-def flow(hbm_ref, vmem_ref, sems, pieces):
+def flow(source_ref, target_ref, sems, pieces):
     return [
-        (
-            pltpu.make_async_copy(hbm_ref.at[piece], vmem_ref.at[piece], sems.at[index]),
-            pltpu.make_async_copy(vmem_ref.at[piece], hbm_ref.at[piece], sems.at[index]),
-        )
+        pltpu.make_async_copy(source_ref.at[piece], target_ref.at[piece], sems.at[index])
         for index, piece in enumerate(pieces)
     ]
 
@@ -351,23 +348,23 @@
     get_slots = pltpu.make_async_copy(slots_hbm.at[pl.ds(0, images)], slots_ref, slots_sem)
     get_inputs = pltpu.make_async_copy(inputs_hbm, inputs_ref, inputs_sem)
     hidden = flow(hidden_grad_hbm, hidden_grad_ref, hidden_sems, column_cuts(hidden_grad_ref))
-    put_expand = flow(expand_hbm, expand_ref, expand_sems, column_cuts(expand_ref))
-    put_layer = flow(layer_hbm, layer_ref, layer_sems, range(images))
+    put_expand = flow(expand_ref, expand_hbm, expand_sems, column_cuts(expand_ref))
+    put_layer = flow(layer_ref, layer_hbm, layer_sems, range(images))
     get_inputs.start()
-    for get, _ in hidden:
+    for get in hidden:
         get.start()
     get_slots.start()
     get_inputs.wait()
     turned = inputs_ref[...].T
-    for (get, _), (_, put), piece in zip(hidden, put_expand, column_cuts(expand_ref)):
+    for get, put, piece in zip(hidden, put_expand, column_cuts(expand_ref)):
         get.wait()
         expand_ref[piece] = mul(turned, hidden_grad_ref[piece]).astype(BF16)
         put.start()
     get_slots.wait()
     for image in range(images):
         layer_ref[image] = mul(combine_ref[image].astype(BF16), slots_ref[image]).astype(BF16)
-        put_layer[image][1].start()
-    for _, put in put_expand + put_layer:
+        put_layer[image].start()
+    for put in put_expand + put_layer:
         put.wait()
 
 
@@ -395,16 +392,16 @@
     get_slots = pltpu.make_async_copy(slots_hbm.at[pl.ds(images, images)], slots_ref, slots_sem)
     get_grads = pltpu.make_async_copy(grads_hbm, grads_ref, grads_sem)
     activated = flow(activated_hbm, activated_ref, activated_sems, column_cuts(activated_ref))
-    put_shrink = flow(shrink_hbm, shrink_ref, shrink_sems, row_cuts(shrink_ref))
-    put_tokens = flow(tokens_hbm, tokens_ref, tokens_sems, range(images))
+    put_shrink = flow(shrink_ref, shrink_hbm, shrink_sems, row_cuts(shrink_ref))
+    put_tokens = flow(tokens_ref, tokens_hbm, tokens_sems, range(images))
     get_grads.start()
-    for get, _ in activated:
+    for get in activated:
         get.start()
     get_slots.start()
     back = mul(params_ref[...], place_order(params_ref.shape[1])).astype(BF16).T
     get_grads.wait()
     pieces = zip(column_cuts(activated_ref), row_cuts(shrink_ref))
-    for (get, _), (_, put), (source, target) in zip(activated, put_shrink, pieces):
+    for get, put, (source, target) in zip(activated, put_shrink, pieces):
         get.wait()
         shrink_ref[target] = mul(activated_ref[source].T, grads_ref[...]).astype(BF16)
         put.start()
@@ -413,8 +410,8 @@
         factors = jnp.concatenate([dispatch_ref[image].astype(BF16), grad_logits_ref[image]], axis=1)
         sources = jnp.concatenate([slots_ref[image], back], axis=0)
         tokens_ref[image] = mul(factors, sources).astype(BF16)
-        put_tokens[image][1].start()
-    for _, put in put_shrink + put_tokens:
+        put_tokens[image].start()
+    for put in put_shrink + put_tokens:
         put.wait()
 
 

time: 128 us -> 128 us (level)
  no operation moved by 1% of the time
where the time goes in v7:
time: 128 us
  blocking collectives  75.7 us (59%)
  Pallas kernels  32.2 us (25%)
  starting transfers between devices  10.3 us (8%)
  waiting for transfers between devices  9.23 us (7%)
    all_to_all x2, blocking collectives, exchange(): return lax.all_to_all(chunks, AXES, split_axis=0, concat_axis=0, tiled=True)  75.7 us
    pallas_call x2, Pallas kernels, finish(): pl.pallas_call(kernel, in_specs=[pl.BlockSpec(memory_space=pltpu.HBM)] *...  12.8 us
    all_to_all x2, starting transfers between devices, exchange(): return lax.all_to_all(chunks, AXES, split_axis=0, concat_axis=0, tiled=True)  10.3 us
    pallas_call x1, Pallas kernels, expert(): pl.pallas_call(lambda *refs: expert_kernel(kinds, *refs), in_specs=whole(...  9.47 us
    all_to_all x2, waiting for transfers between devices, exchange(): return lax.all_to_all(chunks, AXES, split_axis=0, concat_axis=0, tiled=True)  9.23 us
    pallas_call x1, Pallas kernels, pre(): pl.pallas_call(pre_kernel, in_specs=[pl.BlockSpec(memory_space=pltpu.HBM)...  5.02 us
    pallas_call x1, Pallas kernels, post(): pl.pallas_call(lambda *refs: post_kernel(images, *refs), in_specs=whole(a...  3.26 us
  transfers between devices with their start and end apart: 2, of which 2 were waited for; matrix products, arithmetic and copies ran while one was open for 0% of the time, Pallas kernels for 10%

profile of v7, /device:TPU:1, one launch (start us, length us, event | category | flops | bytes accessed | tf_op | source)
XLA Modules:
  0.0 128.3 jit_solution(5058333668096115841)
XLA Ops:
  0.6 0.0 copy-start.3
  0.6 5.0 %pre.1 = (bf16[1024,1024]{1,0:T(8,128)(2,1)S(1)}, f32[4,256,128]{2,1,0:T(8,128)S(1)}, f32[4,256,128]{2,1,0:T(8,128)S(1)}) custom-call(bf16[4,256,1024]{2,1,0:T(8,128)(2,1)} %refs_1_.1, bf16[4,256,1024]{2,1,0:T(8,128)(2,1)} %refs_2_.1, bf16[1024,128]{1,0:T(8,128)(2,1)} %params_ref.1), custom_call_target="tpu_custom_call" | custom-call | tf_op jit(solution)/shard_map/pre/pallas_call | solution.py:121
  5.7 0.0 copy-start.2
  5.7 41.2 %all_to_all.20 = bf16[128,8,1024]{2,1,0:T(8,128)(2,1)S(1)} all-to-all(bf16[128,8,1024]{2,1,0:T(8,128)(2,1)S(1)} %bitcast.15), channel_id=1, replica_groups=mesh['gx'=32,'zh'=2,'core'=2] {'core','gx','zh'}, dimensions={0} | all-to-all | bytes 4194304 | tf_op jit(solution)/shard_map/all_to_all | solution.py:27
  46.9 0.0 copy-done.3
  46.9 0.0 copy-done.2
  46.9 9.5 %expert.1 = (bf16[1024,1024]{1,0:T(8,128)(2,1)S(1)}, bf16[512,1024]{1,0:T(8,128)(2,1)}, bf16[512,1024]{1,0:T(8,128)(2,1)}, bf16[512,2048]{1,0:T(8,128)(2,1)S(1)}, bf16[512,2048]{1,0:T(8,128)(2,1)S(1)}) custom-call(bf16[1024,1024]{1,0:T(8,128)(2,1)S(1)} %bitcast.10, bf16[1024,2048]{1,0:T(8,128)(2,1)S(1)} %bitcast.12, bf16[2048,1024]{1,0:T(8,128)(2,1)S(1)} %bitcast.13), custom_call_target="tpu_custom_call" | custom-call | tf_op jit(solution)/shard_map/expert/pallas_call | solution.py:217
  56.3 0.0 copy-start.5
  56.4 0.0 copy-start.6
  56.4 0.0 copy-start
  56.4 0.0 copy-start.1
  56.4 34.6 %all_to_all.21 = bf16[128,8,1024]{2,1,0:T(8,128)(2,1)S(1)} all-to-all(bf16[128,8,1024]{2,1,0:T(8,128)(2,1)S(1)} %bitcast.14), channel_id=1, replica_groups=mesh['gx'=32,'zh'=2,'core'=2] {'core','gx','zh'}, dimensions={0} | all-to-all | bytes 4194304 | tf_op jit(solution)/shard_map/all_to_all | solution.py:27
  91.0 0.0 copy-done.5
  91.0 0.0 copy-done.6
  91.0 0.0 copy-done
  91.0 0.0 copy-done.1
  91.0 3.3 %post.1 = (bf16[8,128,1024]{2,1,0:T(8,128)(2,1)}, bf16[4,256,128]{2,1,0:T(8,128)(2,1)S(1)}, bf16[1024,128]{1,0:T(8,128)(2,1)}) custom-call(bf16[1024,1024]{1,0:T(8,128)(2,1)S(1)} %bitcast.11, bf16[4,256,1024]{2,1,0:T(8,128)(2,1)S(1)} %copy-done, bf16[4,256,1024]{2,1,0:T(8,128)(2,1)S(1)} %copy-done.1, ...), custom_call_target="tpu_custom_call" | custom-call | tf_op jit(solution)/shard_map/post/pallas_call | solution.py:291
  94.2 4.9 %all-to-all-start.2 = ((bf16[128,8,128]{2,1,0:T(8,128)(2,1)}), bf16[128,8,128]{2,1,0:T(8,128)(2,1)S(1)}, u32[]{:S(2)}, u32[]{:S(2)}) async-start(bf16[128,8,128]{2,1,0:T(8,128)(2,1)} %bitcast.17), calls=%async_computation.2 | async-start | bytes 524288 | tf_op jit(solution)/shard_map/all_to_all | solution.py:27
  99.1 0.0 copy-start.4
  99.2 6.6 %forward_finish.1 = (bf16[4,256,1024]{2,1,0:T(8,128)(2,1)}, bf16[1024,2048]{1,0:T(8,128)(2,1)}) custom-call(bf16[512,1024]{1,0:T(8,128)(2,1)} %get-tuple-element.30.inputs_hbm, bf16[512,2048]{1,0:T(8,128)(2,1)} %copy-done.6, bf16[8,128,1024]{2,1,0:T(8,128)(2,1)} %get-tuple-element.32.slots_hbm, f32[4,256,128]{2,1,0:T(8,128)S(1)} %get-tuple-element.28.refs_4_.combine_ref), custom_call_target="tpu_custom_call" | custom-call | flops 6442450944 | bytes 10485760 | tf_op jit(solution)/shard_map/forward_finish/pallas_call | solution.py:421
  105.8 4.4 %all-to-all-done.2.pieces_ref = bf16[128,8,128]{2,1,0:T(8,128)(2,1)S(1)} async-done(((bf16[128,8,128]{2,1,0:T(8,128)(2,1)}), bf16[128,8,128]{2,1,0:T(8,128)(2,1)S(1)}, u32[]{:S(2)}, u32[]{:S(2)}) %all-to-all-start.2) | async-done | bytes 262176 | tf_op jit(solution)/shard_map/all_to_all | solution.py:27
  110.2 0.9 sum.1
  111.0 5.4 %all-to-all-start.3 = ((bf16[128,8,128]{2,1,0:T(8,128)(2,1)}), bf16[128,8,128]{2,1,0:T(8,128)(2,1)S(1)}, u32[]{:S(2)}, u32[]{:S(2)}) async-start(bf16[128,8,128]{2,1,0:T(8,128)(2,1)} %sum.1), calls=%async_computation.3 | async-start | bytes 524288 | tf_op jit(solution)/shard_map/all_to_all | solution.py:27
  116.4 0.0 copy-done.4
  116.5 6.1 %backward_finish.1 = (bf16[4,256,1024]{2,1,0:T(8,128)(2,1)}, bf16[2048,1024]{1,0:T(8,128)(2,1)}) custom-call(bf16[512,1024]{1,0:T(8,128)(2,1)} %get-tuple-element.36.grads_hbm, bf16[512,2048]{1,0:T(8,128)(2,1)} %copy-done.5, bf16[8,128,1024]{2,1,0:T(8,128)(2,1)} %get-tuple-element.32.slots_hbm, f32[4,256,128]{2,1,0:T(8,128)S(1)} %get-tuple-element.27.refs_3_.dispatch_ref, ...), custom_call_target="tpu_custom_call" | custom-call | flops 6442450944 | bytes 10485760 | tf_op jit(solution)/shard_map/backward_finish/pallas_call | solution.py:421
  122.6 4.9 %all-to-all-done.3 = bf16[128,8,128]{2,1,0:T(8,128)(2,1)S(1)} async-done(((bf16[128,8,128]{2,1,0:T(8,128)(2,1)}), bf16[128,8,128]{2,1,0:T(8,128)(2,1)S(1)}, u32[]{:S(2)}, u32[]{:S(2)}) %all-to-all-start.3) | async-done | bytes 262176 | tf_op jit(solution)/shard_map/all_to_all | solution.py:27
  127.5 0.8 widen.1
Async XLA Ops:
  0.6 46.2 %copy-start.3 = (bf16[1,2048,1024]{2,1,0:T(8,128)(2,1)S(1)}, bf16[1,2048,1024]{2,1,0:T(8,128)(2,1)}, u32[]{:S(2)}) copy-start(bf16[1,2048,1024]{2,1,0:T(8,128)(2,1)} %param.8) | copy-start | bytes 12582916
  5.7 41.2 %copy-start.2 = (bf16[1,1024,2048]{2,1,0:T(8,128)(2,1)S(1)}, bf16[1,1024,2048]{2,1,0:T(8,128)(2,1)}, u32[]{:S(2)}) copy-start(bf16[1,1024,2048]{2,1,0:T(8,128)(2,1)} %param.7) | copy-start | bytes 12582916
  56.3 34.6 %copy-start.5 = (bf16[512,2048]{1,0:T(8,128)(2,1)}, bf16[512,2048]{1,0:T(8,128)(2,1)S(1)}, u32[]{:S(2)}) copy-start(bf16[512,2048]{1,0:T(8,128)(2,1)S(1)} %get-tuple-element.39.activated_hbm) | copy-start | bytes 6291460
  56.4 34.6 %copy-start.6 = (bf16[512,2048]{1,0:T(8,128)(2,1)}, bf16[512,2048]{1,0:T(8,128)(2,1)S(1)}, u32[]{:S(2)}) copy-start(bf16[512,2048]{1,0:T(8,128)(2,1)S(1)} %get-tuple-element.31.hidden_grad_hbm) | copy-start | bytes 6291460
  56.4 34.6 %copy-start = (bf16[4,256,1024]{2,1,0:T(8,128)(2,1)S(1)}, bf16[4,256,1024]{2,1,0:T(8,128)(2,1)}, u32[]{:S(2)}) copy-start(bf16[4,256,1024]{2,1,0:T(8,128)(2,1)} %refs_1_.1) | copy-start | bytes 6291460
  56.4 34.6 %copy-start.1 = (bf16[4,256,1024]{2,1,0:T(8,128)(2,1)S(1)}, bf16[4,256,1024]{2,1,0:T(8,128)(2,1)}, u32[]{:S(2)}) copy-start(bf16[4,256,1024]{2,1,0:T(8,128)(2,1)} %refs_2_.1) | copy-start | bytes 6291460
  94.2 15.9 %all-to-all-start.2 = ((bf16[128,8,128]{2,1,0:T(8,128)(2,1)}), bf16[128,8,128]{2,1,0:T(8,128)(2,1)S(1)}, u32[]{:S(2)}, u32[]{:S(2)}) async-start(bf16[128,8,128]{2,1,0:T(8,128)(2,1)} %bitcast.17), calls=%async_computation.2 | async-start | bytes 524288 | tf_op jit(solution)/shard_map/all_to_all | solution.py:27
  99.1 17.3 %copy-start.4 = (bf16[1024,128]{1,0:T(8,128)(2,1)S(1)}, bf16[1024,128]{1,0:T(8,128)(2,1)}, u32[]{:S(2)}) copy-start(bf16[1024,128]{1,0:T(8,128)(2,1)} %params_ref.1) | copy-start | bytes 786436
  111.0 16.4 %all-to-all-start.3 = ((bf16[128,8,128]{2,1,0:T(8,128)(2,1)}), bf16[128,8,128]{2,1,0:T(8,128)(2,1)S(1)}, u32[]{:S(2)}, u32[]{:S(2)}) async-start(bf16[128,8,128]{2,1,0:T(8,128)(2,1)} %sum.1), calls=%async_computation.3 | async-start | bytes 524288 | tf_op jit(solution)/shard_map/all_to_all | solution.py:27

commit v8 on v7

--- a/solution.py
+++ b/solution.py
@@ -266,7 +266,7 @@
         grad_logits_ref[image] = grad_logits.astype(BF16)
         parts.append(grad_logits.astype(BF16).T)
     all_tokens = tokens_ref[...].reshape(images * patches, width)
-    turned = mul(place_order(slots), jnp.concatenate(parts, axis=1)).astype(BF16)
+    turned = jnp.concatenate(parts, axis=1)
     cut = width // 2
     puts = []
     for index in range(2):
@@ -441,8 +441,9 @@
 
 
 def sum_kernel(pieces_ref, copies_ref):
-    own = jnp.sum(pieces_ref[...].astype(F32), axis=0, keepdims=True).astype(BF16)
-    copies_ref[...] = jnp.broadcast_to(own, copies_ref.shape)
+    own = jnp.sum(pieces_ref[...].astype(F32), axis=0).astype(BF16)
+    own = mul(own, place_order(own.shape[1]), NT).astype(BF16)
+    copies_ref[...] = jnp.broadcast_to(own[None], copies_ref.shape)
 
 
 def widen_kernel(narrow_ref, wide_ref):

time: 128 us -> 128 us (level)
  no operation moved by 1% of the time
where the time goes in v8:
time: 128 us
  blocking collectives  75.7 us (59%)
  Pallas kernels  32.2 us (25%)
  starting transfers between devices  10.3 us (8%)
  waiting for transfers between devices  9.23 us (7%)
    all_to_all x2, blocking collectives, exchange(): return lax.all_to_all(chunks, AXES, split_axis=0, concat_axis=0, tiled=True)  75.7 us
    pallas_call x2, Pallas kernels, finish(): pl.pallas_call(kernel, in_specs=[pl.BlockSpec(memory_space=pltpu.HBM)] *...  12.8 us
    all_to_all x2, starting transfers between devices, exchange(): return lax.all_to_all(chunks, AXES, split_axis=0, concat_axis=0, tiled=True)  10.3 us
    pallas_call x1, Pallas kernels, expert(): pl.pallas_call(lambda *refs: expert_kernel(kinds, *refs), in_specs=whole(...  9.47 us
    all_to_all x2, waiting for transfers between devices, exchange(): return lax.all_to_all(chunks, AXES, split_axis=0, concat_axis=0, tiled=True)  9.23 us
    pallas_call x1, Pallas kernels, pre(): pl.pallas_call(pre_kernel, in_specs=[pl.BlockSpec(memory_space=pltpu.HBM)...  5.02 us
    pallas_call x1, Pallas kernels, post(): pl.pallas_call(lambda *refs: post_kernel(images, *refs), in_specs=whole(a...  3.11 us
  transfers between devices with their start and end apart: 2, of which 2 were waited for; matrix products, arithmetic and copies ran while one was open for 0% of the time, Pallas kernels for 10%

profile of v8, /device:TPU:1, one launch (start us, length us, event | category | flops | bytes accessed | tf_op | source)
XLA Modules:
  0.0 128.3 jit_solution(11965056209407825144)
XLA Ops:
  0.6 0.0 copy-start.3
  0.6 5.0 %pre.1 = (bf16[1024,1024]{1,0:T(8,128)(2,1)S(1)}, f32[4,256,128]{2,1,0:T(8,128)S(1)}, f32[4,256,128]{2,1,0:T(8,128)S(1)}) custom-call(bf16[4,256,1024]{2,1,0:T(8,128)(2,1)} %refs_1_.1, bf16[4,256,1024]{2,1,0:T(8,128)(2,1)} %refs_2_.1, bf16[1024,128]{1,0:T(8,128)(2,1)} %params_ref.1), custom_call_target="tpu_custom_call" | custom-call | tf_op jit(solution)/shard_map/pre/pallas_call | solution.py:121
  5.7 0.0 copy-start.2
  5.7 41.2 %all_to_all.20 = bf16[128,8,1024]{2,1,0:T(8,128)(2,1)S(1)} all-to-all(bf16[128,8,1024]{2,1,0:T(8,128)(2,1)S(1)} %bitcast.15), channel_id=1, replica_groups=mesh['gx'=32,'zh'=2,'core'=2] {'core','gx','zh'}, dimensions={0} | all-to-all | bytes 4194304 | tf_op jit(solution)/shard_map/all_to_all | solution.py:27
  46.9 0.0 copy-done.3
  46.9 0.0 copy-done.2
  46.9 9.5 %expert.1 = (bf16[1024,1024]{1,0:T(8,128)(2,1)S(1)}, bf16[512,1024]{1,0:T(8,128)(2,1)}, bf16[512,1024]{1,0:T(8,128)(2,1)}, bf16[512,2048]{1,0:T(8,128)(2,1)S(1)}, bf16[512,2048]{1,0:T(8,128)(2,1)S(1)}) custom-call(bf16[1024,1024]{1,0:T(8,128)(2,1)S(1)} %bitcast.10, bf16[1024,2048]{1,0:T(8,128)(2,1)S(1)} %bitcast.12, bf16[2048,1024]{1,0:T(8,128)(2,1)S(1)} %bitcast.13), custom_call_target="tpu_custom_call" | custom-call | tf_op jit(solution)/shard_map/expert/pallas_call | solution.py:217
  56.3 0.0 copy-start.5
  56.4 0.0 copy-start.6
  56.4 0.0 copy-start
  56.4 0.0 copy-start.1
  56.4 34.6 %all_to_all.21 = bf16[128,8,1024]{2,1,0:T(8,128)(2,1)S(1)} all-to-all(bf16[128,8,1024]{2,1,0:T(8,128)(2,1)S(1)} %bitcast.14), channel_id=1, replica_groups=mesh['gx'=32,'zh'=2,'core'=2] {'core','gx','zh'}, dimensions={0} | all-to-all | bytes 4194304 | tf_op jit(solution)/shard_map/all_to_all | solution.py:27
  91.0 0.0 copy-done.5
  91.0 0.0 copy-done.6
  91.0 0.0 copy-done
  91.0 0.0 copy-done.1
  91.0 3.1 %post.1 = (bf16[8,128,1024]{2,1,0:T(8,128)(2,1)}, bf16[4,256,128]{2,1,0:T(8,128)(2,1)S(1)}, bf16[1024,128]{1,0:T(8,128)(2,1)}) custom-call(bf16[1024,1024]{1,0:T(8,128)(2,1)S(1)} %bitcast.11, bf16[4,256,1024]{2,1,0:T(8,128)(2,1)S(1)} %copy-done, bf16[4,256,1024]{2,1,0:T(8,128)(2,1)S(1)} %copy-done.1, ...), custom_call_target="tpu_custom_call" | custom-call | tf_op jit(solution)/shard_map/post/pallas_call | solution.py:291
  94.1 4.9 %all-to-all-start.2 = ((bf16[128,8,128]{2,1,0:T(8,128)(2,1)}), bf16[128,8,128]{2,1,0:T(8,128)(2,1)S(1)}, u32[]{:S(2)}, u32[]{:S(2)}) async-start(bf16[128,8,128]{2,1,0:T(8,128)(2,1)} %bitcast.17), calls=%async_computation.2 | async-start | bytes 524288 | tf_op jit(solution)/shard_map/all_to_all | solution.py:27
  99.0 0.0 copy-start.4
  99.0 6.7 %forward_finish.1 = (bf16[4,256,1024]{2,1,0:T(8,128)(2,1)}, bf16[1024,2048]{1,0:T(8,128)(2,1)}) custom-call(bf16[512,1024]{1,0:T(8,128)(2,1)} %get-tuple-element.30.inputs_hbm, bf16[512,2048]{1,0:T(8,128)(2,1)} %copy-done.6, bf16[8,128,1024]{2,1,0:T(8,128)(2,1)} %get-tuple-element.32.slots_hbm, f32[4,256,128]{2,1,0:T(8,128)S(1)} %get-tuple-element.28.refs_4_.combine_ref), custom_call_target="tpu_custom_call" | custom-call | flops 6442450944 | bytes 10485760 | tf_op jit(solution)/shard_map/forward_finish/pallas_call | solution.py:421
  105.7 4.3 %all-to-all-done.2.pieces_ref = bf16[128,8,128]{2,1,0:T(8,128)(2,1)S(1)} async-done(((bf16[128,8,128]{2,1,0:T(8,128)(2,1)}), bf16[128,8,128]{2,1,0:T(8,128)(2,1)S(1)}, u32[]{:S(2)}, u32[]{:S(2)}) %all-to-all-start.2) | async-done | bytes 262176 | tf_op jit(solution)/shard_map/all_to_all | solution.py:27
  110.0 1.0 sum.1
  111.0 5.4 %all-to-all-start.3 = ((bf16[128,8,128]{2,1,0:T(8,128)(2,1)}), bf16[128,8,128]{2,1,0:T(8,128)(2,1)S(1)}, u32[]{:S(2)}, u32[]{:S(2)}) async-start(bf16[128,8,128]{2,1,0:T(8,128)(2,1)} %sum.1), calls=%async_computation.3 | async-start | bytes 524288 | tf_op jit(solution)/shard_map/all_to_all | solution.py:27
  116.4 0.0 copy-done.4
  116.4 6.1 %backward_finish.1 = (bf16[4,256,1024]{2,1,0:T(8,128)(2,1)}, bf16[2048,1024]{1,0:T(8,128)(2,1)}) custom-call(bf16[512,1024]{1,0:T(8,128)(2,1)} %get-tuple-element.36.grads_hbm, bf16[512,2048]{1,0:T(8,128)(2,1)} %copy-done.5, bf16[8,128,1024]{2,1,0:T(8,128)(2,1)} %get-tuple-element.32.slots_hbm, f32[4,256,128]{2,1,0:T(8,128)S(1)} %get-tuple-element.27.refs_3_.dispatch_ref, ...), custom_call_target="tpu_custom_call" | custom-call | flops 6442450944 | bytes 10485760 | tf_op jit(solution)/shard_map/backward_finish/pallas_call | solution.py:421
  122.6 4.9 %all-to-all-done.3 = bf16[128,8,128]{2,1,0:T(8,128)(2,1)S(1)} async-done(((bf16[128,8,128]{2,1,0:T(8,128)(2,1)}), bf16[128,8,128]{2,1,0:T(8,128)(2,1)S(1)}, u32[]{:S(2)}, u32[]{:S(2)}) %all-to-all-start.3) | async-done | bytes 262176 | tf_op jit(solution)/shard_map/all_to_all | solution.py:27
  127.4 0.8 widen.1
Async XLA Ops:
  0.6 46.2 %copy-start.3 = (bf16[1,2048,1024]{2,1,0:T(8,128)(2,1)S(1)}, bf16[1,2048,1024]{2,1,0:T(8,128)(2,1)}, u32[]{:S(2)}) copy-start(bf16[1,2048,1024]{2,1,0:T(8,128)(2,1)} %param.8) | copy-start | bytes 12582916
  5.7 41.2 %copy-start.2 = (bf16[1,1024,2048]{2,1,0:T(8,128)(2,1)S(1)}, bf16[1,1024,2048]{2,1,0:T(8,128)(2,1)}, u32[]{:S(2)}) copy-start(bf16[1,1024,2048]{2,1,0:T(8,128)(2,1)} %param.7) | copy-start | bytes 12582916
  56.3 34.6 %copy-start.5 = (bf16[512,2048]{1,0:T(8,128)(2,1)}, bf16[512,2048]{1,0:T(8,128)(2,1)S(1)}, u32[]{:S(2)}) copy-start(bf16[512,2048]{1,0:T(8,128)(2,1)S(1)} %get-tuple-element.39.activated_hbm) | copy-start | bytes 6291460
  56.4 34.6 %copy-start.6 = (bf16[512,2048]{1,0:T(8,128)(2,1)}, bf16[512,2048]{1,0:T(8,128)(2,1)S(1)}, u32[]{:S(2)}) copy-start(bf16[512,2048]{1,0:T(8,128)(2,1)S(1)} %get-tuple-element.31.hidden_grad_hbm) | copy-start | bytes 6291460
  56.4 34.6 %copy-start = (bf16[4,256,1024]{2,1,0:T(8,128)(2,1)S(1)}, bf16[4,256,1024]{2,1,0:T(8,128)(2,1)}, u32[]{:S(2)}) copy-start(bf16[4,256,1024]{2,1,0:T(8,128)(2,1)} %refs_1_.1) | copy-start | bytes 6291460
  56.4 34.6 %copy-start.1 = (bf16[4,256,1024]{2,1,0:T(8,128)(2,1)S(1)}, bf16[4,256,1024]{2,1,0:T(8,128)(2,1)}, u32[]{:S(2)}) copy-start(bf16[4,256,1024]{2,1,0:T(8,128)(2,1)} %refs_2_.1) | copy-start | bytes 6291460
  94.1 15.9 %all-to-all-start.2 = ((bf16[128,8,128]{2,1,0:T(8,128)(2,1)}), bf16[128,8,128]{2,1,0:T(8,128)(2,1)S(1)}, u32[]{:S(2)}, u32[]{:S(2)}) async-start(bf16[128,8,128]{2,1,0:T(8,128)(2,1)} %bitcast.17), calls=%async_computation.2 | async-start | bytes 524288 | tf_op jit(solution)/shard_map/all_to_all | solution.py:27
  99.0 17.4 %copy-start.4 = (bf16[1024,128]{1,0:T(8,128)(2,1)S(1)}, bf16[1024,128]{1,0:T(8,128)(2,1)}, u32[]{:S(2)}) copy-start(bf16[1024,128]{1,0:T(8,128)(2,1)} %params_ref.1) | copy-start | bytes 786436
  111.0 16.5 %all-to-all-start.3 = ((bf16[128,8,128]{2,1,0:T(8,128)(2,1)}), bf16[128,8,128]{2,1,0:T(8,128)(2,1)S(1)}, u32[]{:S(2)}, u32[]{:S(2)}) async-start(bf16[128,8,128]{2,1,0:T(8,128)(2,1)} %sum.1), calls=%async_computation.3 | async-start | bytes 524288 | tf_op jit(solution)/shard_map/all_to_all | solution.py:27
